TPU v7x, 128 devices: a whole 4x4x4 slice. The times are simulated.
128 devices in a mesh: gx: 8 (over y, core), gy: 16 (over z, x).
Axes of the slice: x: 4, y: 4, z: 4, core: 2. Of those that a mesh axis runs over, the one named last changes fastest.
Arguments:
- interface_conditions: float32 [8, 1024, 2048], P(None, 'gx', 'gy'), may hold values from -3 to 1.5, as said below
- level_warmth_profile: float32 [4096, 5, 10, 1024], P(('gx', 'gy')), may hold values from -2 to -0.1
- class_coverage_share: float32 [4096, 5, 1024], P(('gx', 'gy')), may hold values from 0.02 to 0.4
- class_floe_depth: float32 [4096, 5, 1024], P(('gx', 'gy')), may hold values from 0.5 to 4
- class_drift_depth: float32 [4096, 5, 1024], P(('gx', 'gy')), may hold values from 0.05 to 0.5
- floe_drift_speed: float32 [2, 1024, 2048], P(None, 'gx', 'gy'), may hold values from -3 to 3
- internal_tension_tensor: float32 [3, 1024, 2048], P(None, 'gx', 'gy'), may hold values from -3 to 3
- external_drive: float32 [4, 1024, 2048], P(None, 'gx', 'gy'), may hold values from -2 to 2
- floe_weight: float32 [1024, 2048], P('gx', 'gy'), may hold values from 0.3 to 3
- floe_pressure: float32 [1024, 2048], P('gx', 'gy'), may hold values from 0.2 to 2
- holder_lookup: int32 [2048, 1], P(('gx', 'gy')), may hold values from 0 to 15, as said below
- ground_tile_marker: int32 [2048], P(('gx', 'gy')), may hold values from 0 to 1, as said below
Outputs:
- revised_level_warmth: float32 [4096, 5, 10, 1024], P(('gx', 'gy'))
- interface_exchanges: float32 [8, 1024, 2048], P(None, 'gx', 'gy')
- velocity_new: float32 [2, 1024, 2048], P(None, 'gx', 'gy')
- stress_new: float32 [3, 1024, 2048], P(None, 'gx', 'gy')
Inputs may be any that keep to these rules, and one draw needn't show every extreme that they name: `interface_conditions`: fields in order: ocean temperature in -0.2 to 0.1, salinity in 0.5 to 1, air temperature in -3 to -0.2, visible and near-infrared shortwave in 0 to 1, longwave in 0.5 to 1.5, snowfall and wind speed in 0 to 1. `holder_lookup`: each tile names one owner for at most 2 of its blocks. In every row of tiles there is one owner that every tile of the row names for exactly 2 blocks, none of them land. `ground_tile_marker`: 1 marks a land block.
All inputs are finite; a program needn't handle non-finite values.
Results may differ from a plain program's by a relative error of at most 0.0003.
Values sent between devices are 32-bit elements; how exact they have to be, the bound alone decides.
No kernel may reach another device: no remote copies, remote signals or barrier semaphores. Data moves between devices by JAX's collectives and lax.ppermute only.
A program may use at most 128 MiB of HBM per device.

v0:
```python
import jax
import jax.numpy as jnp
from jax import lax
from jax.sharding import PartitionSpec as P

BS = 32
BPX = 4
BPY = 4
CAP = 2
FROZEN_LEVELS = 7
DRIFT_LEVELS = 3
POINT_QUANTITIES = 8
SUB = 4
TILE_POINTS = 1024
B = 16


RELAX_RATE = 0.5
ECC_SQUARED = 4.0
DELTA_FLOOR = 0.04
MOTION_STEP = 0.5
WATER_DRAG = 1.0
CORIOLIS = 0.3
HEAT_STEP = 0.5
SNOW_COND = 0.3
SNOW_GAIN = 0.3
GROWTH_RATE = 0.05


def padded_2(array, sides, width):
    for axis, dim in sides:
        peers, length = (lax.axis_size(axis), array.shape[dim])
        up = [(i, (i + 1) % peers) for i in range(peers - 1)]
        down = [(j, i) for i, j in up]
        last = lax.slice_in_dim(array, length - width, length, axis=dim)
        leading = lax.slice_in_dim(array, 0, width, axis=dim)
        before = lax.ppermute(last, axis, up)
        after = lax.ppermute(leading, axis, down)
        array = jnp.concatenate([before, array, after], axis=dim)
    return array


def column_step(layer_temp, cat_area, cat_thick, cat_snow, forcing_fields):
    ocean_temp = forcing_fields[:, 0:1]
    salinity = forcing_fields[:, 1:2]
    air_temp = forcing_fields[:, 2:3]
    visible = forcing_fields[:, 3:4]
    near_red = forcing_fields[:, 4:5]
    longwave = forcing_fields[:, 5:6]
    snowfall = forcing_fields[:, 6:7]
    wind_speed = forcing_fields[:, 7:8]
    snow_depth = cat_snow + SNOW_GAIN * snowfall
    layer_total = DRIFT_LEVELS + FROZEN_LEVELS
    depths = []
    heat_caps = []
    resist = []
    for layer_num in range(layer_total):
        old_temp = layer_temp[:, :, layer_num]
        if layer_num < DRIFT_LEVELS:
            layer_depth = snow_depth / DRIFT_LEVELS
            heat_cap = jnp.ones_like(layer_depth)
            conduct = SNOW_COND
        else:
            brine_term = salinity * (0.2 + 0.1 * (layer_num - DRIFT_LEVELS))
            layer_depth = cat_thick / FROZEN_LEVELS
            heat_cap = 1.0 + 0.2 * brine_term / (old_temp * old_temp + 0.1)
            conduct = 2.0 + 0.1 * brine_term / (old_temp - 0.5)
        depths.append(layer_depth)
        heat_caps.append(heat_cap)
        resist.append(layer_depth / conduct)
    top_cond = 1.0 / (0.5 * resist[0] + 1.0 / (1.0 + 2.0 * wind_speed))
    bottom_cond = 2.0 / resist[-1]
    inner_cond = [
        1.0 / (0.5 * (resist[layer_num] + resist[layer_num + 1]))
        for layer_num in range(layer_total - 1)
    ]
    cond_above = [top_cond] + inner_cond
    cond_below = inner_cond + [bottom_cond]
    sweep_ratio = []
    sweep_value = []
    for layer_num in range(layer_total):
        mass_term = heat_caps[layer_num] * depths[layer_num] / HEAT_STEP
        diagonal = mass_term + cond_above[layer_num] + cond_below[layer_num]
        source = mass_term * layer_temp[:, :, layer_num]
        if layer_num == 0:
            source = (
                source + top_cond * air_temp + 0.25 * visible + 0.45 * near_red + 0.3 * longwave
            )
        if layer_num == layer_total - 1:
            source = source + bottom_cond * ocean_temp
        if layer_num > 0:
            pivot_term = diagonal - cond_above[layer_num] * sweep_ratio[-1]
            carried = source + cond_above[layer_num] * sweep_value[-1]
        else:
            pivot_term = diagonal
            carried = source
        sweep_ratio.append(cond_below[layer_num] / pivot_term)
        sweep_value.append(carried / pivot_term)
    solved = [sweep_value[-1]]
    for layer_num in range(layer_total - 2, -1, -1):
        solved.insert(0, sweep_value[layer_num] + sweep_ratio[layer_num] * solved[0])
    advanced_warmth = jnp.stack(solved, axis=2)
    bottom_flux = bottom_cond * (solved[-1] - ocean_temp)
    growth = -GROWTH_RATE * bottom_flux
    energy = heat_caps[0] * depths[0] * solved[0]
    for layer_num in range(1, layer_total):
        energy = energy + heat_caps[layer_num] * depths[layer_num] * solved[layer_num]
    light_through = 0.7 * visible * jnp.exp(-5.0 * snow_depth - 1.5 * cat_thick)
    flux_terms = [
        bottom_flux,
        top_cond * (air_temp - solved[0]),
        light_through,
        solved[0],
        snow_depth,
        cat_thick + growth,
        0.1 * energy,
        growth * salinity,
    ]
    slot_fluxes = jnp.stack(
        [jnp.sum(cat_area * term_value, axis=1) for term_value in flux_terms], axis=1
    )
    return (advanced_warmth, slot_fluxes)


def strain_rates(drift_kinematics):
    east_vel = drift_kinematics[0]
    north_vel = drift_kinematics[1]
    du_x = 0.5 * (east_vel[2:, 1:-1] - east_vel[:-2, 1:-1])
    du_y = 0.5 * (east_vel[1:-1, 2:] - east_vel[1:-1, :-2])
    dv_x = 0.5 * (north_vel[2:, 1:-1] - north_vel[:-2, 1:-1])
    dv_y = 0.5 * (north_vel[1:-1, 2:] - north_vel[1:-1, :-2])
    return (du_x + dv_y, du_x - dv_y, du_y + dv_x)


def update_stress(stress_old, strength, drift_kinematics):
    diverge, tension, shearing = strain_rates(drift_kinematics)
    spread = jnp.sqrt(
        diverge * diverge + (tension * tension + shearing * shearing) / ECC_SQUARED + DELTA_FLOOR
    )
    ratio = strength / spread
    first = (stress_old[0] + RELAX_RATE * ratio * (diverge - spread)) / (1.0 + RELAX_RATE)
    second = (stress_old[1] + RELAX_RATE * ratio * tension / ECC_SQUARED) / (1.0 + RELAX_RATE)
    third = (stress_old[2] + RELAX_RATE * ratio * shearing / (2.0 * ECC_SQUARED)) / (
        1.0 + RELAX_RATE
    )
    return jnp.stack([first, second, third])


def stress_force(stress_pad):
    stress_sum = stress_pad[0] + stress_pad[1]
    differ = stress_pad[0] - stress_pad[1]
    shear_part = stress_pad[2]
    force_x = 0.25 * (stress_sum[2:, 1:-1] - stress_sum[:-2, 1:-1]) + 0.5 * (
        shear_part[1:-1, 2:] - shear_part[1:-1, :-2]
    )
    force_y = 0.25 * (differ[1:-1, 2:] - differ[1:-1, :-2]) + 0.5 * (
        shear_part[2:, 1:-1] - shear_part[:-2, 1:-1]
    )
    return (force_x, force_y)


def update_motion(drift_kinematics, force_x, force_y, floe_weight, external_drive, water_mask):
    east_vel = drift_kinematics[0]
    north_vel = drift_kinematics[1]
    denominator = floe_weight + MOTION_STEP * WATER_DRAG
    new_east = (
        floe_weight * east_vel
        + MOTION_STEP
        * (
            force_x
            + external_drive[0]
            + WATER_DRAG * external_drive[2]
            + CORIOLIS * floe_weight * north_vel
        )
    ) / denominator
    new_north = (
        floe_weight * north_vel
        + MOTION_STEP
        * (
            force_y
            + external_drive[1]
            + WATER_DRAG * external_drive[3]
            - CORIOLIS * floe_weight * east_vel
        )
    ) / denominator
    return jnp.stack([new_east * water_mask, new_north * water_mask])


def to_blocks(tile_data):
    field_count, row_count, column_count = tile_data.shape
    shaped = tile_data.reshape(field_count, BPX, BS, BPY, BS)
    return shaped.transpose(1, 3, 0, 2, 4).reshape(B, field_count, TILE_POINTS)


def from_blocks(block_data):
    field_count = block_data.shape[1]
    shaped = block_data.reshape(BPX, BPY, field_count, BS, BS)
    return shaped.transpose(2, 0, 3, 1, 4).reshape(field_count, BPX * BS, BPY * BS)


def slot_rank(target, slot_covered):
    length = target.shape[0]
    earlier = lax.broadcasted_iota(jnp.int32, (length, length), 1) < lax.broadcasted_iota(
        jnp.int32, (length, length), 0
    )
    matching = (target[:, None] == target[None, :]) & (slot_covered[None, :] == 1) & earlier
    return jnp.sum(matching.astype(jnp.int32), axis=1)


def local(
    interface_conditions,
    level_warmth_profile,
    class_coverage_share,
    class_floe_depth,
    class_drift_depth,
    floe_drift_speed,
    internal_tension_tensor,
    external_drive,
    floe_weight,
    floe_pressure,
    holder_lookup,
    ground_tile_marker,
):
    group_size = lax.axis_size("gy")
    slot_count = group_size * CAP
    blocks_of_grid = to_blocks(interface_conditions)
    target = holder_lookup[:, 0]
    slot_covered = 1 - ground_tile_marker
    order_rank = slot_rank(target, slot_covered)
    own_slot = target * CAP + order_rank
    slot_iota = lax.broadcasted_iota(jnp.int32, (B, slot_count), 1)
    own_choose = ((own_slot[:, None] == slot_iota) & (slot_covered[:, None] == 1)).astype(
        jnp.float32
    )
    outgoing = jnp.einsum(
        "bs,bfc->sfc", own_choose, blocks_of_grid, precision=lax.Precision.HIGHEST
    )
    flags = jnp.sum(own_choose, axis=0)
    parcel, occupied_mask = (
        lax.all_to_all(
            outgoing.reshape(group_size, CAP, POINT_QUANTITIES, TILE_POINTS),
            "gy",
            split_axis=0,
            concat_axis=0,
            tiled=True,
        ),
        lax.all_to_all(
            flags.reshape(group_size, CAP), "gy", split_axis=0, concat_axis=0, tiled=True
        ),
    )
    parcel = parcel.reshape(slot_count, POINT_QUANTITIES, TILE_POINTS)
    occupied_mask = occupied_mask.reshape(slot_count)
    advanced_warmth, slot_fluxes = column_step(
        level_warmth_profile, class_coverage_share, class_floe_depth, class_drift_depth, parcel
    )
    revised_level_warmth = jnp.where(
        occupied_mask[:, None, None, None] > 0.5, advanced_warmth, level_warmth_profile
    )
    returned = lax.all_to_all(
        slot_fluxes.reshape(group_size, CAP, 8, TILE_POINTS),
        "gy",
        split_axis=0,
        concat_axis=0,
        tiled=True,
    )
    returned = returned.reshape(slot_count, 8, TILE_POINTS)
    block_fluxes = jnp.einsum("bs,sfc->bfc", own_choose, returned, precision=lax.Precision.HIGHEST)
    interface_exchanges = from_blocks(block_fluxes)
    land_tile = (1.0 - ground_tile_marker.astype(jnp.float32)).reshape(BPX, BPY)
    water_mask = jnp.repeat(jnp.repeat(land_tile, BS, axis=0), BS, axis=1)
    drift_kinematics = floe_drift_speed
    tension_components = internal_tension_tensor
    for subcycle in range(SUB):
        padded = padded_2(drift_kinematics, (("gx", 1), ("gy", 2)), 1)
        tension_components = update_stress(tension_components, floe_pressure, padded)
        stress_pad = padded_2(tension_components, (("gx", 1), ("gy", 2)), 1)
        force_x, force_y = stress_force(stress_pad)
        drift_kinematics = update_motion(
            drift_kinematics, force_x, force_y, floe_weight, external_drive, water_mask
        )
    return (revised_level_warmth, interface_exchanges, drift_kinematics, tension_components)


def solution(mesh):
    return jax.shard_map(
        local,
        mesh=mesh,
        in_specs=(
            P(None, "gx", "gy"),
            P(("gx", "gy"), None, None, None),
            P(("gx", "gy"), None, None),
            P(("gx", "gy"), None, None),
            P(("gx", "gy"), None, None),
            P(None, "gx", "gy"),
            P(None, "gx", "gy"),
            P(None, "gx", "gy"),
            P("gx", "gy"),
            P("gx", "gy"),
            P(("gx", "gy"), None),
            P(("gx", "gy")),
        ),
        out_specs=(
            P(("gx", "gy"), None, None, None),
            P(None, "gx", "gy"),
            P(None, "gx", "gy"),
            P(None, "gx", "gy"),
        ),
        check_vma=False,
    )
```

profile of v0, /device:TPU:7, one launch (start us, length us, event | category | flops | bytes accessed | tf_op | source)
XLA Modules:
  0.0 263.5 jit_solution(17662705262205695980)
XLA Ops:
  1.5 3.8 %collective-permute-start = (f32[2,1,128]{1,2,0:T(8,128)S(1)}, f32[2,1,128]{1,2,0:T(8,128)S(1)}, u32[]{:S(2)}, u32[]{:S(2)}) collective-permute-start(f32[2,1,128]{1,2,0:T(8,128)S(1)} %copy.173), channel_id=1, source_target_pairs={{0,16},{16,32},{32,48},{48,64},{64,80},{80,96},{96,112},{1,17},{17... | collective-permute-start | bytes 3080 | tf_op jit(solution)/shard_map/ppermute | solution.py:37
  8.4 3.3 %collective-permute-done.1 = f32[2,1,128]{1,2,0:T(8,128)S(1)} collective-permute-done((f32[2,1,128]{1,2,0:T(8,128)S(1)}, f32[2,1,128]{1,2,0:T(8,128)S(1)}, u32[]{:S(2)}, u32[]{:S(2)}) %collective-permute-start.1) | collective-permute-done | bytes 1056 | tf_op jit(solution)/shard_map/ppermute | solution.py:38
  11.8 3.5 %collective-permute-start.2 = (f32[2,130,1]{1,2,0:T(1,128)S(1)}, f32[2,130,1]{1,2,0:T(1,128)S(1)}, u32[]{:S(2)}, u32[]{:S(2)}) collective-permute-start(f32[2,130,1]{1,2,0:T(1,128)S(1)} %get-tuple-element.112), channel_id=1, source_target_pairs={{0,1},{1,2},{2,3},{3,4},{4,5},{5,6},{6,7},{7,8},{8,9},{9,10},{10,1... | collective-permute-start | bytes 3128 | tf_op jit(solution)/shard_map/ppermute | solution.py:37
  22.4 3.2 %collective-permute-start.4 = (f32[3,1,128]{1,2,0:T(8,128)S(1)}, f32[3,1,128]{1,2,0:T(8,128)S(1)}, u32[]{:S(2)}, u32[]{:S(2)}) collective-permute-start(f32[3,1,128]{1,2,0:T(8,128)S(1)} %get-tuple-element.140), channel_id=1, source_target_pairs={{0,16},{16,32},{32,48},{48,64},{64,80},{80,96},{96,112},{1,17},{17... | collective-permute-start | bytes 4616 | tf_op jit(solution)/shard_map/ppermute | solution.py:37
  28.6 4.1 %collective-permute-done.5 = f32[3,1,128]{1,2,0:T(8,128)S(1)} collective-permute-done((f32[3,1,128]{1,2,0:T(8,128)S(1)}, f32[3,1,128]{1,2,0:T(8,128)S(1)}, u32[]{:S(2)}, u32[]{:S(2)}) %collective-permute-start.5) | collective-permute-done | bytes 1568 | tf_op jit(solution)/shard_map/ppermute | solution.py:38
  35.0 3.0 %collective-permute-start.7 = (f32[3,130,1]{1,2,0:T(1,128)S(1)}, f32[3,130,1]{1,2,0:T(1,128)S(1)}, u32[]{:S(2)}, u32[]{:S(2)}) collective-permute-start(f32[3,130,1]{1,2,0:T(1,128)S(1)} %get-tuple-element.93), channel_id=1, source_target_pairs={{1,0},{2,1},{3,2},{4,3},{5,4},{6,5},{7,6},{8,7},{9,8},{10,9},{11,1... | collective-permute-start | bytes 4688 | tf_op jit(solution)/shard_map/ppermute | solution.py:38
  42.0 3.2 %collective-permute-start.8 = (f32[2,1,128]{1,2,0:T(8,128)S(1)}, f32[2,1,128]{1,2,0:T(8,128)S(1)}, u32[]{:S(2)}, u32[]{:S(2)}) collective-permute-start(f32[2,1,128]{1,2,0:T(8,128)S(1)} %get-tuple-element.149), channel_id=1, source_target_pairs={{0,16},{16,32},{32,48},{48,64},{64,80},{80,96},{96,112},{1,17},{17... | collective-permute-start | bytes 3080 | tf_op jit(solution)/shard_map/ppermute | solution.py:37
  47.2 4.3 %collective-permute-done.9 = f32[2,1,128]{1,2,0:T(8,128)S(1)} collective-permute-done((f32[2,1,128]{1,2,0:T(8,128)S(1)}, f32[2,1,128]{1,2,0:T(8,128)S(1)}, u32[]{:S(2)}, u32[]{:S(2)}) %collective-permute-start.9) | collective-permute-done | bytes 1056 | tf_op jit(solution)/shard_map/ppermute | solution.py:38
  53.5 3.4 %collective-permute-start.11 = (f32[2,130,1]{1,2,0:T(1,128)S(1)}, f32[2,130,1]{1,2,0:T(1,128)S(1)}, u32[]{:S(2)}, u32[]{:S(2)}) collective-permute-start(f32[2,130,1]{1,2,0:T(1,128)S(1)} %get-tuple-element.111), channel_id=1, source_target_pairs={{1,0},{2,1},{3,2},{4,3},{5,4},{6,5},{7,6},{8,7},{9,8},{10,9},{11,1... | collective-permute-start | bytes 3128 | tf_op jit(solution)/shard_map/ppermute | solution.py:38
  56.9 3.1 %collective-permute-done.11 = f32[2,130,1]{1,2,0:T(1,128)S(1)} collective-permute-done((f32[2,130,1]{1,2,0:T(1,128)S(1)}, f32[2,130,1]{1,2,0:T(1,128)S(1)}, u32[]{:S(2)}, u32[]{:S(2)}) %collective-permute-start.11) | collective-permute-done | bytes 1072 | tf_op jit(solution)/shard_map/ppermute | solution.py:38
  60.6 3.1 %collective-permute-start.12 = (f32[3,1,128]{1,2,0:T(8,128)S(1)}, f32[3,1,128]{1,2,0:T(8,128)S(1)}, u32[]{:S(2)}, u32[]{:S(2)}) collective-permute-start(f32[3,1,128]{1,2,0:T(8,128)S(1)} %get-tuple-element.138), channel_id=1, source_target_pairs={{0,16},{16,32},{32,48},{48,64},{64,80},{80,96},{96,112},{1,17},{17... | collective-permute-start | bytes 4616 | tf_op jit(solution)/shard_map/ppermute | solution.py:37
  66.3 4.4 %collective-permute-done.13 = f32[3,1,128]{1,2,0:T(8,128)S(1)} collective-permute-done((f32[3,1,128]{1,2,0:T(8,128)S(1)}, f32[3,1,128]{1,2,0:T(8,128)S(1)}, u32[]{:S(2)}, u32[]{:S(2)}) %collective-permute-start.13) | collective-permute-done | bytes 1568 | tf_op jit(solution)/shard_map/ppermute | solution.py:38
  72.7 3.4 %collective-permute-start.15 = (f32[3,130,1]{1,2,0:T(1,128)S(1)}, f32[3,130,1]{1,2,0:T(1,128)S(1)}, u32[]{:S(2)}, u32[]{:S(2)}) collective-permute-start(f32[3,130,1]{1,2,0:T(1,128)S(1)} %get-tuple-element.91), channel_id=1, source_target_pairs={{1,0},{2,1},{3,2},{4,3},{5,4},{6,5},{7,6},{8,7},{9,8},{10,9},{11,1... | collective-permute-start | bytes 4688 | tf_op jit(solution)/shard_map/ppermute | solution.py:38
  76.1 3.1 %collective-permute-done.15 = f32[3,130,1]{1,2,0:T(1,128)S(1)} collective-permute-done((f32[3,130,1]{1,2,0:T(1,128)S(1)}, f32[3,130,1]{1,2,0:T(1,128)S(1)}, u32[]{:S(2)}, u32[]{:S(2)}) %collective-permute-start.15) | collective-permute-done | bytes 1592 | tf_op jit(solution)/shard_map/ppermute | solution.py:38
  79.7 2.9 %collective-permute-start.16 = (f32[2,1,128]{1,2,0:T(8,128)S(1)}, f32[2,1,128]{1,2,0:T(8,128)S(1)}, u32[]{:S(2)}, u32[]{:S(2)}) collective-permute-start(f32[2,1,128]{1,2,0:T(8,128)S(1)} %get-tuple-element.147), channel_id=1, source_target_pairs={{0,16},{16,32},{32,48},{48,64},{64,80},{80,96},{96,112},{1,17},{17... | collective-permute-start | bytes 3080 | tf_op jit(solution)/shard_map/ppermute | solution.py:37
  84.6 4.3 %collective-permute-done.17 = f32[2,1,128]{1,2,0:T(8,128)S(1)} collective-permute-done((f32[2,1,128]{1,2,0:T(8,128)S(1)}, f32[2,1,128]{1,2,0:T(8,128)S(1)}, u32[]{:S(2)}, u32[]{:S(2)}) %collective-permute-start.17) | collective-permute-done | bytes 1056 | tf_op jit(solution)/shard_map/ppermute | solution.py:38
  90.9 3.4 %collective-permute-start.19 = (f32[2,130,1]{1,2,0:T(1,128)S(1)}, f32[2,130,1]{1,2,0:T(1,128)S(1)}, u32[]{:S(2)}, u32[]{:S(2)}) collective-permute-start(f32[2,130,1]{1,2,0:T(1,128)S(1)} %get-tuple-element.109), channel_id=1, source_target_pairs={{1,0},{2,1},{3,2},{4,3},{5,4},{6,5},{7,6},{8,7},{9,8},{10,9},{11,1... | collective-permute-start | bytes 3128 | tf_op jit(solution)/shard_map/ppermute | solution.py:38
  98.1 2.9 %collective-permute-start.20 = (f32[3,1,128]{1,2,0:T(8,128)S(1)}, f32[3,1,128]{1,2,0:T(8,128)S(1)}, u32[]{:S(2)}, u32[]{:S(2)}) collective-permute-start(f32[3,1,128]{1,2,0:T(8,128)S(1)} %get-tuple-element.136), channel_id=1, source_target_pairs={{0,16},{16,32},{32,48},{48,64},{64,80},{80,96},{96,112},{1,17},{17... | collective-permute-start | bytes 4616 | tf_op jit(solution)/shard_map/ppermute | solution.py:37
  103.6 4.4 %collective-permute-done.21 = f32[3,1,128]{1,2,0:T(8,128)S(1)} collective-permute-done((f32[3,1,128]{1,2,0:T(8,128)S(1)}, f32[3,1,128]{1,2,0:T(8,128)S(1)}, u32[]{:S(2)}, u32[]{:S(2)}) %collective-permute-start.21) | collective-permute-done | bytes 1568 | tf_op jit(solution)/shard_map/ppermute | solution.py:38
  110.0 3.4 %collective-permute-start.23 = (f32[3,130,1]{1,2,0:T(1,128)S(1)}, f32[3,130,1]{1,2,0:T(1,128)S(1)}, u32[]{:S(2)}, u32[]{:S(2)}) collective-permute-start(f32[3,130,1]{1,2,0:T(1,128)S(1)} %get-tuple-element.89), channel_id=1, source_target_pairs={{1,0},{2,1},{3,2},{4,3},{5,4},{6,5},{7,6},{8,7},{9,8},{10,9},{11,1... | collective-permute-start | bytes 4688 | tf_op jit(solution)/shard_map/ppermute | solution.py:38
  114.2 7.0 %all-to-all-start = ((f32[16,1,2]{2,1,0:T(1,128)}), f32[16,1,2]{2,1,0:T(1,128)S(1)}, u32[]{:S(2)}, u32[]{:S(2)}) async-start(f32[16,1,2]{2,1,0:T(1,128)} %bitcast.3), calls=%async_computation | async-start | bytes 16384 | tf_op jit(solution)/shard_map/all_to_all | solution.py:247
  133.2 3.1 %collective-permute-start.26 = (f32[2,130,1]{1,2,0:T(1,128)S(1)}, f32[2,130,1]{1,2,0:T(1,128)S(1)}, u32[]{:S(2)}, u32[]{:S(2)}) collective-permute-start(f32[2,130,1]{1,2,0:T(1,128)S(1)} %get-tuple-element.106), channel_id=1, source_target_pairs={{0,1},{1,2},{2,3},{3,4},{4,5},{5,6},{6,7},{7,8},{8,9},{9,10},{10,1... | collective-permute-start | bytes 3128 | tf_op jit(solution)/shard_map/ppermute | solution.py:37
  144.2 6.1 %all-to-all-start.1 = ((f32[16,2,8,1024]{3,2,1,0:T(8,128)}), f32[16,2,8,1024]{3,2,1,0:T(8,128)}, u32[]{:S(2)}, u32[]{:S(2)}) async-start(f32[16,2,8,1024]{3,2,1,0:T(8,128)} %copy.146), calls=%async_computation.1 | async-start | bytes 2097152 | tf_op jit(solution)/shard_map/all_to_all | solution.py:240
  151.1 5.9 %collective-permute-start.28 = (f32[3,1,128]{1,2,0:T(8,128)}, f32[3,1,128]{1,2,0:T(8,128)}, u32[]{:S(2)}, u32[]{:S(2)}) collective-permute-start(f32[3,1,128]{1,2,0:T(8,128)} %get-tuple-element.134), channel_id=1, source_target_pairs={{0,16},{16,32},{32,48},{48,64},{64,80},{80,96},{96,112},{1,17},{17... | collective-permute-start | bytes 4616 | tf_op jit(solution)/shard_map/ppermute | solution.py:37
  160.3 4.2 %collective-permute-done.29 = f32[3,1,128]{1,2,0:T(8,128)} collective-permute-done((f32[3,1,128]{1,2,0:T(8,128)}, f32[3,1,128]{1,2,0:T(8,128)}, u32[]{:S(2)}, u32[]{:S(2)}) %collective-permute-start.29) | collective-permute-done | bytes 1568 | tf_op jit(solution)/shard_map/ppermute | solution.py:38
  166.0 3.2 %collective-permute-start.30 = (f32[3,130,1]{1,2,0:T(1,128)}, f32[3,130,1]{1,2,0:T(1,128)}, u32[]{:S(2)}, u32[]{:S(2)}) collective-permute-start(f32[3,130,1]{1,2,0:T(1,128)} %get-tuple-element.86), channel_id=1, source_target_pairs={{0,1},{1,2},{2,3},{3,4},{4,5},{5,6},{6,7},{7,8},{8,9},{9,10},{10,1... | collective-permute-start | bytes 4688 | tf_op jit(solution)/shard_map/ppermute | solution.py:37
  179.2 6.4 %broadcast_multiply_fusion.1 = (f32[32,1,1024]{2,1,0:T(1,128)S(1)}, f32[32,1,1024]{2,1,0:T(1,128)S(1)}, f32[32,1,1024]{2,1,0:T(1,128)S(1)}, f32[32,1,1024]{2,1,0...) fusion(f32[32,8,1024]{2,1,0:T(8,128)} %bitcast.7), kind=kLoop, calls=%fused_computation.393 | loop fusion | flops 622592 | bytes 3407872 | tf_op jit(solution)/shard_map/mul | solution.py:117
  187.5 3.6 %multiply_divide_fusion.2 = (f32[32,5,1024]{2,0,1:T(8,128)S(1)}, f32[32,5,1024]{2,0,1:T(8,128)S(1)}, f32[32,5,1024]{2,0,1:T(8,128)S(1)}, f32[32,5,1024]{2,0,1:T(...) fusion(f32[32,5,10,1024]{3,0,2,1:T(8,128)S(1)} %bitcast.526, ...), kind=kLoop, calls=%fused_computation.139 | loop fusion | flops 20807680 | bytes 16515072 | tf_op jit(solution)/shard_map/div | solution.py:97
  193.9 4.7 %fusion.80 = (f32[32,1024]{1,0:T(8,128)S(1)}, f32[32,5,1024]{2,0,1:T(8,128)S(1)}, f32[32,5,1024]{2,0,1:T(8,128)}, f32[32,5,1024]{2,0,1:T(8,128)}, f32[32,5,1024]...) fusion(f32[32,5,1024]{2,0,1:T(8,128)S(1)} %copy-done.8, ...), kind=kLoop, calls=%fused_computation.117 | loop fusion | flops 19955712 | bytes 23855104 | tf_op jit(solution)/shard_map/reduce_sum | solution.py:120
  219.5 6.1 %all-to-all-start.2 = ((f32[16,2,8,1024]{3,1,2,0:T(2,128)}), f32[16,2,8,1024]{3,1,2,0:T(2,128)}, u32[]{:S(2)}, u32[]{:S(2)}) async-start(f32[16,2,8,1024]{3,1,2,0:T(2,128)} %copy.166), calls=%async_computation.2 | async-start | bytes 2097152 | tf_op jit(solution)/shard_map/all_to_all | solution.py:259
  239.7 7.3 %broadcast_select_fusion = f32[32,5,10,1024]{3,0,2,1:T(8,128)} fusion(f32[32,5,10,1024]{3,0,2,1:T(8,128)} %bitcast_dynamic-update-slice_fusion.9, f32[32,5,10,1024]{3,0,2,1:T(8,128)S(1)} %bitcast.528, pred[32]{0:T(512)(128)(4,1)S(1)} %gt.16), kind=kLoop, calls=%fused_computation | loop fusion | flops 1638400 | bytes 19660832 | tf_op jit(solution)/shard_map/jit(_where)/select_n | solution.py:256
  251.3 10.5 %convolution_bitcast_fusion = f32[8,4,32,4,32]{4,3,2,0,1:T(4,128)S(1)} fusion(f32[8,32,32,32,1]{3,2,1,0,4:T(8,128)} %bitcast.529, s32[4,4]{1,0:T(4,128)S(1)} %eq.71, pred[4,4]{1,0:T(4,128)(4,1)S(1)} %copy-done.21), kind=kOutput, calls=%fused_computation.1 | convolution fusion | flops 50332672 | bytes 1572944 | tf_op jit(solution)/shard_map/bs,sfc->bfc/dot_general | solution.py:267
  (228 shorter events, 123.7 us)
Async XLA Ops:
  1.5 6.9 %collective-permute-start = (f32[2,1,128]{1,2,0:T(8,128)S(1)}, f32[2,1,128]{1,2,0:T(8,128)S(1)}, u32[]{:S(2)}, u32[]{:S(2)}) collective-permute-start(f32[2,1,128]{1,2,0:T(8,128)S(1)} %copy.173), channel_id=1, source_target_pairs={{0,16},{16,32},{32,48},{48,64},{64,80},{80,96},{96,112},{1,17},{17... | collective-permute-start | bytes 3080 | tf_op jit(solution)/shard_map/ppermute | solution.py:37
  5.5 6.3 %collective-permute-start.1 = (f32[2,1,128]{1,2,0:T(8,128)S(1)}, f32[2,1,128]{1,2,0:T(8,128)S(1)}, u32[]{:S(2)}, u32[]{:S(2)}) collective-permute-start(f32[2,1,128]{1,2,0:T(8,128)S(1)} %copy.174), channel_id=1, source_target_pairs={{16,0},{32,16},{48,32},{64,48},{80,64},{96,80},{112,96},{17,1},{33... | collective-permute-start | bytes 3080 | tf_op jit(solution)/shard_map/ppermute | solution.py:38
  11.8 7.6 %collective-permute-start.2 = (f32[2,130,1]{1,2,0:T(1,128)S(1)}, f32[2,130,1]{1,2,0:T(1,128)S(1)}, u32[]{:S(2)}, u32[]{:S(2)}) collective-permute-start(f32[2,130,1]{1,2,0:T(1,128)S(1)} %get-tuple-element.112), channel_id=1, source_target_pairs={{0,1},{1,2},{2,3},{3,4},{4,5},{5,6},{6,7},{7,8},{8,9},{9,10},{10,1... | collective-permute-start | bytes 3128 | tf_op jit(solution)/shard_map/ppermute | solution.py:37
  15.3 6.4 %collective-permute-start.3 = (f32[2,130,1]{1,2,0:T(1,128)S(1)}, f32[2,130,1]{1,2,0:T(1,128)S(1)}, u32[]{:S(2)}, u32[]{:S(2)}) collective-permute-start(f32[2,130,1]{1,2,0:T(1,128)S(1)} %get-tuple-element.113), channel_id=1, source_target_pairs={{1,0},{2,1},{3,2},{4,3},{5,4},{6,5},{7,6},{8,7},{9,8},{10,9},{11,1... | collective-permute-start | bytes 3128 | tf_op jit(solution)/shard_map/ppermute | solution.py:38
  22.4 6.1 %collective-permute-start.4 = (f32[3,1,128]{1,2,0:T(8,128)S(1)}, f32[3,1,128]{1,2,0:T(8,128)S(1)}, u32[]{:S(2)}, u32[]{:S(2)}) collective-permute-start(f32[3,1,128]{1,2,0:T(8,128)S(1)} %get-tuple-element.140), channel_id=1, source_target_pairs={{0,16},{16,32},{32,48},{48,64},{64,80},{80,96},{96,112},{1,17},{17... | collective-permute-start | bytes 4616 | tf_op jit(solution)/shard_map/ppermute | solution.py:37
  25.6 7.0 %collective-permute-start.5 = (f32[3,1,128]{1,2,0:T(8,128)S(1)}, f32[3,1,128]{1,2,0:T(8,128)S(1)}, u32[]{:S(2)}, u32[]{:S(2)}) collective-permute-start(f32[3,1,128]{1,2,0:T(8,128)S(1)} %get-tuple-element.141), channel_id=1, source_target_pairs={{16,0},{32,16},{48,32},{64,48},{80,64},{96,80},{112,96},{17,1},{33... | collective-permute-start | bytes 4616 | tf_op jit(solution)/shard_map/ppermute | solution.py:38
  32.7 6.2 %collective-permute-start.6 = (f32[3,130,1]{1,2,0:T(1,128)S(1)}, f32[3,130,1]{1,2,0:T(1,128)S(1)}, u32[]{:S(2)}, u32[]{:S(2)}) collective-permute-start(f32[3,130,1]{1,2,0:T(1,128)S(1)} %get-tuple-element.92), channel_id=1, source_target_pairs={{0,1},{1,2},{2,3},{3,4},{4,5},{5,6},{6,7},{7,8},{8,9},{9,10},{10,1... | collective-permute-start | bytes 4688 | tf_op jit(solution)/shard_map/ppermute | solution.py:37
  35.0 6.5 %collective-permute-start.7 = (f32[3,130,1]{1,2,0:T(1,128)S(1)}, f32[3,130,1]{1,2,0:T(1,128)S(1)}, u32[]{:S(2)}, u32[]{:S(2)}) collective-permute-start(f32[3,130,1]{1,2,0:T(1,128)S(1)} %get-tuple-element.93), channel_id=1, source_target_pairs={{1,0},{2,1},{3,2},{4,3},{5,4},{6,5},{7,6},{8,7},{9,8},{10,9},{11,1... | collective-permute-start | bytes 4688 | tf_op jit(solution)/shard_map/ppermute | solution.py:38
  45.2 6.3 %collective-permute-start.9 = (f32[2,1,128]{1,2,0:T(8,128)S(1)}, f32[2,1,128]{1,2,0:T(8,128)S(1)}, u32[]{:S(2)}, u32[]{:S(2)}) collective-permute-start(f32[2,1,128]{1,2,0:T(8,128)S(1)} %get-tuple-element.150), channel_id=1, source_target_pairs={{16,0},{32,16},{48,32},{64,48},{80,64},{96,80},{112,96},{17,1},{33... | collective-permute-start | bytes 3080 | tf_op jit(solution)/shard_map/ppermute | solution.py:38
  51.6 5.3 %collective-permute-start.10 = (f32[2,130,1]{1,2,0:T(1,128)S(1)}, f32[2,130,1]{1,2,0:T(1,128)S(1)}, u32[]{:S(2)}, u32[]{:S(2)}) collective-permute-start(f32[2,130,1]{1,2,0:T(1,128)S(1)} %get-tuple-element.110), channel_id=1, source_target_pairs={{0,1},{1,2},{2,3},{3,4},{4,5},{5,6},{6,7},{7,8},{8,9},{9,10},{10,1... | collective-permute-start | bytes 3128 | tf_op jit(solution)/shard_map/ppermute | solution.py:37
  53.5 6.4 %collective-permute-start.11 = (f32[2,130,1]{1,2,0:T(1,128)S(1)}, f32[2,130,1]{1,2,0:T(1,128)S(1)}, u32[]{:S(2)}, u32[]{:S(2)}) collective-permute-start(f32[2,130,1]{1,2,0:T(1,128)S(1)} %get-tuple-element.111), channel_id=1, source_target_pairs={{1,0},{2,1},{3,2},{4,3},{5,4},{6,5},{7,6},{8,7},{9,8},{10,9},{11,1... | collective-permute-start | bytes 3128 | tf_op jit(solution)/shard_map/ppermute | solution.py:38
  60.6 5.7 %collective-permute-start.12 = (f32[3,1,128]{1,2,0:T(8,128)S(1)}, f32[3,1,128]{1,2,0:T(8,128)S(1)}, u32[]{:S(2)}, u32[]{:S(2)}) collective-permute-start(f32[3,1,128]{1,2,0:T(8,128)S(1)} %get-tuple-element.138), channel_id=1, source_target_pairs={{0,16},{16,32},{32,48},{48,64},{64,80},{80,96},{96,112},{1,17},{17... | collective-permute-start | bytes 4616 | tf_op jit(solution)/shard_map/ppermute | solution.py:37
  63.7 7.0 %collective-permute-start.13 = (f32[3,1,128]{1,2,0:T(8,128)S(1)}, f32[3,1,128]{1,2,0:T(8,128)S(1)}, u32[]{:S(2)}, u32[]{:S(2)}) collective-permute-start(f32[3,1,128]{1,2,0:T(8,128)S(1)} %get-tuple-element.139), channel_id=1, source_target_pairs={{16,0},{32,16},{48,32},{64,48},{80,64},{96,80},{112,96},{17,1},{33... | collective-permute-start | bytes 4616 | tf_op jit(solution)/shard_map/ppermute | solution.py:38
  72.7 6.5 %collective-permute-start.15 = (f32[3,130,1]{1,2,0:T(1,128)S(1)}, f32[3,130,1]{1,2,0:T(1,128)S(1)}, u32[]{:S(2)}, u32[]{:S(2)}) collective-permute-start(f32[3,130,1]{1,2,0:T(1,128)S(1)} %get-tuple-element.91), channel_id=1, source_target_pairs={{1,0},{2,1},{3,2},{4,3},{5,4},{6,5},{7,6},{8,7},{9,8},{10,9},{11,1... | collective-permute-start | bytes 4688 | tf_op jit(solution)/shard_map/ppermute | solution.py:38
  82.6 6.3 %collective-permute-start.17 = (f32[2,1,128]{1,2,0:T(8,128)S(1)}, f32[2,1,128]{1,2,0:T(8,128)S(1)}, u32[]{:S(2)}, u32[]{:S(2)}) collective-permute-start(f32[2,1,128]{1,2,0:T(8,128)S(1)} %get-tuple-element.148), channel_id=1, source_target_pairs={{16,0},{32,16},{48,32},{64,48},{80,64},{96,80},{112,96},{17,1},{33... | collective-permute-start | bytes 3080 | tf_op jit(solution)/shard_map/ppermute | solution.py:38
  89.0 5.5 %collective-permute-start.18 = (f32[2,130,1]{1,2,0:T(1,128)S(1)}, f32[2,130,1]{1,2,0:T(1,128)S(1)}, u32[]{:S(2)}, u32[]{:S(2)}) collective-permute-start(f32[2,130,1]{1,2,0:T(1,128)S(1)} %get-tuple-element.108), channel_id=1, source_target_pairs={{0,1},{1,2},{2,3},{3,4},{4,5},{5,6},{6,7},{7,8},{8,9},{9,10},{10,1... | collective-permute-start | bytes 3128 | tf_op jit(solution)/shard_map/ppermute | solution.py:37
  90.9 6.4 %collective-permute-start.19 = (f32[2,130,1]{1,2,0:T(1,128)S(1)}, f32[2,130,1]{1,2,0:T(1,128)S(1)}, u32[]{:S(2)}, u32[]{:S(2)}) collective-permute-start(f32[2,130,1]{1,2,0:T(1,128)S(1)} %get-tuple-element.109), channel_id=1, source_target_pairs={{1,0},{2,1},{3,2},{4,3},{5,4},{6,5},{7,6},{8,7},{9,8},{10,9},{11,1... | collective-permute-start | bytes 3128 | tf_op jit(solution)/shard_map/ppermute | solution.py:38
  98.1 5.5 %collective-permute-start.20 = (f32[3,1,128]{1,2,0:T(8,128)S(1)}, f32[3,1,128]{1,2,0:T(8,128)S(1)}, u32[]{:S(2)}, u32[]{:S(2)}) collective-permute-start(f32[3,1,128]{1,2,0:T(8,128)S(1)} %get-tuple-element.136), channel_id=1, source_target_pairs={{0,16},{16,32},{32,48},{48,64},{64,80},{80,96},{96,112},{1,17},{17... | collective-permute-start | bytes 4616 | tf_op jit(solution)/shard_map/ppermute | solution.py:37
  101.0 7.0 %collective-permute-start.21 = (f32[3,1,128]{1,2,0:T(8,128)S(1)}, f32[3,1,128]{1,2,0:T(8,128)S(1)}, u32[]{:S(2)}, u32[]{:S(2)}) collective-permute-start(f32[3,1,128]{1,2,0:T(8,128)S(1)} %get-tuple-element.137), channel_id=1, source_target_pairs={{16,0},{32,16},{48,32},{64,48},{80,64},{96,80},{112,96},{17,1},{33... | collective-permute-start | bytes 4616 | tf_op jit(solution)/shard_map/ppermute | solution.py:38
  108.1 13.1 %collective-permute-start.22 = (f32[3,130,1]{1,2,0:T(1,128)S(1)}, f32[3,130,1]{1,2,0:T(1,128)S(1)}, u32[]{:S(2)}, u32[]{:S(2)}) collective-permute-start(f32[3,130,1]{1,2,0:T(1,128)S(1)} %get-tuple-element.88), channel_id=1, source_target_pairs={{0,1},{1,2},{2,3},{3,4},{4,5},{5,6},{6,7},{7,8},{8,9},{9,10},{10,1... | collective-permute-start | bytes 4688 | tf_op jit(solution)/shard_map/ppermute | solution.py:37
  110.0 11.1 %collective-permute-start.23 = (f32[3,130,1]{1,2,0:T(1,128)S(1)}, f32[3,130,1]{1,2,0:T(1,128)S(1)}, u32[]{:S(2)}, u32[]{:S(2)}) collective-permute-start(f32[3,130,1]{1,2,0:T(1,128)S(1)} %get-tuple-element.89), channel_id=1, source_target_pairs={{1,0},{2,1},{3,2},{4,3},{5,4},{6,5},{7,6},{8,7},{9,8},{10,9},{11,1... | collective-permute-start | bytes 4688 | tf_op jit(solution)/shard_map/ppermute | solution.py:38
  114.2 30.0 %all-to-all-start = ((f32[16,1,2]{2,1,0:T(1,128)}), f32[16,1,2]{2,1,0:T(1,128)S(1)}, u32[]{:S(2)}, u32[]{:S(2)}) async-start(f32[16,1,2]{2,1,0:T(1,128)} %bitcast.3), calls=%async_computation | async-start | bytes 16384 | tf_op jit(solution)/shard_map/all_to_all | solution.py:247
  122.4 9.9 %collective-permute-start.24 = (f32[2,1,128]{1,2,0:T(8,128)}, f32[2,1,128]{1,2,0:T(8,128)S(1)}, u32[]{:S(2)}, u32[]{:S(2)}) collective-permute-start(f32[2,1,128]{1,2,0:T(8,128)} %get-tuple-element.145), channel_id=1, source_target_pairs={{0,16},{16,32},{32,48},{48,64},{64,80},{80,96},{96,112},{1,17},{17... | collective-permute-start | bytes 3080 | tf_op jit(solution)/shard_map/ppermute | solution.py:37
  125.3 7.0 %collective-permute-start.25 = (f32[2,1,128]{1,2,0:T(8,128)}, f32[2,1,128]{1,2,0:T(8,128)}, u32[]{:S(2)}, u32[]{:S(2)}) collective-permute-start(f32[2,1,128]{1,2,0:T(8,128)} %get-tuple-element.146), channel_id=1, source_target_pairs={{16,0},{32,16},{48,32},{64,48},{80,64},{96,80},{112,96},{17,1},{33... | collective-permute-start | bytes 3080 | tf_op jit(solution)/shard_map/ppermute | solution.py:38
  133.2 7.5 %collective-permute-start.26 = (f32[2,130,1]{1,2,0:T(1,128)S(1)}, f32[2,130,1]{1,2,0:T(1,128)S(1)}, u32[]{:S(2)}, u32[]{:S(2)}) collective-permute-start(f32[2,130,1]{1,2,0:T(1,128)S(1)} %get-tuple-element.106), channel_id=1, source_target_pairs={{0,1},{1,2},{2,3},{3,4},{4,5},{5,6},{6,7},{7,8},{8,9},{9,10},{10,1... | collective-permute-start | bytes 3128 | tf_op jit(solution)/shard_map/ppermute | solution.py:37
  136.3 6.4 %collective-permute-start.27 = (f32[2,130,1]{1,2,0:T(1,128)S(1)}, f32[2,130,1]{1,2,0:T(1,128)S(1)}, u32[]{:S(2)}, u32[]{:S(2)}) collective-permute-start(f32[2,130,1]{1,2,0:T(1,128)S(1)} %get-tuple-element.107), channel_id=1, source_target_pairs={{1,0},{2,1},{3,2},{4,3},{5,4},{6,5},{7,6},{8,7},{9,8},{10,9},{11,1... | collective-permute-start | bytes 3128 | tf_op jit(solution)/shard_map/ppermute | solution.py:38
  144.2 35.0 %all-to-all-start.1 = ((f32[16,2,8,1024]{3,2,1,0:T(8,128)}), f32[16,2,8,1024]{3,2,1,0:T(8,128)}, u32[]{:S(2)}, u32[]{:S(2)}) async-start(f32[16,2,8,1024]{3,2,1,0:T(8,128)} %copy.146), calls=%async_computation.1 | async-start | bytes 2097152 | tf_op jit(solution)/shard_map/all_to_all | solution.py:240
  151.1 9.1 %collective-permute-start.28 = (f32[3,1,128]{1,2,0:T(8,128)}, f32[3,1,128]{1,2,0:T(8,128)}, u32[]{:S(2)}, u32[]{:S(2)}) collective-permute-start(f32[3,1,128]{1,2,0:T(8,128)} %get-tuple-element.134), channel_id=1, source_target_pairs={{0,16},{16,32},{32,48},{48,64},{64,80},{80,96},{96,112},{1,17},{17... | collective-permute-start | bytes 4616 | tf_op jit(solution)/shard_map/ppermute | solution.py:37
  157.0 7.5 %collective-permute-start.29 = (f32[3,1,128]{1,2,0:T(8,128)}, f32[3,1,128]{1,2,0:T(8,128)}, u32[]{:S(2)}, u32[]{:S(2)}) collective-permute-start(f32[3,1,128]{1,2,0:T(8,128)} %get-tuple-element.135), channel_id=1, source_target_pairs={{16,0},{32,16},{48,32},{64,48},{80,64},{96,80},{112,96},{17,1},{33... | collective-permute-start | bytes 4616 | tf_op jit(solution)/shard_map/ppermute | solution.py:38
  166.0 7.7 %collective-permute-start.30 = (f32[3,130,1]{1,2,0:T(1,128)}, f32[3,130,1]{1,2,0:T(1,128)}, u32[]{:S(2)}, u32[]{:S(2)}) collective-permute-start(f32[3,130,1]{1,2,0:T(1,128)} %get-tuple-element.86), channel_id=1, source_target_pairs={{0,1},{1,2},{2,3},{3,4},{4,5},{5,6},{6,7},{7,8},{8,9},{9,10},{10,1... | collective-permute-start | bytes 4688 | tf_op jit(solution)/shard_map/ppermute | solution.py:37
  169.2 6.8 %collective-permute-start.31 = (f32[3,130,1]{1,2,0:T(1,128)}, f32[3,130,1]{1,2,0:T(1,128)}, u32[]{:S(2)}, u32[]{:S(2)}) collective-permute-start(f32[3,130,1]{1,2,0:T(1,128)} %get-tuple-element.87), channel_id=1, source_target_pairs={{1,0},{2,1},{3,2},{4,3},{5,4},{6,5},{7,6},{8,7},{9,8},{10,9},{11,1... | collective-permute-start | bytes 4688 | tf_op jit(solution)/shard_map/ppermute | solution.py:38
  219.5 27.5 %all-to-all-start.2 = ((f32[16,2,8,1024]{3,1,2,0:T(2,128)}), f32[16,2,8,1024]{3,1,2,0:T(2,128)}, u32[]{:S(2)}, u32[]{:S(2)}) async-start(f32[16,2,8,1024]{3,1,2,0:T(2,128)} %copy.166), calls=%async_computation.2 | async-start | bytes 2097152 | tf_op jit(solution)/shard_map/all_to_all | solution.py:259
  (30 other events, 605.8 us)
where the time goes:
time: 267 us; the launch traced here: 264 us
  starting transfers between devices  105 us (39%)
  local copies, waits for them, and re-layouts  56.7 us (21%)
  waiting for transfers between devices  48.2 us (18%)
  other arithmetic  40.9 us (15%)
  matrix products  11.1 us (4%)
    ppermute x16, starting transfers between devices, padded_2(): before = lax.ppermute(last, axis, up)  47.5 us
    ppermute x16, waiting for transfers between devices, padded_2(): after = lax.ppermute(leading, axis, down)  47.4 us
    ppermute x16, starting transfers between devices, padded_2(): after = lax.ppermute(leading, axis, down)  38.2 us
    unnamed x91, local copies, waits for them, and re-layouts  24.1 us
    another operation x10, local copies, waits for them, and re-layouts, column_step(): jnp.stack([jnp.sum(cat_area * term_value, axis=1) for term_value in flux_...  11.8 us
    dot_general x1, matrix products, local(): jnp.einsum('bs,sfc->bfc', own_choose, returned, precision=lax.Precision.H...  10.5 us
    select_n x1, other arithmetic, local(): jnp.where(occupied_mask[:, None, None, None] > 0.5, advanced_warmth, leve...  7.29 us
    all_to_all x1, starting transfers between devices, local(): lax.all_to_all(flags.reshape(group_size, CAP), 'gy', split_axis=0, concat...  6.98 us
  transfers between devices with their start and end apart: 35, of which 16 were waited for; matrix products, arithmetic and copies ran while one was open for 18% of the time, Pallas kernels for 0%

commit v1 on v0

v1 whole, which is shorter than its diff:
```python
import jax
import jax.numpy as jnp
from jax import lax
from jax.experimental import pallas as pl
from jax.experimental.pallas import tpu as pltpu
from jax.sharding import PartitionSpec as P

B = 16
CAP = 2
NSEND = 6
NBACK = 7
NF = 10
SUB = 4
NCAT = 5
NLAY = 10
NSNOW = 3
ROWS_OUT = NSEND * 8
ROWS_BACK = NBACK * 8

F32 = jnp.float32
VM = pltpu.VMEM
VSPEC = pl.BlockSpec(memory_space=pltpu.VMEM)
SSPEC = pl.BlockSpec(memory_space=pltpu.SMEM)


def lane_groups():
    return lax.broadcasted_iota(jnp.int32, (8, 128), 1) // 32


def swap_groups(rows, group):
    low = group < 2
    even = (group & 1) == 0
    v0, v1, v2, v3 = rows

    def roll(x, s):
        return pltpu.roll(x, s, 1)

    a0 = jnp.where(low, v0, roll(v2, 64))
    a2 = jnp.where(low, roll(v0, 64), v2)
    a1 = jnp.where(low, v1, roll(v3, 64))
    a3 = jnp.where(low, roll(v1, 64), v3)
    return (
        jnp.where(even, a0, roll(a1, 32)),
        jnp.where(even, roll(a0, 96), a1),
        jnp.where(even, a2, roll(a3, 32)),
        jnp.where(even, roll(a2, 96), a3),
    )


def block_slots(own, land, count):
    for o in range(B):
        count[o] = 0
    slots = []
    for b in range(B):
        o = own[b]
        r = count[o]
        slots.append(jnp.minimum(o * CAP + r, B * CAP - 1))
        count[o] = r + 1 - land[b]
    return slots


def pack_kernel(own, land, x, out, count):
    out[...] = jnp.zeros_like(out)
    slots = block_slots(own, land, count)
    group = lane_groups()
    for bx in range(4):
        def rows(f):
            return [x[f, pl.ds(32 * bx + q, 8, stride=4), :] for q in range(4)]

        visible, near_red, longwave = rows(3), rows(4), rows(5)
        fields = [
            rows(0),
            rows(1),
            rows(2),
            [0.25 * a + 0.45 * b + 0.3 * c for a, b, c in zip(visible, near_red, longwave)],
            rows(6),
            [1.0 / (1.0 + 2.0 * w) for w in rows(7)],
        ]
        blocks = [swap_groups(r, group) for r in fields]
        for by in range(4):
            b = 4 * bx + by

            @pl.when(land[b] == 0)
            def _():
                for f in range(NSEND):
                    out[pl.ds(pl.multiple_of(slots[b] * ROWS_OUT + f * 8, 8), 8), :] = blocks[f][by]


def pack(own, land, conditions):
    return pl.pallas_call(
        pack_kernel,
        out_shape=jax.ShapeDtypeStruct((B * CAP * ROWS_OUT, 128), F32),
        in_specs=[SSPEC, SSPEC, VSPEC],
        out_specs=VSPEC,
        scratch_shapes=[pltpu.SMEM((B,), jnp.int32)],
        name="pack",
    )(own, land, conditions)


def one_column(temps, share, floe, snow_depth, forcing, sig):
    ocean, air, source_top, top_resist = forcing
    h14 = floe * (1.0 / 14.0)
    h27 = floe * (2.0 / 7.0)
    h47 = floe * (4.0 / 7.0)
    m_snow = snow_depth * (2.0 / 3.0)
    half_snow = snow_depth * (0.5 / 0.9)
    g_snow = 0.9 / snow_depth
    g_top = 1.0 / (half_snow + top_resist)
    inv_cond = []
    mass = [m_snow] * NSNOW
    for j in range(NLAY - NSNOW):
        t = temps[NSNOW + j]
        inv_cond.append(1.0 / (2.0 + sig[j] / (t - 0.5)))
        mass.append(h27 + h47 * (sig[j] / (t * t + 0.1)))
    cond = [g_snow, g_snow, 1.0 / (half_snow + h14 * inv_cond[0])]
    for j in range(NLAY - NSNOW - 1):
        cond.append(1.0 / (h14 * (inv_cond[j] + inv_cond[j + 1])))
    g_bot = 1.0 / (h14 * inv_cond[-1])
    ratios = []
    values = []
    u = mass[0] + g_top
    held = mass[0] * temps[0]
    y = held + g_top * air + source_top
    for l in range(NLAY):
        below = cond[l] if l < NLAY - 1 else g_bot
        pivot = 1.0 / (u + below)
        ratio = below * pivot
        if l < NLAY - 1:
            ratios.append(ratio)
            values.append(y * pivot)
            u = mass[l + 1] + ratio * u
            mt = mass[l + 1] * temps[l + 1]
            held = held + mt
            y = mt + ratio * y
        else:
            last = y * pivot + ratio * ocean
    solved = [last]
    for l in range(NLAY - 2, -1, -1):
        solved.insert(0, values[l] + ratios[l] * solved[0])
    bottom = share * (g_bot * (last - ocean))
    top = share * (g_top * (air - solved[0]))
    light = share * jnp.exp(-5.0 * snow_depth - 1.5 * floe)
    return solved, (
        bottom,
        top,
        light,
        share * solved[0],
        share * snow_depth,
        share * floe,
        share * held,
        share,
    )


def column_kernel(warm, share, floe, drift, recv, new_warm, flux):
    half = pl.program_id(1)

    def tile(k, carry):
        lanes = pl.ds(pl.multiple_of(k * 128, 128), 128)
        kk = half * 4 + k

        def field(f):
            return recv[pl.ds(f * 8 + kk, 8, stride=ROWS_OUT), :]

        ocean, salinity, air, source_top, snowfall, top_resist = [field(f) for f in range(NSEND)]
        filled = salinity > 0.25
        sig = [salinity * (0.02 + 0.01 * j) for j in range(NLAY - NSNOW)]
        snow_add = 0.3 * snowfall
        sums = None
        for c in range(NCAT):
            temps = [warm[c, l, :, lanes] for l in range(NLAY)]
            solved, terms = one_column(
                temps,
                share[c, :, lanes],
                floe[c, :, lanes],
                drift[c, :, lanes] + snow_add,
                (ocean, air, source_top, top_resist),
                sig,
            )
            for l in range(NLAY):
                new_warm[c, l, :, lanes] = jnp.where(filled, solved[l], temps[l])
            sums = terms if sums is None else tuple(a + b for a, b in zip(sums, terms))
        bottom, top, light, surface, snow, thick, held, total = sums
        back = (
            bottom,
            top,
            light,
            surface,
            snow,
            thick - 0.05 * bottom,
            0.05 * (held + top - bottom + source_top * total),
        )
        for f in range(NBACK):
            flux[pl.ds(f * 8 + kk, 8, stride=ROWS_BACK), :] = back[f]
        return carry

    lax.fori_loop(0, 4, tile, 0)


def columns(warm, share, floe, drift, recv):
    cls = pl.BlockSpec((NCAT, 8, 512), lambda g, h: (0, g, h))
    col = pl.BlockSpec((NCAT, NLAY, 8, 512), lambda g, h: (0, 0, g, h))
    return pl.pallas_call(
        column_kernel,
        grid=(4, 2),
        out_shape=(
            jax.ShapeDtypeStruct((NCAT, NLAY, 32, 1024), F32),
            jax.ShapeDtypeStruct((B * CAP * ROWS_BACK, 128), F32),
        ),
        in_specs=[col, cls, cls, cls, pl.BlockSpec((8 * ROWS_OUT, 128), lambda g, h: (g, 0))],
        out_specs=(col, pl.BlockSpec((8 * ROWS_BACK, 128), lambda g, h: (g, 0))),
        name="columns",
    )(warm, share, floe, drift, recv)


def unpack_kernel(own, land, back, salinity, visible, out, count):
    slots = block_slots(own, land, count)
    group = lane_groups()
    for bx in range(4):
        rows = []
        for f in range(NBACK):
            blocks = []
            for by in range(4):
                b = 4 * bx + by
                v = back[pl.ds(pl.multiple_of(slots[b] * ROWS_BACK + f * 8, 8), 8), :]
                blocks.append(jnp.where(land[b] == 0, v, 0.0))
            rows.append(swap_groups(blocks, group))
        for q in range(4):
            at = pl.ds(32 * bx + q, 8, stride=4)
            sal = salinity[0, at, :]
            vis = visible[0, at, :]
            for f in range(NBACK):
                v = rows[f][q]
                out[f, at, :] = (0.7 * vis) * v if f == 2 else v
            out[7, at, :] = (-0.05 * sal) * rows[0][q]


def unpack(own, land, back, conditions):
    return pl.pallas_call(
        unpack_kernel,
        grid=(1,),
        out_shape=jax.ShapeDtypeStruct((8, 128, 128), F32),
        in_specs=[
            SSPEC,
            SSPEC,
            pl.BlockSpec((B * CAP * ROWS_BACK, 128), lambda i: (0, 0)),
            pl.BlockSpec((1, 128, 128), lambda i: (1, 0, 0)),
            pl.BlockSpec((1, 128, 128), lambda i: (3, 0, 0)),
        ],
        out_specs=pl.BlockSpec((8, 128, 128), lambda i: (0, 0, 0)),
        scratch_shapes=[pltpu.SMEM((B,), jnp.int32)],
        name="unpack",
    )(own, land, back, conditions, conditions)


def prepare_kernel(land, vel, stress, drive, weight, pressure, coef, up, down):
    group = lax.broadcasted_iota(jnp.int32, (32, 128), 1) // 32
    for bx in range(4):
        at = pl.ds(32 * bx, 32)
        water = jnp.zeros((32, 128), F32)
        for by in range(4):
            water = jnp.where(group == by, (1 - land[4 * bx + by]).astype(F32), water)
        w = weight[at, :]
        scale = water / (w + 0.5)
        beta = 0.5 * scale
        coef[0, at, :] = pressure[at, :] * (1.0 / 3.0)
        coef[1, at, :] = scale * w
        coef[2, at, :] = 0.25 * beta
        coef[3, at, :] = beta * (drive[0, at, :] + drive[2, at, :])
        coef[4, at, :] = beta * (drive[1, at, :] + drive[3, at, :])
    for rows, dst in ((pl.ds(0, 8), up), (pl.ds(120, 8), down)):
        dst[0:2] = vel[:, rows, :]
        dst[2:5] = stress[:, rows, :]
        dst[5:10] = coef[:, rows, :]


def prepare(land, vel, stress, drive, weight, pressure):
    edge = jax.ShapeDtypeStruct((NF, 8, 128), F32)
    return pl.pallas_call(
        prepare_kernel,
        out_shape=(jax.ShapeDtypeStruct((5, 128, 128), F32), edge, edge),
        in_specs=[SSPEC] + [VSPEC] * 5,
        out_specs=(VSPEC, VSPEC, VSPEC),
        name="prepare",
    )(land, vel, stress, drive, weight, pressure)


NPACK = 12


def field_tile(f, t, vel, stress, coef, top, bottom):
    if t == 0:
        return top[f]
    if t == 17:
        return bottom[f]
    rows = slice(8 * (t - 1), 8 * t)
    if f < 2:
        return vel[f, rows, :]
    if f < 5:
        return stress[f - 2, rows, :]
    return coef[f - 5, rows, :]


def edges_kernel(vel, stress, coef, top, bottom, left, right):
    piece = lax.broadcasted_iota(jnp.int32, (8, 128), 1) // 8
    for v in range(NPACK):
        to_left = jnp.zeros((8, 128), F32)
        to_right = jnp.zeros((8, 128), F32)
        for i in range(16):
            n = 16 * v + i
            if n >= NF * 18:
                break
            x = field_tile(n // 18, n % 18, vel, stress, coef, top, bottom)
            xl = pltpu.roll(x, 8 * i, 1) if i else x
            xr = pltpu.roll(x, (8 * i + 8) % 128, 1) if i < 15 else x
            to_left = jnp.where(piece == i, xl, to_left)
            to_right = jnp.where(piece == i, xr, to_right)
        left[v] = to_left
        right[v] = to_right


def edges(vel, stress, coef, top, bottom):
    side = jax.ShapeDtypeStruct((NPACK, 8, 128), F32)
    return pl.pallas_call(
        edges_kernel,
        out_shape=(side, side),
        in_specs=[VSPEC] * 5,
        out_specs=(VSPEC, VSPEC),
        name="edges",
    )(vel, stress, coef, top, bottom)


GUARD = 8


def evp_kernel(vel, stress, coef, top, bottom, left, right, vel_out, stress_out, ext):
    lane = lax.broadcasted_iota(jnp.int32, (8, 128), 1)
    for f in range(NF):
        ext[f, 0:8, :] = jnp.zeros((8, 256), F32)
        ext[f, 152:160, :] = jnp.zeros((8, 256), F32)
        for t in range(18):
            n = f * 18 + t
            v, i = divmod(n, 16)
            rows = slice(GUARD + 8 * t, GUARD + 8 * t + 8)
            ext[f, rows, 0:128] = field_tile(f, t, vel, stress, coef, top, bottom)
            from_right = pltpu.roll(right[v], (128 - 8 * i) % 128, 1) if i else right[v]
            from_left = pltpu.roll(left[v], (120 - 8 * i) % 128, 1) if i < 15 else left[v]
            ext[f, rows, 128:256] = jnp.where(
                lane < 8, from_right, jnp.where(lane >= 120, from_left, 0.0)
            )

    def before(x):
        return pltpu.roll(x, 1, 1)

    def after(x):
        return pltpu.roll(x, 255, 1)

    def subcycle(step, carry):
        for t in range(18):
            r = GUARD + 8 * t
            here = pl.ds(r, 8)
            east = ext[0, here, :]
            north = ext[1, here, :]
            a = ext[0, pl.ds(r + 1, 8), :] - ext[0, pl.ds(r - 1, 8), :]
            d = ext[1, pl.ds(r + 1, 8), :] - ext[1, pl.ds(r - 1, 8), :]
            b = after(north) - before(north)
            c = after(east) - before(east)
            plus = a + b
            minus = a - b
            shear = c + d
            square = 0.25 * (plus * plus) + 0.0625 * (minus * minus + shear * shear) + 0.04
            p3 = ext[5, here, :]
            k = p3 * lax.rsqrt(square)
            ext[2, here, :] = (2.0 / 3.0) * ext[2, here, :] + (0.5 * k) * plus - p3
            ext[3, here, :] = (2.0 / 3.0) * ext[3, here, :] + (0.125 * k) * minus
            ext[4, here, :] = (2.0 / 3.0) * ext[4, here, :] + (0.0625 * k) * shear
        for t in range(18):
            r = GUARD + 8 * t
            here = pl.ds(r, 8)
            down = pl.ds(r + 1, 8)
            up = pl.ds(r - 1, 8)
            s2 = ext[4, here, :]
            differ = ext[2, here, :] - ext[3, here, :]
            force_x = (ext[2, down, :] + ext[3, down, :]) - (ext[2, up, :] + ext[3, up, :])
            force_x = force_x + 2.0 * (after(s2) - before(s2))
            force_y = after(differ) - before(differ)
            force_y = force_y + 2.0 * (ext[4, down, :] - ext[4, up, :])
            alpha = ext[6, here, :]
            beta = ext[7, here, :]
            east = ext[0, here, :]
            north = ext[1, here, :]
            ext[0, here, :] = alpha * (east + 0.15 * north) + beta * force_x + ext[8, here, :]
            ext[1, here, :] = alpha * (north - 0.15 * east) + beta * force_y + ext[9, here, :]
        return carry

    lax.fori_loop(0, SUB, subcycle, 0)
    inner = slice(GUARD + 8, GUARD + 136)
    for f in range(2):
        vel_out[f] = ext[f, inner, 0:128]
    for f in range(3):
        stress_out[f] = ext[2 + f, inner, 0:128]


def evp(vel, stress, coef, top, bottom, left, right):
    return pl.pallas_call(
        evp_kernel,
        out_shape=(
            jax.ShapeDtypeStruct((2, 128, 128), F32),
            jax.ShapeDtypeStruct((3, 128, 128), F32),
        ),
        in_specs=[VSPEC] * 7,
        out_specs=(VSPEC, VSPEC),
        scratch_shapes=[pltpu.VMEM((NF, 160, 256), F32)],
        name="evp",
    )(vel, stress, coef, top, bottom, left, right)


def exchange(axis, to_lower, to_upper):
    peers = lax.axis_size(axis)
    up = [(i, i + 1) for i in range(peers - 1)]
    down = [(i + 1, i) for i in range(peers - 1)]
    return lax.ppermute(to_upper, axis, up), lax.ppermute(to_lower, axis, down)


def swap(payload, rows):
    n = lax.axis_size("gy")
    out = lax.all_to_all(
        payload.reshape(n, CAP * rows, 128), "gy", split_axis=0, concat_axis=0, tiled=True
    )
    return out.reshape(n * CAP * rows, 128)


def local(
    conditions,
    warmth,
    share,
    floe,
    drift,
    velocity,
    stress,
    drive,
    weight,
    pressure,
    holder,
    land,
):
    own = holder.reshape(B)
    recv = swap(pack(own, land, conditions), ROWS_OUT)

    coef, first_rows, last_rows = prepare(land, velocity, stress, drive, weight, pressure)
    top, bottom = exchange("gx", first_rows, last_rows)
    to_left, to_right = edges(velocity, stress, coef, top, bottom)
    left, right = exchange("gy", to_left, to_right)

    new_warm, flux = columns(
        warmth.transpose(1, 2, 0, 3),
        share.transpose(1, 0, 2),
        floe.transpose(1, 0, 2),
        drift.transpose(1, 0, 2),
        recv,
    )
    back = swap(flux, ROWS_BACK)
    velocity_new, stress_new = evp(velocity, stress, coef, top, bottom, left, right)
    exchanges = unpack(own, land, back, conditions)
    return (new_warm.transpose(2, 0, 1, 3), exchanges, velocity_new, stress_new)


def solution(mesh):
    return jax.shard_map(
        local,
        mesh=mesh,
        in_specs=(
            P(None, "gx", "gy"),
            P(("gx", "gy"), None, None, None),
            P(("gx", "gy"), None, None),
            P(("gx", "gy"), None, None),
            P(("gx", "gy"), None, None),
            P(None, "gx", "gy"),
            P(None, "gx", "gy"),
            P(None, "gx", "gy"),
            P("gx", "gy"),
            P("gx", "gy"),
            P(("gx", "gy"), None),
            P(("gx", "gy")),
        ),
        out_specs=(
            P(("gx", "gy"), None, None, None),
            P(None, "gx", "gy"),
            P(None, "gx", "gy"),
            P(None, "gx", "gy"),
        ),
        check_vma=False,
    )
```

time: 267 us -> 76.9 us (0.29); the launches traced: 264 us -> 76.2 us
  starting transfers between devices: 105 us -> 18 us
  local copies, waits for them, and re-layouts: 56.7 us -> 2.15 us
  other arithmetic: 40.9 us -> 0 us
  waiting for transfers between devices: 48.2 us -> 8.83 us
  Pallas kernels: 0 us -> 27.3 us
  blocking collectives: 0 us -> 19.2 us
  matrix products: 11.1 us -> 0 us
    ppermute x32 -> x4, starting transfers between devices: 85.7 us -> 12.3 us  [the longest x2 8.21 us: exchange(): lax.ppermute(to_upper, axis, up)]
    ppermute x32 -> x4, waiting for transfers between devices: 48.2 us -> 8.82 us  [the longest x2 8.82 us: exchange(): lax.ppermute(to_lower, axis, down)]
    pallas_call x0 -> x6, Pallas kernels: none -> 27.3 us  [the longest x1 12.9 us: columns(): pl.pallas_call(column_kernel, grid=(4, 2), out_shape=(jax.ShapeDtypeStruc...]
    unnamed x91 -> x10, local copies, waits for them, and re-layouts: 24.1 us -> 2.15 us
    all_to_all x0 -> x1, blocking collectives: none -> 19.2 us  [swap(): lax.all_to_all(payload.reshape(n, CAP * rows, 128), 'gy', split_axis=0, c...]
    all_to_all x3 -> x1, starting transfers between devices: 19.2 us -> 5.66 us  [swap(): lax.all_to_all(payload.reshape(n, CAP * rows, 128), 'gy', split_axis=0, c...]
    another operation x11 -> x0, local copies, waits for them, and re-layouts: 12.6 us -> none  [the longest x10 11.8 us: column_step(): jnp.stack([jnp.sum(cat_area * term_value, axis=1) for term_value in flux_...]
    dot_general x2 -> x0, matrix products: 11.1 us -> none  [the longest x1 10.5 us: local(): jnp.einsum('bs,sfc->bfc', own_choose, returned, precision=lax.Precision.H...]
  transfers between devices with their start and end apart: 35 -> 5, of which waited for: 16 -> 2; matrix products, arithmetic and copies ran while one was open for 18% -> 0% of each run, Pallas kernels for 0% -> 12%
where the time goes in v1:
time: 76.9 us; the launch traced here: 76.2 us
  Pallas kernels  27.3 us (36%)
  blocking collectives  19.2 us (25%)
  starting transfers between devices  18 us (23%)
  waiting for transfers between devices  8.83 us (11%)
  local copies, waits for them, and re-layouts  2.15 us (3%)
    all_to_all x1, blocking collectives, swap(): lax.all_to_all(payload.reshape(n, CAP * rows, 128), 'gy', split_axis=0, c...  19.2 us
    pallas_call x1, Pallas kernels, columns(): pl.pallas_call(column_kernel, grid=(4, 2), out_shape=(jax.ShapeDtypeStruc...  12.9 us
    ppermute x2, waiting for transfers between devices, exchange(): lax.ppermute(to_lower, axis, down)  8.82 us
    ppermute x2, starting transfers between devices, exchange(): lax.ppermute(to_upper, axis, up)  8.21 us
    all_to_all x1, starting transfers between devices, swap(): lax.all_to_all(payload.reshape(n, CAP * rows, 128), 'gy', split_axis=0, c...  5.66 us
    pallas_call x1, Pallas kernels, evp(): pl.pallas_call(evp_kernel, out_shape=(jax.ShapeDtypeStruct((2, 128, 128),...  4.75 us
    ppermute x2, starting transfers between devices, exchange(): lax.ppermute(to_lower, axis, down)  4.1 us
    pallas_call x1, Pallas kernels, unpack(): pl.pallas_call(unpack_kernel, grid=(1,), out_shape=jax.ShapeDtypeStruct((...  2.87 us
  transfers between devices with their start and end apart: 5, of which 2 were waited for; matrix products, arithmetic and copies ran while one was open for 0% of the time, Pallas kernels for 12%

profile of v1, /device:TPU:7, one launch (start us, length us, event | category | flops | bytes accessed | tf_op | source)
XLA Modules:
  0.0 76.2 jit_solution(14661376886009360504)
XLA Ops:
  0.6 2.6 %pack.1 = f32[1536,128]{1,0:T(8,128)} custom-call(s32[16]{0:T(128)} %bitcast.18, s32[16]{0:T(128)} %land.5, f32[8,128,128]{2,1,0:T(8,128)} %visible.1), custom_call_target="tpu_custom_call" | custom-call | tf_op jit(solution)/shard_map/pack/pallas_call | solution.py:90
  3.3 19.2 %all_to_all.10 = f32[16,96,128]{2,1,0:T(8,128)} all-to-all(f32[16,96,128]{2,1,0:T(8,128)} %bitcast.13), channel_id=1, replica_groups=mesh['gx'=8,'gy'=16] {'gy'}, dimensions={0} | all-to-all | bytes 1572864 | tf_op jit(solution)/shard_map/all_to_all | solution.py:427
  22.5 12.9 %columns.1 = (f32[5,10,32,1024]{3,2,1,0:T(8,128)}, f32[1792,128]{1,0:T(8,128)}) custom-call(f32[5,10,32,1024]{3,2,1,0:T(8,128)} %bitcast.10, f32[5,32,1024]{2,1,0:T(8,128)} %bitcast.15, f32[5,32,1024]{2,1,0:T(8,128)} %bitcast.16, f32[5,32,1024]{2,1,0:T(8,128)} %bitcast.17, f32[1536,128]{1,0:T(8,128)} %bitcast.12), custom_call_target="tpu_custom_call" | custom-call | tf_op jit(solution)/shard_map/columns/pallas_call | solution.py:203
  35.4 5.7 %all-to-all-start.1 = ((f32[16,112,128]{2,1,0:T(8,128)}), f32[16,112,128]{2,1,0:T(8,128)S(1)}, u32[]{:S(2)}, u32[]{:S(2)}) async-start(f32[16,112,128]{2,1,0:T(8,128)} %bitcast.14), calls=%async_computation.1 | async-start | bytes 1835008 | tf_op jit(solution)/shard_map/all_to_all | solution.py:427
  41.1 1.9 %prepare.1 = (f32[5,128,128]{2,1,0:T(8,128)}, f32[10,8,128]{2,1,0:T(8,128)}, f32[10,8,128]{2,1,0:T(8,128)}) custom-call(s32[16]{0:T(128)} %land.5, f32[2,128,128]{2,1,0:T(8,128)} %vel.5, f32[3,128,128]{2,1,0:T(8,128)} %stress.5, f32[4,128,128]{2,1,0:T(8,128)} %drive.1, f32[128,128]{1,0:T(8,128)} %weight.1, f32[128,128]{1,0:T(8,128)} %pressure.1), custom_call_target="tpu_custom_call" | custom-call | tf_op jit(solution)/shard_map/prepare/pallas_call | solution.py:279
  43.0 5.1 %collective-permute-start = (f32[10,8,128]{2,1,0:T(8,128)}, f32[10,8,128]{2,1,0:T(8,128)S(1)}, u32[]{:S(2)}, u32[]{:S(2)}) collective-permute-start(f32[10,8,128]{2,1,0:T(8,128)} %get-tuple-element.16), channel_id=1, source_target_pairs={{0,16},{16,32},{32,48},{48,64},{64,80},{80,96},{96,112},{1,17},{17... | collective-permute-start | bytes 122888 | tf_op jit(solution)/shard_map/ppermute | solution.py:422
  48.1 1.9 %collective-permute-start.1 = (f32[10,8,128]{2,1,0:T(8,128)}, f32[10,8,128]{2,1,0:T(8,128)S(1)}, u32[]{:S(2)}, u32[]{:S(2)}) collective-permute-start(f32[10,8,128]{2,1,0:T(8,128)} %get-tuple-element.17), channel_id=1, source_target_pairs={{16,0},{32,16},{48,32},{64,48},{80,64},{96,80},{112,96},{17,1},{33... | collective-permute-start | bytes 122888 | tf_op jit(solution)/shard_map/ppermute | solution.py:422
  50.0 0.0 collective-permute-done.top
  50.1 0.0 copy-start.1
  50.1 3.9 %collective-permute-done.1.bottom = f32[10,8,128]{2,1,0:T(8,128)S(1)} collective-permute-done((f32[10,8,128]{2,1,0:T(8,128)}, f32[10,8,128]{2,1,0:T(8,128)S(1)}, u32[]{:S(2)}, u32[]{:S(2)}) %collective-permute-start.1) | collective-permute-done | bytes 40992 | tf_op jit(solution)/shard_map/ppermute | solution.py:422
  53.9 0.0 copy-start.2
  54.0 0.0 copy-done.1
  54.0 0.6 copy-done.2
  54.5 2.2 %edges.1 = (f32[12,8,128]{2,1,0:T(8,128)}, f32[12,8,128]{2,1,0:T(8,128)}) custom-call(f32[2,128,128]{2,1,0:T(8,128)} %vel.5, f32[3,128,128]{2,1,0:T(8,128)} %stress.5, f32[5,128,128]{2,1,0:T(8,128)} %get-tuple-element.15.coef, f32[10,8,128]{2,1,0:T(8,128)} %copy-done.1, f32[10,8,128]{2,1,0:T(8,128)} %copy-done.2), custom_call_target="tpu_custom_call" | custom-call | tf_op jit(solution)/shard_map/edges/pallas_call | solution.py:324
  56.8 3.1 %collective-permute-start.2 = (f32[12,8,128]{2,1,0:T(8,128)}, f32[12,8,128]{2,1,0:T(8,128)S(1)}, u32[]{:S(2)}, u32[]{:S(2)}) collective-permute-start(f32[12,8,128]{2,1,0:T(8,128)} %get-tuple-element.18), channel_id=1, source_target_pairs={{0,1},{1,2},{2,3},{3,4},{4,5},{5,6},{6,7},{7,8},{8,9},{9,10},{10,1... | collective-permute-start | bytes 147464 | tf_op jit(solution)/shard_map/ppermute | solution.py:422
  59.9 2.2 %collective-permute-start.3 = (f32[12,8,128]{2,1,0:T(8,128)}, f32[12,8,128]{2,1,0:T(8,128)S(1)}, u32[]{:S(2)}, u32[]{:S(2)}) collective-permute-start(f32[12,8,128]{2,1,0:T(8,128)} %get-tuple-element.19), channel_id=1, source_target_pairs={{1,0},{2,1},{3,2},{4,3},{5,4},{6,5},{7,6},{8,7},{9,8},{10,9},{11,1... | collective-permute-start | bytes 147464 | tf_op jit(solution)/shard_map/ppermute | solution.py:422
  62.1 0.0 collective-permute-done.2.left
  62.1 0.0 copy-start.3
  62.1 4.9 %collective-permute-done.3.right = f32[12,8,128]{2,1,0:T(8,128)S(1)} collective-permute-done((f32[12,8,128]{2,1,0:T(8,128)}, f32[12,8,128]{2,1,0:T(8,128)S(1)}, u32[]{:S(2)}, u32[]{:S(2)}) %collective-permute-start.3) | collective-permute-done | bytes 49184 | tf_op jit(solution)/shard_map/ppermute | solution.py:422
  67.0 0.0 copy-done.3
  67.0 0.0 copy-start.4
  67.0 0.6 copy-done.4
  67.6 4.7 %evp.1 = (f32[2,128,128]{2,1,0:T(8,128)}, f32[3,128,128]{2,1,0:T(8,128)}) custom-call(f32[2,128,128]{2,1,0:T(8,128)} %vel.5, f32[3,128,128]{2,1,0:T(8,128)} %stress.5, f32[5,128,128]{2,1,0:T(8,128)} %get-tuple-element.15.coef, f32[10,8,128]{2,1,0:T(8,128)} %copy-done.1, f32[10,8,128]{2,1,0:T(8,128)} %copy-done.2, f32[12,8,128]{2,1,0:T(8,128)} %copy-done.3, ...), custom_call_target="tpu_custom_call" | custom-call | tf_op jit(solution)/shard_map/evp/pallas_call | solution.py:405
  72.4 0.0 all-to-all-done.1
  72.4 0.0 copy-start
  72.4 0.9 %copy-done = f32[16,112,128]{2,1,0:T(8,128)} copy-done((f32[16,112,128]{2,1,0:T(8,128)}, f32[16,112,128]{2,1,0:T(8,128)S(1)}, u32[]{:S(2)}) %copy-start) | copy-done | bytes 917528
  73.3 2.9 %unpack.1 = f32[8,128,128]{2,1,0:T(8,128)} custom-call(s32[16]{0:T(128)} %bitcast.19, s32[16]{0:T(128)} %land.5, f32[1792,128]{1,0:T(8,128)} %bitcast.11, f32[8,128,128]{2,1,0:T(8,128)} %visible.1, f32[8,128,128]{2,1,0:T(8,128)} %visible.1), custom_call_target="tpu_custom_call" | custom-call | tf_op jit(solution)/shard_map/unpack/pallas_call | solution.py:239
Async XLA Ops:
  35.4 37.0 %all-to-all-start.1 = ((f32[16,112,128]{2,1,0:T(8,128)}), f32[16,112,128]{2,1,0:T(8,128)S(1)}, u32[]{:S(2)}, u32[]{:S(2)}) async-start(f32[16,112,128]{2,1,0:T(8,128)} %bitcast.14), calls=%async_computation.1 | async-start | bytes 1835008 | tf_op jit(solution)/shard_map/all_to_all | solution.py:427
  43.0 7.1 %collective-permute-start = (f32[10,8,128]{2,1,0:T(8,128)}, f32[10,8,128]{2,1,0:T(8,128)S(1)}, u32[]{:S(2)}, u32[]{:S(2)}) collective-permute-start(f32[10,8,128]{2,1,0:T(8,128)} %get-tuple-element.16), channel_id=1, source_target_pairs={{0,16},{16,32},{32,48},{48,64},{64,80},{80,96},{96,112},{1,17},{17... | collective-permute-start | bytes 122888 | tf_op jit(solution)/shard_map/ppermute | solution.py:422
  48.1 5.8 %collective-permute-start.1 = (f32[10,8,128]{2,1,0:T(8,128)}, f32[10,8,128]{2,1,0:T(8,128)S(1)}, u32[]{:S(2)}, u32[]{:S(2)}) collective-permute-start(f32[10,8,128]{2,1,0:T(8,128)} %get-tuple-element.17), channel_id=1, source_target_pairs={{16,0},{32,16},{48,32},{64,48},{80,64},{96,80},{112,96},{17,1},{33... | collective-permute-start | bytes 122888 | tf_op jit(solution)/shard_map/ppermute | solution.py:422
  50.1 3.9 %copy-start.1 = (f32[10,8,128]{2,1,0:T(8,128)}, f32[10,8,128]{2,1,0:T(8,128)S(1)}, u32[]{:S(2)}) copy-start(f32[10,8,128]{2,1,0:T(8,128)S(1)} %collective-permute-done.top) | copy-start | bytes 122884
  53.9 0.6 copy-start.2
  56.8 5.3 %collective-permute-start.2 = (f32[12,8,128]{2,1,0:T(8,128)}, f32[12,8,128]{2,1,0:T(8,128)S(1)}, u32[]{:S(2)}, u32[]{:S(2)}) collective-permute-start(f32[12,8,128]{2,1,0:T(8,128)} %get-tuple-element.18), channel_id=1, source_target_pairs={{0,1},{1,2},{2,3},{3,4},{4,5},{5,6},{6,7},{7,8},{8,9},{9,10},{10,1... | collective-permute-start | bytes 147464 | tf_op jit(solution)/shard_map/ppermute | solution.py:422
  59.9 7.2 %collective-permute-start.3 = (f32[12,8,128]{2,1,0:T(8,128)}, f32[12,8,128]{2,1,0:T(8,128)S(1)}, u32[]{:S(2)}, u32[]{:S(2)}) collective-permute-start(f32[12,8,128]{2,1,0:T(8,128)} %get-tuple-element.19), channel_id=1, source_target_pairs={{1,0},{2,1},{3,2},{4,3},{5,4},{6,5},{7,6},{8,7},{9,8},{10,9},{11,1... | collective-permute-start | bytes 147464 | tf_op jit(solution)/shard_map/ppermute | solution.py:422
  62.1 5.0 %copy-start.3 = (f32[12,8,128]{2,1,0:T(8,128)}, f32[12,8,128]{2,1,0:T(8,128)S(1)}, u32[]{:S(2)}) copy-start(f32[12,8,128]{2,1,0:T(8,128)S(1)} %collective-permute-done.2.left) | copy-start | bytes 147460
  67.0 0.6 copy-start.4
  72.4 0.9 %copy-start = (f32[16,112,128]{2,1,0:T(8,128)}, f32[16,112,128]{2,1,0:T(8,128)S(1)}, u32[]{:S(2)}) copy-start(f32[16,112,128]{2,1,0:T(8,128)S(1)} %all-to-all-done.1) | copy-start | bytes 2752516

commit v2 on v1

--- a/solution.py
+++ b/solution.py
@@ -21,6 +21,11 @@
 VM = pltpu.VMEM
 VSPEC = pl.BlockSpec(memory_space=pltpu.VMEM)
 SSPEC = pl.BlockSpec(memory_space=pltpu.SMEM)
+
+
+def vmem(*arrays):
+    out = [pltpu.with_memory_space_constraint(a, pltpu.VMEM) for a in arrays]
+    return out if len(out) > 1 else out[0]
 
 
 def lane_groups():
@@ -89,7 +94,7 @@
 def pack(own, land, conditions):
     return pl.pallas_call(
         pack_kernel,
-        out_shape=jax.ShapeDtypeStruct((B * CAP * ROWS_OUT, 128), F32),
+        out_shape=pltpu.VMEM((B * CAP * ROWS_OUT, 128), F32),
         in_specs=[SSPEC, SSPEC, VSPEC],
         out_specs=VSPEC,
         scratch_shapes=[pltpu.SMEM((B,), jnp.int32)],
@@ -153,6 +158,7 @@
 
 
 def column_kernel(warm, share, floe, drift, recv, new_warm, flux):
+    first = pl.program_id(0) * 8
     half = pl.program_id(1)
 
     def tile(k, carry):
@@ -160,7 +166,7 @@
         kk = half * 4 + k
 
         def field(f):
-            return recv[pl.ds(f * 8 + kk, 8, stride=ROWS_OUT), :]
+            return recv[pl.ds(first * ROWS_OUT + f * 8 + kk, 8, stride=ROWS_OUT), :]
 
         ocean, salinity, air, source_top, snowfall, top_resist = [field(f) for f in range(NSEND)]
         filled = salinity > 0.25
@@ -191,7 +197,7 @@
             0.05 * (held + top - bottom + source_top * total),
         )
         for f in range(NBACK):
-            flux[pl.ds(f * 8 + kk, 8, stride=ROWS_BACK), :] = back[f]
+            flux[pl.ds(first * ROWS_BACK + f * 8 + kk, 8, stride=ROWS_BACK), :] = back[f]
         return carry
 
     lax.fori_loop(0, 4, tile, 0)
@@ -205,12 +211,12 @@
         grid=(4, 2),
         out_shape=(
             jax.ShapeDtypeStruct((NCAT, NLAY, 32, 1024), F32),
-            jax.ShapeDtypeStruct((B * CAP * ROWS_BACK, 128), F32),
+            pltpu.VMEM((B * CAP * ROWS_BACK, 128), F32),
         ),
-        in_specs=[col, cls, cls, cls, pl.BlockSpec((8 * ROWS_OUT, 128), lambda g, h: (g, 0))],
-        out_specs=(col, pl.BlockSpec((8 * ROWS_BACK, 128), lambda g, h: (g, 0))),
+        in_specs=[col, cls, cls, cls, VSPEC],
+        out_specs=(col, VSPEC),
         name="columns",
-    )(warm, share, floe, drift, recv)
+    )(warm, share, floe, drift, vmem(recv))
 
 
 def unpack_kernel(own, land, back, salinity, visible, out, count):
@@ -243,18 +249,20 @@
         in_specs=[
             SSPEC,
             SSPEC,
-            pl.BlockSpec((B * CAP * ROWS_BACK, 128), lambda i: (0, 0)),
+            VSPEC,
             pl.BlockSpec((1, 128, 128), lambda i: (1, 0, 0)),
             pl.BlockSpec((1, 128, 128), lambda i: (3, 0, 0)),
         ],
         out_specs=pl.BlockSpec((8, 128, 128), lambda i: (0, 0, 0)),
         scratch_shapes=[pltpu.SMEM((B,), jnp.int32)],
         name="unpack",
-    )(own, land, back, conditions, conditions)
-
-
-def prepare_kernel(land, vel, stress, drive, weight, pressure, coef, up, down):
+    )(own, land, vmem(back), conditions, conditions)
+
+
+def prepare_kernel(land, vel, stress, drive, weight, pressure, fields, up, down):
     group = lax.broadcasted_iota(jnp.int32, (32, 128), 1) // 32
+    fields[0:2] = vel[...]
+    fields[2:5] = stress[...]
     for bx in range(4):
         at = pl.ds(32 * bx, 32)
         water = jnp.zeros((32, 128), F32)
@@ -263,22 +271,20 @@
         w = weight[at, :]
         scale = water / (w + 0.5)
         beta = 0.5 * scale
-        coef[0, at, :] = pressure[at, :] * (1.0 / 3.0)
-        coef[1, at, :] = scale * w
-        coef[2, at, :] = 0.25 * beta
-        coef[3, at, :] = beta * (drive[0, at, :] + drive[2, at, :])
-        coef[4, at, :] = beta * (drive[1, at, :] + drive[3, at, :])
-    for rows, dst in ((pl.ds(0, 8), up), (pl.ds(120, 8), down)):
-        dst[0:2] = vel[:, rows, :]
-        dst[2:5] = stress[:, rows, :]
-        dst[5:10] = coef[:, rows, :]
+        fields[5, at, :] = pressure[at, :] * (1.0 / 3.0)
+        fields[6, at, :] = scale * w
+        fields[7, at, :] = 0.25 * beta
+        fields[8, at, :] = beta * (drive[0, at, :] + drive[2, at, :])
+        fields[9, at, :] = beta * (drive[1, at, :] + drive[3, at, :])
+    up[...] = fields[:, 0:8, :]
+    down[...] = fields[:, 120:128, :]
 
 
 def prepare(land, vel, stress, drive, weight, pressure):
-    edge = jax.ShapeDtypeStruct((NF, 8, 128), F32)
+    edge = pltpu.VMEM((NF, 8, 128), F32)
     return pl.pallas_call(
         prepare_kernel,
-        out_shape=(jax.ShapeDtypeStruct((5, 128, 128), F32), edge, edge),
+        out_shape=(pltpu.VMEM((NF, 128, 128), F32), edge, edge),
         in_specs=[SSPEC] + [VSPEC] * 5,
         out_specs=(VSPEC, VSPEC, VSPEC),
         name="prepare",
@@ -288,20 +294,15 @@
 NPACK = 12
 
 
-def field_tile(f, t, vel, stress, coef, top, bottom):
+def field_tile(f, t, fields, top, bottom):
     if t == 0:
         return top[f]
     if t == 17:
         return bottom[f]
-    rows = slice(8 * (t - 1), 8 * t)
-    if f < 2:
-        return vel[f, rows, :]
-    if f < 5:
-        return stress[f - 2, rows, :]
-    return coef[f - 5, rows, :]
-
-
-def edges_kernel(vel, stress, coef, top, bottom, left, right):
+    return fields[f, 8 * (t - 1) : 8 * t, :]
+
+
+def edges_kernel(fields, top, bottom, left, right):
     piece = lax.broadcasted_iota(jnp.int32, (8, 128), 1) // 8
     for v in range(NPACK):
         to_left = jnp.zeros((8, 128), F32)
@@ -310,7 +311,7 @@
             n = 16 * v + i
             if n >= NF * 18:
                 break
-            x = field_tile(n // 18, n % 18, vel, stress, coef, top, bottom)
+            x = field_tile(n // 18, n % 18, fields, top, bottom)
             xl = pltpu.roll(x, 8 * i, 1) if i else x
             xr = pltpu.roll(x, (8 * i + 8) % 128, 1) if i < 15 else x
             to_left = jnp.where(piece == i, xl, to_left)
@@ -319,21 +320,21 @@
         right[v] = to_right
 
 
-def edges(vel, stress, coef, top, bottom):
-    side = jax.ShapeDtypeStruct((NPACK, 8, 128), F32)
+def edges(fields, top, bottom):
+    side = pltpu.VMEM((NPACK, 8, 128), F32)
     return pl.pallas_call(
         edges_kernel,
         out_shape=(side, side),
-        in_specs=[VSPEC] * 5,
+        in_specs=[VSPEC] * 3,
         out_specs=(VSPEC, VSPEC),
         name="edges",
-    )(vel, stress, coef, top, bottom)
+    )(*vmem(fields, top, bottom))
 
 
 GUARD = 8
 
 
-def evp_kernel(vel, stress, coef, top, bottom, left, right, vel_out, stress_out, ext):
+def evp_kernel(fields, top, bottom, left, right, vel_out, stress_out, ext):
     lane = lax.broadcasted_iota(jnp.int32, (8, 128), 1)
     for f in range(NF):
         ext[f, 0:8, :] = jnp.zeros((8, 256), F32)
@@ -342,7 +343,7 @@
             n = f * 18 + t
             v, i = divmod(n, 16)
             rows = slice(GUARD + 8 * t, GUARD + 8 * t + 8)
-            ext[f, rows, 0:128] = field_tile(f, t, vel, stress, coef, top, bottom)
+            ext[f, rows, 0:128] = field_tile(f, t, fields, top, bottom)
             from_right = pltpu.roll(right[v], (128 - 8 * i) % 128, 1) if i else right[v]
             from_left = pltpu.roll(left[v], (120 - 8 * i) % 128, 1) if i < 15 else left[v]
             ext[f, rows, 128:256] = jnp.where(
@@ -401,18 +402,18 @@
         stress_out[f] = ext[2 + f, inner, 0:128]
 
 
-def evp(vel, stress, coef, top, bottom, left, right):
+def evp(fields, top, bottom, left, right):
     return pl.pallas_call(
         evp_kernel,
         out_shape=(
             jax.ShapeDtypeStruct((2, 128, 128), F32),
             jax.ShapeDtypeStruct((3, 128, 128), F32),
         ),
-        in_specs=[VSPEC] * 7,
+        in_specs=[VSPEC] * 5,
         out_specs=(VSPEC, VSPEC),
         scratch_shapes=[pltpu.VMEM((NF, 160, 256), F32)],
         name="evp",
-    )(vel, stress, coef, top, bottom, left, right)
+    )(*vmem(fields, top, bottom, left, right))
 
 
 def exchange(axis, to_lower, to_upper):
@@ -447,11 +448,10 @@
     own = holder.reshape(B)
     recv = swap(pack(own, land, conditions), ROWS_OUT)
 
-    coef, first_rows, last_rows = prepare(land, velocity, stress, drive, weight, pressure)
+    fields, first_rows, last_rows = prepare(land, velocity, stress, drive, weight, pressure)
     top, bottom = exchange("gx", first_rows, last_rows)
-    to_left, to_right = edges(velocity, stress, coef, top, bottom)
-    left, right = exchange("gy", to_left, to_right)
-
+    to_left, to_right = edges(fields, top, bottom)
+    warmth, to_left, to_right = lax.optimization_barrier((warmth, to_left, to_right))
     new_warm, flux = columns(
         warmth.transpose(1, 2, 0, 3),
         share.transpose(1, 0, 2),
@@ -460,7 +460,8 @@
         recv,
     )
     back = swap(flux, ROWS_BACK)
-    velocity_new, stress_new = evp(velocity, stress, coef, top, bottom, left, right)
+    left, right = exchange("gy", to_left, to_right)
+    velocity_new, stress_new = evp(fields, top, bottom, left, right)
     exchanges = unpack(own, land, back, conditions)
     return (new_warm.transpose(2, 0, 1, 3), exchanges, velocity_new, stress_new)
 

time: 76.9 us -> 62.6 us (0.81)
  the two profiles are of different devices: /device:TPU:7 before, /device:TPU:32 now
where the time goes in v2:
time: 62.6 us; the launch traced here: 61.9 us
  starting transfers between devices  24.7 us (39%)
  Pallas kernels  23.1 us (37%)
  waiting for transfers between devices  13.4 us (21%)
  between operations  0.69 us (1%)
    all_to_all x2, starting transfers between devices, swap(): lax.all_to_all(payload.reshape(n, CAP * rows, 128), 'gy', split_axis=0, c...  14.2 us
    pallas_call x1, Pallas kernels, columns(): pl.pallas_call(column_kernel, grid=(4, 2), out_shape=(jax.ShapeDtypeStruc...  12.8 us
    ppermute x2, waiting for transfers between devices, exchange(): lax.ppermute(to_upper, axis, up)  5.89 us
    ppermute x2, starting transfers between devices, exchange(): lax.ppermute(to_lower, axis, down)  5.87 us
    ppermute x2, starting transfers between devices, exchange(): lax.ppermute(to_upper, axis, up)  4.66 us
    all_to_all x2, waiting for transfers between devices, swap(): lax.all_to_all(payload.reshape(n, CAP * rows, 128), 'gy', split_axis=0, c...  3.88 us
    ppermute x2, waiting for transfers between devices, exchange(): lax.ppermute(to_lower, axis, down)  3.62 us
    pallas_call x1, Pallas kernels, evp(): pl.pallas_call(evp_kernel, out_shape=(jax.ShapeDtypeStruct((2, 128, 128),...  3.51 us
  transfers between devices with their start and end apart: 6, of which 3 were waited for; matrix products, arithmetic and copies ran while one was open for 0% of the time, Pallas kernels for 8%

profile of v2, /device:TPU:32, one launch (start us, length us, event | category | flops | bytes accessed | tf_op | source)
XLA Modules:
  0.0 61.9 jit_solution(12720760770667941307)
XLA Ops:
  0.6 2.6 %pack.1 = f32[1536,128]{1,0:T(8,128)} custom-call(s32[16]{0:T(128)} %bitcast.16, s32[16]{0:T(128)} %land.5, f32[8,128,128]{2,1,0:T(8,128)} %visible.1), custom_call_target="tpu_custom_call" | custom-call | tf_op jit(solution)/shard_map/pack/pallas_call | solution.py:95
  3.3 7.9 %all-to-all-start = ((f32[16,96,128]{2,1,0:T(8,128)}), f32[16,96,128]{2,1,0:T(8,128)S(1)}, u32[]{:S(2)}, u32[]{:S(2)}) async-start(f32[16,96,128]{2,1,0:T(8,128)} %bitcast.5), calls=%async_computation | async-start | bytes 1572864 | tf_op jit(solution)/shard_map/all_to_all | solution.py:428
  11.2 1.2 %prepare.1 = (f32[10,128,128]{2,1,0:T(8,128)S(1)}, f32[10,8,128]{2,1,0:T(8,128)S(1)}, f32[10,8,128]{2,1,0:T(8,128)S(1)}) custom-call(s32[16]{0:T(128)} %land.5, f32[2,128,128]{2,1,0:T(8,128)} %vel.1, f32[3,128,128]{2,1,0:T(8,128)} %stress.1, f32[4,128,128]{2,1,0:T(8,128)} %drive.1, f32[128,128]{1,0:T(8,128)} %weight.1, f32[128,128]{1,0:T(8,128)} %pressure.1), custom_call_target="tpu_custom_call" | custom-call | tf_op jit(solution)/shard_map/prepare/pallas_call | solution.py:285
  12.4 1.3 %collective-permute-start = (f32[10,8,128]{2,1,0:T(8,128)S(1)}, f32[10,8,128]{2,1,0:T(8,128)S(1)}, u32[]{:S(2)}, u32[]{:S(2)}) collective-permute-start(f32[10,8,128]{2,1,0:T(8,128)S(1)} %get-tuple-element.17), channel_id=1, source_target_pairs={{0,16},{16,32},{32,48},{48,64},{64,80},{80,96},{96,112},{1,17},{17... | collective-permute-start | bytes 122888 | tf_op jit(solution)/shard_map/ppermute | solution.py:423
  13.7 1.3 %collective-permute-start.1 = (f32[10,8,128]{2,1,0:T(8,128)S(1)}, f32[10,8,128]{2,1,0:T(8,128)S(1)}, u32[]{:S(2)}, u32[]{:S(2)}) collective-permute-start(f32[10,8,128]{2,1,0:T(8,128)S(1)} %get-tuple-element.18), channel_id=1, source_target_pairs={{16,0},{32,16},{48,32},{64,48},{80,64},{96,80},{112,96},{17,1},{33... | collective-permute-start | bytes 122888 | tf_op jit(solution)/shard_map/ppermute | solution.py:423
  15.0 0.0 collective-permute-done.top
  15.0 3.6 %collective-permute-done.1.bottom = f32[10,8,128]{2,1,0:T(8,128)S(1)} collective-permute-done((f32[10,8,128]{2,1,0:T(8,128)S(1)}, f32[10,8,128]{2,1,0:T(8,128)S(1)}, u32[]{:S(2)}, u32[]{:S(2)}) %collective-permute-start.1) | collective-permute-done | bytes 40992 | tf_op jit(solution)/shard_map/ppermute | solution.py:423
  18.6 0.4 edges.1
  19.1 3.9 %all-to-all-done = f32[16,96,128]{2,1,0:T(8,128)S(1)} async-done(((f32[16,96,128]{2,1,0:T(8,128)}), f32[16,96,128]{2,1,0:T(8,128)S(1)}, u32[]{:S(2)}, u32[]{:S(2)}) %all-to-all-start) | async-done | bytes 786464 | tf_op jit(solution)/shard_map/all_to_all | solution.py:428
  22.9 12.8 %columns.1 = (f32[5,10,32,1024]{3,2,1,0:T(8,128)}, f32[1792,128]{1,0:T(8,128)}) custom-call(f32[5,10,32,1024]{3,2,1,0:T(8,128)} %bitcast.12, f32[5,32,1024]{2,1,0:T(8,128)} %bitcast.13, f32[5,32,1024]{2,1,0:T(8,128)} %bitcast.14, f32[5,32,1024]{2,1,0:T(8,128)} %bitcast.15, f32[1536,128]{1,0:T(8,128)S(1)} %bitcast.11), custom_call_target="tpu_custom_call" | custom-call | tf_op jit(solution)/shard_map/columns/pallas_call | solution.py:209
  35.8 6.3 %all-to-all-start.1 = ((f32[16,112,128]{2,1,0:T(8,128)}), f32[16,112,128]{2,1,0:T(8,128)S(1)}, u32[]{:S(2)}, u32[]{:S(2)}) async-start(f32[16,112,128]{2,1,0:T(8,128)} %bitcast.8), calls=%async_computation.1 | async-start | bytes 1835008 | tf_op jit(solution)/shard_map/all_to_all | solution.py:428
  42.1 3.4 %collective-permute-start.2 = (f32[12,8,128]{2,1,0:T(8,128)S(1)}, f32[12,8,128]{2,1,0:T(8,128)S(1)}, u32[]{:S(2)}, u32[]{:S(2)}) collective-permute-start(f32[12,8,128]{2,1,0:T(8,128)S(1)} %get-tuple-element.24), channel_id=1, source_target_pairs={{0,1},{1,2},{2,3},{3,4},{4,5},{5,6},{6,7},{7,8},{8,9},{9,10},{10,1... | collective-permute-start | bytes 147464 | tf_op jit(solution)/shard_map/ppermute | solution.py:423
  45.4 4.6 %collective-permute-start.3 = (f32[12,8,128]{2,1,0:T(8,128)S(1)}, f32[12,8,128]{2,1,0:T(8,128)S(1)}, u32[]{:S(2)}, u32[]{:S(2)}) collective-permute-start(f32[12,8,128]{2,1,0:T(8,128)S(1)} %get-tuple-element.25), channel_id=1, source_target_pairs={{1,0},{2,1},{3,2},{4,3},{5,4},{6,5},{7,6},{8,7},{9,8},{10,9},{11,1... | collective-permute-start | bytes 147464 | tf_op jit(solution)/shard_map/ppermute | solution.py:423
  50.0 5.9 %collective-permute-done.2.left = f32[12,8,128]{2,1,0:T(8,128)S(1)} collective-permute-done((f32[12,8,128]{2,1,0:T(8,128)S(1)}, f32[12,8,128]{2,1,0:T(8,128)S(1)}, u32[]{:S(2)}, u32[]{:S(2)}) %collective-permute-start.2) | collective-permute-done | bytes 49184 | tf_op jit(solution)/shard_map/ppermute | solution.py:423
  55.9 0.0 collective-permute-done.3.right
  55.9 3.5 %evp.1 = (f32[2,128,128]{2,1,0:T(8,128)}, f32[3,128,128]{2,1,0:T(8,128)}) custom-call(f32[10,128,128]{2,1,0:T(8,128)S(1)} %get-tuple-element.16.fields, f32[10,8,128]{2,1,0:T(8,128)S(1)} %collective-permute-done.top, f32[10,8,128]{2,1,0:T(8,128)S(1)} %collective-permute-done.1.bottom, f32[12,8,128]{2,1,0:T(8,128)S(1)} %collective-permute-done.2.left, ...), custom_call_target="tpu_custom_call" | custom-call | tf_op jit(solution)/shard_map/evp/pallas_call | solution.py:406
  59.4 0.0 all-to-all-done.1
  59.4 2.5 %unpack.1 = f32[8,128,128]{2,1,0:T(8,128)} custom-call(s32[16]{0:T(128)} %bitcast.17, s32[16]{0:T(128)} %land.5, f32[1792,128]{1,0:T(8,128)S(1)} %bitcast.10, f32[8,128,128]{2,1,0:T(8,128)} %visible.1, f32[8,128,128]{2,1,0:T(8,128)} %visible.1), custom_call_target="tpu_custom_call" | custom-call | tf_op jit(solution)/shard_map/unpack/pallas_call | solution.py:245
Async XLA Ops:
  3.3 19.7 %all-to-all-start = ((f32[16,96,128]{2,1,0:T(8,128)}), f32[16,96,128]{2,1,0:T(8,128)S(1)}, u32[]{:S(2)}, u32[]{:S(2)}) async-start(f32[16,96,128]{2,1,0:T(8,128)} %bitcast.5), calls=%async_computation | async-start | bytes 1572864 | tf_op jit(solution)/shard_map/all_to_all | solution.py:428
  12.4 2.6 %collective-permute-start = (f32[10,8,128]{2,1,0:T(8,128)S(1)}, f32[10,8,128]{2,1,0:T(8,128)S(1)}, u32[]{:S(2)}, u32[]{:S(2)}) collective-permute-start(f32[10,8,128]{2,1,0:T(8,128)S(1)} %get-tuple-element.17), channel_id=1, source_target_pairs={{0,16},{16,32},{32,48},{48,64},{64,80},{80,96},{96,112},{1,17},{17... | collective-permute-start | bytes 122888 | tf_op jit(solution)/shard_map/ppermute | solution.py:423
  13.7 4.9 %collective-permute-start.1 = (f32[10,8,128]{2,1,0:T(8,128)S(1)}, f32[10,8,128]{2,1,0:T(8,128)S(1)}, u32[]{:S(2)}, u32[]{:S(2)}) collective-permute-start(f32[10,8,128]{2,1,0:T(8,128)S(1)} %get-tuple-element.18), channel_id=1, source_target_pairs={{16,0},{32,16},{48,32},{64,48},{80,64},{96,80},{112,96},{17,1},{33... | collective-permute-start | bytes 122888 | tf_op jit(solution)/shard_map/ppermute | solution.py:423
  35.8 23.7 %all-to-all-start.1 = ((f32[16,112,128]{2,1,0:T(8,128)}), f32[16,112,128]{2,1,0:T(8,128)S(1)}, u32[]{:S(2)}, u32[]{:S(2)}) async-start(f32[16,112,128]{2,1,0:T(8,128)} %bitcast.8), calls=%async_computation.1 | async-start | bytes 1835008 | tf_op jit(solution)/shard_map/all_to_all | solution.py:428
  42.1 13.8 %collective-permute-start.2 = (f32[12,8,128]{2,1,0:T(8,128)S(1)}, f32[12,8,128]{2,1,0:T(8,128)S(1)}, u32[]{:S(2)}, u32[]{:S(2)}) collective-permute-start(f32[12,8,128]{2,1,0:T(8,128)S(1)} %get-tuple-element.24), channel_id=1, source_target_pairs={{0,1},{1,2},{2,3},{3,4},{4,5},{5,6},{6,7},{7,8},{8,9},{9,10},{10,1... | collective-permute-start | bytes 147464 | tf_op jit(solution)/shard_map/ppermute | solution.py:423
  45.4 10.5 %collective-permute-start.3 = (f32[12,8,128]{2,1,0:T(8,128)S(1)}, f32[12,8,128]{2,1,0:T(8,128)S(1)}, u32[]{:S(2)}, u32[]{:S(2)}) collective-permute-start(f32[12,8,128]{2,1,0:T(8,128)S(1)} %get-tuple-element.25), channel_id=1, source_target_pairs={{1,0},{2,1},{3,2},{4,3},{5,4},{6,5},{7,6},{8,7},{9,8},{10,9},{11,1... | collective-permute-start | bytes 147464 | tf_op jit(solution)/shard_map/ppermute | solution.py:423

commit v3 on v2

v3 whole, which is shorter than its diff:
```python
import jax
import jax.numpy as jnp
from jax import lax
from jax.experimental import pallas as pl
from jax.experimental.pallas import tpu as pltpu
from jax.sharding import PartitionSpec as P


B = 16
CAP = 2
NSEND = 6
NBACK = 7
NF = 10
SUB = 4
NCAT = 5
NLAY = 10
NSNOW = 3
ROWS_OUT = NSEND * 8
ROWS_BACK = NBACK * 8

F32 = jnp.float32
LOG2E = 1.4426950408889634
VSPEC = pl.BlockSpec(memory_space=pltpu.VMEM)
SSPEC = pl.BlockSpec(memory_space=pltpu.SMEM)


def vmem(*arrays):
    out = [pltpu.with_memory_space_constraint(a, pltpu.VMEM) for a in arrays]
    return out if len(out) > 1 else out[0]


def lane_groups():
    return lax.broadcasted_iota(jnp.int32, (8, 128), 1) // 32


def swap_groups(rows, group):
    low = group < 2
    even = (group & 1) == 0
    v0, v1, v2, v3 = rows

    def roll(x, s):
        return pltpu.roll(x, s, 1)

    a0 = jnp.where(low, v0, roll(v2, 64))
    a2 = jnp.where(low, roll(v0, 64), v2)
    a1 = jnp.where(low, v1, roll(v3, 64))
    a3 = jnp.where(low, roll(v1, 64), v3)
    return (
        jnp.where(even, a0, roll(a1, 32)),
        jnp.where(even, roll(a0, 96), a1),
        jnp.where(even, a2, roll(a3, 32)),
        jnp.where(even, roll(a2, 96), a3),
    )


def block_slots(own, land, count, blocks):
    slots = []
    for b in blocks:
        o = own[b]
        r = count[o]
        slots.append(jnp.minimum(o * CAP + r, B * CAP - 1))
        count[o] = r + 1 - land[b]
    return slots


def start_count(count):
    for o in range(B):
        count[o] = 0


def pack_kernel(own, land, x, out, kept, count):
    out[...] = jnp.zeros_like(out)
    kept[0] = 0.7 * x[3]
    kept[1] = -0.05 * x[1]
    start_count(count)
    slots = block_slots(own, land, count, range(B))
    group = lane_groups()
    for bx in range(4):

        def rows(f):
            return [x[f, pl.ds(32 * bx + q, 8, stride=4), :] for q in range(4)]

        visible, near_red, longwave = rows(3), rows(4), rows(5)
        fields = [
            rows(0),
            rows(1),
            rows(2),
            [0.25 * a + 0.45 * b + 0.3 * c for a, b, c in zip(visible, near_red, longwave)],
            rows(6),
            [1.0 / (1.0 + 2.0 * w) for w in rows(7)],
        ]
        blocks = [swap_groups(r, group) for r in fields]
        for by in range(4):
            b = 4 * bx + by

            @pl.when(land[b] == 0)
            def _():
                for f in range(NSEND):
                    out[pl.ds(pl.multiple_of(slots[b] * ROWS_OUT + f * 8, 8), 8), :] = blocks[f][by]


def pack(own, land, conditions):
    return pl.pallas_call(
        pack_kernel,
        out_shape=(pltpu.VMEM((B * CAP * ROWS_OUT, 128), F32), pltpu.VMEM((2, 128, 128), F32)),
        in_specs=[SSPEC, SSPEC, VSPEC],
        out_specs=(VSPEC, VSPEC),
        scratch_shapes=[pltpu.SMEM((B,), jnp.int32)],
        name="pack",
    )(own, land, conditions)


def one_column(temps, share, floe, snow_depth, forcing, sig):
    ocean, air, source_top, top_resist = forcing
    h14 = floe * (1.0 / 14.0)
    h27 = floe * (2.0 / 7.0)
    h47 = floe * (4.0 / 7.0)
    m_snow = snow_depth * (2.0 / 3.0)
    half_snow = snow_depth * (0.5 / 0.9)
    g_snow = 0.9 / snow_depth
    g_top = 1.0 / (half_snow + top_resist)
    inv_cond = []
    mass = [m_snow] * NSNOW
    for j in range(NLAY - NSNOW):
        t = temps[NSNOW + j]
        inv_cond.append(1.0 / (2.0 + sig[j] / (t - 0.5)))
        mass.append(h27 + h47 * (sig[j] / (t * t + 0.1)))
    cond = [g_snow, g_snow, 1.0 / (half_snow + h14 * inv_cond[0])]
    for j in range(NLAY - NSNOW - 1):
        cond.append(1.0 / (h14 * (inv_cond[j] + inv_cond[j + 1])))
    g_bot = 1.0 / (h14 * inv_cond[-1])
    ratios = []
    values = []
    u = mass[0] + g_top
    held = mass[0] * temps[0]
    y = held + g_top * air + source_top
    for l in range(NLAY):
        below = cond[l] if l < NLAY - 1 else g_bot
        pivot = 1.0 / (u + below)
        ratio = below * pivot
        if l < NLAY - 1:
            ratios.append(ratio)
            values.append(y * pivot)
            u = mass[l + 1] + ratio * u
            mt = mass[l + 1] * temps[l + 1]
            held = held + mt
            y = mt + ratio * y
        else:
            last = y * pivot + ratio * ocean
    solved = [last]
    for l in range(NLAY - 2, -1, -1):
        solved.insert(0, values[l] + ratios[l] * solved[0])
    bottom = share * (g_bot * (last - ocean))
    top = share * (g_top * (air - solved[0]))
    light = share * jnp.exp2((-5.0 * LOG2E) * snow_depth - (1.5 * LOG2E) * floe)
    return solved, (
        bottom,
        top,
        light,
        share * solved[0],
        share * snow_depth,
        share * floe,
        share * held,
        share,
    )


def column_kernel(warm, share, floe, drift, recv, new_warm, flux):
    first = pl.program_id(0) * 8
    half = pl.program_id(1)

    def tile(k, carry):
        lanes = pl.ds(pl.multiple_of(k * 128, 128), 128)
        kk = half * 4 + k

        def field(f):
            return recv[pl.ds(first * ROWS_OUT + f * 8 + kk, 8, stride=ROWS_OUT), :]

        ocean, salinity, air, source_top, snowfall, top_resist = [field(f) for f in range(NSEND)]
        filled = salinity > 0.25
        sig = [salinity * (0.02 + 0.01 * j) for j in range(NLAY - NSNOW)]
        snow_add = 0.3 * snowfall
        sums = None
        for c in range(NCAT):
            temps = [warm[c, l, :, lanes] for l in range(NLAY)]
            solved, terms = one_column(
                temps,
                share[c, :, lanes],
                floe[c, :, lanes],
                drift[c, :, lanes] + snow_add,
                (ocean, air, source_top, top_resist),
                sig,
            )
            for l in range(NLAY):
                new_warm[c, l, :, lanes] = jnp.where(filled, solved[l], temps[l])
            sums = terms if sums is None else tuple(a + b for a, b in zip(sums, terms))
        bottom, top, light, surface, snow, thick, held, total = sums
        back = (
            bottom,
            top,
            light,
            surface,
            snow,
            thick - 0.05 * bottom,
            0.05 * (held + top - bottom + source_top * total),
        )
        for f in range(NBACK):
            flux[pl.ds(f * 8 + kk, 8, stride=ROWS_BACK), :] = back[f]
        return carry

    lax.fori_loop(0, 4, tile, 0, unroll=True)


def columns(warm, share, floe, drift, recv):
    cls = pl.BlockSpec((NCAT, 8, 512), lambda g, h: (0, g, h))
    col = pl.BlockSpec((NCAT, NLAY, 8, 512), lambda g, h: (0, 0, g, h))
    return pl.pallas_call(
        column_kernel,
        grid=(4, 2),
        out_shape=(
            jax.ShapeDtypeStruct((NCAT, NLAY, 32, 1024), F32),
            jax.ShapeDtypeStruct((B * CAP * ROWS_BACK, 128), F32),
        ),
        in_specs=[col, cls, cls, cls, VSPEC],
        out_specs=(col, pl.BlockSpec((8 * ROWS_BACK, 128), lambda g, h: (g, 0))),
        name="columns",
    )(warm, share, floe, drift, vmem(recv))


def unpack_kernel(own, land, back, kept, out, tile, count, sems):
    start_count(count)
    slots = block_slots(own, land, count, range(B))
    group = lane_groups()
    copies = []
    for bx in range(4):
        rows = []
        for f in range(NBACK):
            blocks = []
            for b in range(4 * bx, 4 * bx + 4):
                v = back[pl.ds(pl.multiple_of(slots[b] * ROWS_BACK + f * 8, 8), 8), :]
                blocks.append(jnp.where(land[b] == 0, v, 0.0))
            rows.append(swap_groups(blocks, group))
        for q in range(4):
            at = pl.ds(32 * bx + q, 8, stride=4)
            for f in range(NBACK):
                v = rows[f][q]
                tile[f, at, :] = kept[0, at, :] * v if f == 2 else v
            tile[7, at, :] = kept[1, at, :] * rows[0][q]
        part = pl.ds(32 * bx, 32)
        copies.append(pltpu.make_async_copy(tile.at[:, part, :], out.at[:, part, :], sems.at[bx]))
        copies[-1].start()
    for copy in copies:
        copy.wait()


def unpack(own, land, back, kept):
    return pl.pallas_call(
        unpack_kernel,
        out_shape=jax.ShapeDtypeStruct((8, 128, 128), F32),
        in_specs=[SSPEC, SSPEC, VSPEC, VSPEC],
        out_specs=pl.BlockSpec(memory_space=pl.ANY),
        scratch_shapes=[
            pltpu.VMEM((8, 128, 128), F32),
            pltpu.SMEM((B,), jnp.int32),
            pltpu.SemaphoreType.DMA((4,)),
        ],
        name="unpack",
    )(own, land, *vmem(back, kept))


def prepare_kernel(land, vel, stress, drive, weight, pressure, fields, left, right):
    group = lax.broadcasted_iota(jnp.int32, (32, 128), 1) // 32
    fields[0:2] = vel[...]
    fields[2:5] = stress[...]
    for bx in range(4):
        at = pl.ds(32 * bx, 32)
        water = jnp.zeros((32, 128), F32)
        for by in range(4):
            water = jnp.where(group == by, (1 - land[4 * bx + by]).astype(F32), water)
        w = weight[at, :]
        scale = water / (w + 0.5)
        beta = 0.5 * scale
        fields[5, at, :] = pressure[at, :] * (1.0 / 3.0)
        fields[6, at, :] = scale * w
        fields[7, at, :] = 0.25 * beta
        fields[8, at, :] = beta * (drive[0, at, :] + drive[2, at, :])
        fields[9, at, :] = beta * (drive[1, at, :] + drive[3, at, :])
    piece = lax.broadcasted_iota(jnp.int32, (8, 128), 1) // 8
    for f in range(NF):
        to_left = jnp.zeros((8, 128), F32)
        to_right = jnp.zeros((8, 128), F32)
        for t in range(16):
            x = fields[f, 8 * t : 8 * t + 8, :]
            to_left = jnp.where(piece == t, turn(x, 8 * t), to_left)
            to_right = jnp.where(piece == t, turn(x, 8 * t + 8), to_right)
        left[f] = to_left
        right[f] = to_right


def turn(x, shift):
    shift = shift % 128
    return pltpu.roll(x, shift, 1) if shift else x


def prepare(land, vel, stress, drive, weight, pressure):
    edge = pltpu.VMEM((NF, 8, 128), F32)
    return pl.pallas_call(
        prepare_kernel,
        out_shape=(pltpu.VMEM((NF, 128, 128), F32), edge, edge),
        in_specs=[SSPEC] + [VSPEC] * 5,
        out_specs=(VSPEC, VSPEC, VSPEC),
        name="prepare",
    )(land, vel, stress, drive, weight, pressure)


def rows_kernel(fields, left, right, up, down):
    piece = lax.broadcasted_iota(jnp.int32, (8, 128), 1) // 8
    for dst, first, t in ((up, 0, 0), (down, 120, 15)):
        dst[0:NF] = fields[:, first : first + 8, :]
        for i, side in enumerate((left, right)):
            corner = jnp.zeros((8, 128), F32)
            for f in range(NF):
                corner = jnp.where(piece == f, turn(side[f], 8 * (f - t)), corner)
            dst[NF + i] = corner


def edge_rows(fields, left, right):
    edge = pltpu.VMEM((NF + 2, 8, 128), F32)
    return pl.pallas_call(
        rows_kernel,
        out_shape=(edge, edge),
        in_specs=[VSPEC] * 3,
        out_specs=(VSPEC, VSPEC),
        name="rows",
    )(*vmem(fields, left, right))


GUARD = 8


def evp_kernel(fields, left, right, top, bottom, vel_out, stress_out, ext):
    lane = lax.broadcasted_iota(jnp.int32, (8, 128), 1)
    zero = jnp.zeros((8, 128), F32)

    def beside(from_right, from_left):
        return jnp.where(lane < 8, from_right, jnp.where(lane >= 120, from_left, 0.0))

    for f in range(NF):
        for h in range(2):
            ext[f, h, 0:8, :] = zero
            ext[f, h, 152:160, :] = zero
        for edge, r in ((top, 8), (bottom, 144)):
            ext[f, 0, r : r + 8, :] = edge[f]
            ext[f, 1, r : r + 8, :] = beside(
                turn(edge[NF + 1], -8 * f), turn(edge[NF], 120 - 8 * f)
            )
        ext[f, 0, 16:144, :] = fields[f]
        for t in range(16):
            r = 16 + 8 * t
            ext[f, 1, r : r + 8, :] = beside(
                turn(right[f], -8 * t), turn(left[f], 120 - 8 * t)
            )

    def across(x):
        n0, n1 = turn(x[0], 127), turn(x[1], 127)
        p0, p1 = turn(x[0], 1), turn(x[1], 1)
        last = lane == 127
        first = lane == 0
        return (
            jnp.where(last, n1, n0) - jnp.where(first, p1, p0),
            jnp.where(last, n0, n1) - jnp.where(first, p0, p1),
        )

    def subcycle(step, carry):
        for t in range(18):
            r = GUARD + 8 * t
            here, down, up = pl.ds(r, 8), pl.ds(r + 1, 8), pl.ds(r - 1, 8)
            b = across([ext[1, h, here, :] for h in range(2)])
            c = across([ext[0, h, here, :] for h in range(2)])
            for h in range(2):
                a = ext[0, h, down, :] - ext[0, h, up, :]
                d = ext[1, h, down, :] - ext[1, h, up, :]
                plus = a + b[h]
                minus = a - b[h]
                shear = c[h] + d
                square = 0.25 * (plus * plus) + 0.0625 * (minus * minus + shear * shear) + 0.04
                p3 = ext[5, h, here, :]
                k = p3 * lax.rsqrt(square)
                ext[2, h, here, :] = (2.0 / 3.0) * ext[2, h, here, :] + (0.5 * k) * plus - p3
                ext[3, h, here, :] = (2.0 / 3.0) * ext[3, h, here, :] + (0.125 * k) * minus
                ext[4, h, here, :] = (2.0 / 3.0) * ext[4, h, here, :] + (0.0625 * k) * shear
        for t in range(18):
            r = GUARD + 8 * t
            here, down, up = pl.ds(r, 8), pl.ds(r + 1, 8), pl.ds(r - 1, 8)
            shear = across([ext[4, h, here, :] for h in range(2)])
            differ = across([ext[2, h, here, :] - ext[3, h, here, :] for h in range(2)])
            for h in range(2):
                force_x = (ext[2, h, down, :] + ext[3, h, down, :]) - (
                    ext[2, h, up, :] + ext[3, h, up, :]
                )
                force_x = force_x + 2.0 * shear[h]
                force_y = differ[h] + 2.0 * (ext[4, h, down, :] - ext[4, h, up, :])
                alpha = ext[6, h, here, :]
                beta = ext[7, h, here, :]
                east = ext[0, h, here, :]
                north = ext[1, h, here, :]
                ext[0, h, here, :] = (
                    alpha * (east + 0.15 * north) + beta * force_x + ext[8, h, here, :]
                )
                ext[1, h, here, :] = (
                    alpha * (north - 0.15 * east) + beta * force_y + ext[9, h, here, :]
                )
        return carry

    lax.fori_loop(0, SUB, subcycle, 0)
    for f in range(2):
        vel_out[f] = ext[f, 0, 16:144, :]
    for f in range(3):
        stress_out[f] = ext[2 + f, 0, 16:144, :]


def evp(fields, left, right, top, bottom):
    return pl.pallas_call(
        evp_kernel,
        out_shape=(
            jax.ShapeDtypeStruct((2, 128, 128), F32),
            jax.ShapeDtypeStruct((3, 128, 128), F32),
        ),
        in_specs=[VSPEC] * 5,
        out_specs=(VSPEC, VSPEC),
        scratch_shapes=[pltpu.VMEM((NF, 2, 160, 128), F32)],
        name="evp",
    )(*vmem(fields, left, right, top, bottom))


def exchange(axis, to_lower, to_upper):
    peers = lax.axis_size(axis)
    up = [(i, i + 1) for i in range(peers - 1)]
    down = [(i + 1, i) for i in range(peers - 1)]
    from_lower = lax.ppermute(to_upper, axis, up)
    from_upper = lax.ppermute(to_lower, axis, down)
    return from_lower, from_upper


def swap(payload, rows):
    n = lax.axis_size("gy")
    out = lax.all_to_all(
        payload.reshape(n, CAP * rows, 128), "gy", split_axis=0, concat_axis=0, tiled=True
    )
    return out.reshape(n * CAP * rows, 128)


def step(
    conditions,
    warmth,
    share,
    floe,
    drift,
    velocity,
    stress,
    drive,
    weight,
    pressure,
    holder,
    land,
):
    own = holder.reshape(B)
    payload, kept = pack(own, land, conditions)
    recv = swap(payload, ROWS_OUT)

    fields, to_left, to_right = prepare(land, velocity, stress, drive, weight, pressure)
    left, right = exchange("gy", to_left, to_right)

    new_warm, flux = columns(
        warmth.transpose(1, 2, 0, 3),
        share.transpose(1, 0, 2),
        floe.transpose(1, 0, 2),
        drift.transpose(1, 0, 2),
        recv,
    )
    back = swap(flux, ROWS_BACK)
    first_rows, last_rows = edge_rows(fields, left, right)
    top, bottom = exchange("gx", first_rows, last_rows)
    velocity_new, stress_new = evp(fields, left, right, top, bottom)
    exchanges = unpack(own, land, back, kept)
    return (new_warm.transpose(2, 0, 1, 3), exchanges, velocity_new, stress_new)


def solution(mesh):
    return jax.shard_map(
        step,
        mesh=mesh,
        in_specs=(
            P(None, "gx", "gy"),
            P(("gx", "gy"), None, None, None),
            P(("gx", "gy"), None, None),
            P(("gx", "gy"), None, None),
            P(("gx", "gy"), None, None),
            P(None, "gx", "gy"),
            P(None, "gx", "gy"),
            P(None, "gx", "gy"),
            P("gx", "gy"),
            P("gx", "gy"),
            P(("gx", "gy"), None),
            P(("gx", "gy")),
        ),
        out_specs=(
            P(("gx", "gy"), None, None, None),
            P(None, "gx", "gy"),
            P(None, "gx", "gy"),
            P(None, "gx", "gy"),
        ),
        check_vma=False,
    )
```

time: 62.6 us -> 67.8 us (1.083)
  the two profiles are of different devices: /device:TPU:32 before, /device:TPU:7 now
where the time goes in v3:
time: 67.8 us; the launch traced here: 67.2 us
  Pallas kernels  20 us (29%)
  blocking collectives  18.9 us (28%)
  starting transfers between devices  18.2 us (27%)
  waiting for transfers between devices  9.4 us (14%)
  between operations  0.7 us (1%)
    all_to_all x1, blocking collectives, swap(): lax.all_to_all(payload.reshape(n, CAP * rows, 128), 'gy', split_axis=0, c...  18.9 us
    pallas_call x1, Pallas kernels, columns(): pl.pallas_call(column_kernel, grid=(4, 2), out_shape=(jax.ShapeDtypeStruc...  11.6 us
    ppermute x2, starting transfers between devices, exchange(): from_lower = lax.ppermute(to_upper, axis, up)  8.41 us
    all_to_all x1, starting transfers between devices, swap(): lax.all_to_all(payload.reshape(n, CAP * rows, 128), 'gy', split_axis=0, c...  5.65 us
    ppermute x2, waiting for transfers between devices, exchange(): from_upper = lax.ppermute(to_lower, axis, down)  5.65 us
    ppermute x2, starting transfers between devices, exchange(): from_upper = lax.ppermute(to_lower, axis, down)  4.11 us
    ppermute x2, waiting for transfers between devices, exchange(): from_lower = lax.ppermute(to_upper, axis, up)  3.74 us
    pallas_call x1, Pallas kernels, evp(): pl.pallas_call(evp_kernel, out_shape=(jax.ShapeDtypeStruct((2, 128, 128),...  2.77 us
  transfers between devices with their start and end apart: 5, of which 3 were waited for; matrix products, arithmetic and copies ran while one was open for 0% of the time, Pallas kernels for 7%

profile of v3, /device:TPU:7, one launch (start us, length us, event | category | flops | bytes accessed | tf_op | source)
XLA Modules:
  0.0 67.2 jit_solution(14333315472819729178)
XLA Ops:
  0.6 1.8 %pack.1 = (f32[1536,128]{1,0:T(8,128)S(1)}, f32[2,128,128]{2,1,0:T(8,128)S(1)}) custom-call(s32[16]{0:T(128)} %bitcast.18, s32[16]{0:T(128)} %land.5, f32[8,128,128]{2,1,0:T(8,128)} %x.1), custom_call_target="tpu_custom_call" | custom-call | tf_op jit(solution)/shard_map/pack/pallas_call | solution.py:103
  2.4 18.9 %all_to_all.10 = f32[16,96,128]{2,1,0:T(8,128)S(1)} all-to-all(f32[16,96,128]{2,1,0:T(8,128)S(1)} %bitcast.12), channel_id=1, replica_groups=mesh['gx'=8,'gy'=16] {'gy'}, dimensions={0} | all-to-all | bytes 1572864 | tf_op jit(solution)/shard_map/all_to_all | solution.py:447
  21.3 11.6 %columns.1 = (f32[5,10,32,1024]{3,2,1,0:T(8,128)}, f32[1792,128]{1,0:T(8,128)}) custom-call(f32[5,10,32,1024]{3,2,1,0:T(8,128)} %bitcast.13, f32[5,32,1024]{2,1,0:T(8,128)} %bitcast.15, f32[5,32,1024]{2,1,0:T(8,128)} %bitcast.16, f32[5,32,1024]{2,1,0:T(8,128)} %bitcast.17, f32[1536,128]{1,0:T(8,128)S(1)} %bitcast.11), custom_call_target="tpu_custom_call" | custom-call | tf_op jit(solution)/shard_map/columns/pallas_call | solution.py:217
  32.9 5.7 %all-to-all-start.1 = ((f32[16,112,128]{2,1,0:T(8,128)}), f32[16,112,128]{2,1,0:T(8,128)S(1)}, u32[]{:S(2)}, u32[]{:S(2)}) async-start(f32[16,112,128]{2,1,0:T(8,128)} %bitcast.14), calls=%async_computation.1 | async-start | bytes 1835008 | tf_op jit(solution)/shard_map/all_to_all | solution.py:447
  38.6 1.5 %prepare.1 = (f32[10,128,128]{2,1,0:T(8,128)S(1)}, f32[10,8,128]{2,1,0:T(8,128)S(1)}, f32[10,8,128]{2,1,0:T(8,128)S(1)}) custom-call(s32[16]{0:T(128)} %land.5, f32[2,128,128]{2,1,0:T(8,128)} %vel.1, f32[3,128,128]{2,1,0:T(8,128)} %stress.1, f32[4,128,128]{2,1,0:T(8,128)} %drive.1, f32[128,128]{1,0:T(8,128)} %weight.1, f32[128,128]{1,0:T(8,128)} %pressure.1), custom_call_target="tpu_custom_call" | custom-call | tf_op jit(solution)/shard_map/prepare/pallas_call | solution.py:307
  40.1 3.1 %collective-permute-start = (f32[10,8,128]{2,1,0:T(8,128)S(1)}, f32[10,8,128]{2,1,0:T(8,128)S(1)}, u32[]{:S(2)}, u32[]{:S(2)}) collective-permute-start(f32[10,8,128]{2,1,0:T(8,128)S(1)} %get-tuple-element.20), channel_id=1, source_target_pairs={{0,1},{1,2},{2,3},{3,4},{4,5},{5,6},{6,7},{7,8},{8,9},{9,10},{10,1... | collective-permute-start | bytes 122888 | tf_op jit(solution)/shard_map/ppermute | solution.py:440
  43.2 2.2 %collective-permute-start.1 = (f32[10,8,128]{2,1,0:T(8,128)S(1)}, f32[10,8,128]{2,1,0:T(8,128)S(1)}, u32[]{:S(2)}, u32[]{:S(2)}) collective-permute-start(f32[10,8,128]{2,1,0:T(8,128)S(1)} %get-tuple-element.21), channel_id=1, source_target_pairs={{1,0},{2,1},{3,2},{4,3},{5,4},{6,5},{7,6},{8,7},{9,8},{10,9},{11,1... | collective-permute-start | bytes 122888 | tf_op jit(solution)/shard_map/ppermute | solution.py:441
  45.4 3.7 %collective-permute-done.left = f32[10,8,128]{2,1,0:T(8,128)S(1)} collective-permute-done((f32[10,8,128]{2,1,0:T(8,128)S(1)}, f32[10,8,128]{2,1,0:T(8,128)S(1)}, u32[]{:S(2)}, u32[]{:S(2)}) %collective-permute-start) | collective-permute-done | bytes 40992 | tf_op jit(solution)/shard_map/ppermute | solution.py:440
  49.2 2.2 %collective-permute-done.1.right = f32[10,8,128]{2,1,0:T(8,128)S(1)} collective-permute-done((f32[10,8,128]{2,1,0:T(8,128)S(1)}, f32[10,8,128]{2,1,0:T(8,128)S(1)}, u32[]{:S(2)}, u32[]{:S(2)}) %collective-permute-start.1) | collective-permute-done | bytes 40992 | tf_op jit(solution)/shard_map/ppermute | solution.py:441
  51.4 0.1 rows.1
  51.5 5.3 %collective-permute-start.2 = (f32[12,8,128]{2,1,0:T(8,128)S(1)}, f32[12,8,128]{2,1,0:T(8,128)S(1)}, u32[]{:S(2)}, u32[]{:S(2)}) collective-permute-start(f32[12,8,128]{2,1,0:T(8,128)S(1)} %get-tuple-element.22), channel_id=1, source_target_pairs={{0,16},{16,32},{32,48},{48,64},{64,80},{80,96},{96,112},{1,17},{17... | collective-permute-start | bytes 147464 | tf_op jit(solution)/shard_map/ppermute | solution.py:440
  56.8 1.9 %collective-permute-start.3 = (f32[12,8,128]{2,1,0:T(8,128)S(1)}, f32[12,8,128]{2,1,0:T(8,128)S(1)}, u32[]{:S(2)}, u32[]{:S(2)}) collective-permute-start(f32[12,8,128]{2,1,0:T(8,128)S(1)} %get-tuple-element.23), channel_id=1, source_target_pairs={{16,0},{32,16},{48,32},{64,48},{80,64},{96,80},{112,96},{17,1},{33... | collective-permute-start | bytes 147464 | tf_op jit(solution)/shard_map/ppermute | solution.py:441
  58.7 0.0 collective-permute-done.2.top
  58.7 3.5 %collective-permute-done.3.bottom = f32[12,8,128]{2,1,0:T(8,128)S(1)} collective-permute-done((f32[12,8,128]{2,1,0:T(8,128)S(1)}, f32[12,8,128]{2,1,0:T(8,128)S(1)}, u32[]{:S(2)}, u32[]{:S(2)}) %collective-permute-start.3) | collective-permute-done | bytes 49184 | tf_op jit(solution)/shard_map/ppermute | solution.py:441
  62.2 2.8 %evp.1 = (f32[2,128,128]{2,1,0:T(8,128)}, f32[3,128,128]{2,1,0:T(8,128)}) custom-call(f32[10,128,128]{2,1,0:T(8,128)S(1)} %get-tuple-element.19.fields, f32[10,8,128]{2,1,0:T(8,128)S(1)} %collective-permute-done.left, f32[10,8,128]{2,1,0:T(8,128)S(1)} %collective-permute-done.1.right, f32[12,8,128]{2,1,0:T(8,128)S(1)} %collective-permute-done.2.top, ...), custom_call_target="tpu_custom_call" | custom-call | tf_op jit(solution)/shard_map/evp/pallas_call | solution.py:423
  65.0 0.0 all-to-all-done.1
  65.0 2.2 %unpack.1 = f32[8,128,128]{2,1,0:T(8,128)} custom-call(s32[16]{0:T(128)} %bitcast.19, s32[16]{0:T(128)} %land.5, f32[1792,128]{1,0:T(8,128)S(1)} %bitcast.10, f32[2,128,128]{2,1,0:T(8,128)S(1)} %get-tuple-element.18.kept), custom_call_target="tpu_custom_call" | custom-call | tf_op jit(solution)/shard_map/unpack/pallas_call | solution.py:257
Async XLA Ops:
  32.9 32.0 %all-to-all-start.1 = ((f32[16,112,128]{2,1,0:T(8,128)}), f32[16,112,128]{2,1,0:T(8,128)S(1)}, u32[]{:S(2)}, u32[]{:S(2)}) async-start(f32[16,112,128]{2,1,0:T(8,128)} %bitcast.14), calls=%async_computation.1 | async-start | bytes 1835008 | tf_op jit(solution)/shard_map/all_to_all | solution.py:447
  40.1 9.0 %collective-permute-start = (f32[10,8,128]{2,1,0:T(8,128)S(1)}, f32[10,8,128]{2,1,0:T(8,128)S(1)}, u32[]{:S(2)}, u32[]{:S(2)}) collective-permute-start(f32[10,8,128]{2,1,0:T(8,128)S(1)} %get-tuple-element.20), channel_id=1, source_target_pairs={{0,1},{1,2},{2,3},{3,4},{4,5},{5,6},{6,7},{7,8},{8,9},{9,10},{10,1... | collective-permute-start | bytes 122888 | tf_op jit(solution)/shard_map/ppermute | solution.py:440
  43.2 8.1 %collective-permute-start.1 = (f32[10,8,128]{2,1,0:T(8,128)S(1)}, f32[10,8,128]{2,1,0:T(8,128)S(1)}, u32[]{:S(2)}, u32[]{:S(2)}) collective-permute-start(f32[10,8,128]{2,1,0:T(8,128)S(1)} %get-tuple-element.21), channel_id=1, source_target_pairs={{1,0},{2,1},{3,2},{4,3},{5,4},{6,5},{7,6},{8,7},{9,8},{10,9},{11,1... | collective-permute-start | bytes 122888 | tf_op jit(solution)/shard_map/ppermute | solution.py:441
  51.5 7.2 %collective-permute-start.2 = (f32[12,8,128]{2,1,0:T(8,128)S(1)}, f32[12,8,128]{2,1,0:T(8,128)S(1)}, u32[]{:S(2)}, u32[]{:S(2)}) collective-permute-start(f32[12,8,128]{2,1,0:T(8,128)S(1)} %get-tuple-element.22), channel_id=1, source_target_pairs={{0,16},{16,32},{32,48},{48,64},{64,80},{80,96},{96,112},{1,17},{17... | collective-permute-start | bytes 147464 | tf_op jit(solution)/shard_map/ppermute | solution.py:440
  56.8 5.4 %collective-permute-start.3 = (f32[12,8,128]{2,1,0:T(8,128)S(1)}, f32[12,8,128]{2,1,0:T(8,128)S(1)}, u32[]{:S(2)}, u32[]{:S(2)}) collective-permute-start(f32[12,8,128]{2,1,0:T(8,128)S(1)} %get-tuple-element.23), channel_id=1, source_target_pairs={{16,0},{32,16},{48,32},{64,48},{80,64},{96,80},{112,96},{17,1},{33... | collective-permute-start | bytes 147464 | tf_op jit(solution)/shard_map/ppermute | solution.py:441

commit v4 on v3

--- a/solution.py
+++ b/solution.py
@@ -165,66 +165,148 @@
     )
 
 
-def column_kernel(warm, share, floe, drift, recv, new_warm, flux):
-    first = pl.program_id(0) * 8
-    half = pl.program_id(1)
-
-    def tile(k, carry):
-        lanes = pl.ds(pl.multiple_of(k * 128, 128), 128)
-        kk = half * 4 + k
-
-        def field(f):
-            return recv[pl.ds(first * ROWS_OUT + f * 8 + kk, 8, stride=ROWS_OUT), :]
-
-        ocean, salinity, air, source_top, snowfall, top_resist = [field(f) for f in range(NSEND)]
-        filled = salinity > 0.25
-        sig = [salinity * (0.02 + 0.01 * j) for j in range(NLAY - NSNOW)]
-        snow_add = 0.3 * snowfall
-        sums = None
-        for c in range(NCAT):
-            temps = [warm[c, l, :, lanes] for l in range(NLAY)]
-            solved, terms = one_column(
-                temps,
-                share[c, :, lanes],
-                floe[c, :, lanes],
-                drift[c, :, lanes] + snow_add,
-                (ocean, air, source_top, top_resist),
-                sig,
+HBM = pl.BlockSpec(memory_space=pltpu.HBM)
+CHUNKS = 8
+CHUNK = 512
+
+
+def chunk_at(s):
+    rows = pl.ds(pl.multiple_of(s // 2 * 8, 8), 8)
+    lanes = pl.ds(pl.multiple_of(s % 2 * CHUNK, CHUNK), CHUNK)
+    return rows, lanes
+
+
+def fetches(s, warm, classes, warm_to, classes_to, sems):
+    rows, lanes = chunk_at(s)
+    return [pltpu.make_async_copy(warm.at[:, :, rows, lanes], warm_to, sems.at[3])] + [
+        pltpu.make_async_copy(src.at[:, rows, lanes], classes_to.at[i], sems.at[i])
+        for i, src in enumerate(classes)
+    ]
+
+
+def column_kernel(
+    warm, share, floe, drift, warm0, classes0, recv, new_warm, flux, wbuf, cbuf, obuf, fbuf, insem, outsem, fsem
+):
+    classes = (share, floe, drift)
+
+    def fetch(s, slot):
+        return fetches(s, warm, classes, wbuf.at[slot], cbuf.at[slot], insem.at[slot])
+
+    def put(s, slot):
+        rows, lanes = chunk_at(s)
+        return pltpu.make_async_copy(obuf.at[slot], new_warm.at[:, :, rows, lanes], outsem.at[slot])
+
+    def put_flux(g):
+        part = pl.ds(pl.multiple_of(g * 8 * ROWS_BACK, 8), 8 * ROWS_BACK)
+        return pltpu.make_async_copy(fbuf.at[part, :], flux.at[part, :], fsem.at[g])
+
+    def compute(s, warm_in, classes_in, out):
+        first = s // 2 * 8
+
+        def tile(k, carry):
+            kk = s % 2 * 4 + k
+            lanes = pl.ds(pl.multiple_of(k * 128, 128), 128)
+
+            def field(f):
+                return recv[pl.ds(first * ROWS_OUT + f * 8 + kk, 8, stride=ROWS_OUT), :]
+
+            ocean, salinity, air, source_top, snowfall, top_resist = [
+                field(f) for f in range(NSEND)
+            ]
+            filled = salinity > 0.25
+            sig = [salinity * (0.02 + 0.01 * j) for j in range(NLAY - NSNOW)]
+            snow_add = 0.3 * snowfall
+            sums = None
+            for c in range(NCAT):
+                temps = [warm_in[c, l, :, lanes] for l in range(NLAY)]
+                solved, terms = one_column(
+                    temps,
+                    classes_in[0, c, :, lanes],
+                    classes_in[1, c, :, lanes],
+                    classes_in[2, c, :, lanes] + snow_add,
+                    (ocean, air, source_top, top_resist),
+                    sig,
+                )
+                for l in range(NLAY):
+                    out[c, l, :, lanes] = jnp.where(filled, solved[l], temps[l])
+                sums = terms if sums is None else tuple(a + b for a, b in zip(sums, terms))
+            bottom, top, light, surface, snow, thick, held, total = sums
+            back = (
+                bottom,
+                top,
+                light,
+                surface,
+                snow,
+                thick - 0.05 * bottom,
+                0.05 * (held + top - bottom + source_top * total),
             )
-            for l in range(NLAY):
-                new_warm[c, l, :, lanes] = jnp.where(filled, solved[l], temps[l])
-            sums = terms if sums is None else tuple(a + b for a, b in zip(sums, terms))
-        bottom, top, light, surface, snow, thick, held, total = sums
-        back = (
-            bottom,
-            top,
-            light,
-            surface,
-            snow,
-            thick - 0.05 * bottom,
-            0.05 * (held + top - bottom + source_top * total),
-        )
-        for f in range(NBACK):
-            flux[pl.ds(f * 8 + kk, 8, stride=ROWS_BACK), :] = back[f]
+            for f in range(NBACK):
+                fbuf[pl.ds(first * ROWS_BACK + f * 8 + kk, 8, stride=ROWS_BACK), :] = back[f]
+            return carry
+
+        lax.fori_loop(0, 4, tile, 0, unroll=True)
+
+    def start(copies):
+        for copy in copies:
+            copy.start()
+
+    def wait(copies):
+        for copy in copies:
+            copy.wait()
+
+    start(fetch(1, 1))
+    start(fetch(2, 0))
+    compute(0, warm0, classes0, obuf.at[0])
+    put(0, 0).start()
+
+    def chunk(s, carry):
+        slot = s % 2
+        wait(fetch(s, slot))
+
+        @pl.when(s >= 2)
+        def _():
+            put(s - 2, slot).wait()
+
+        compute(s, wbuf.at[slot], cbuf.at[slot], obuf.at[slot])
+        put(s, slot).start()
+
+        @pl.when(slot == 1)
+        def _():
+            put_flux(s // 2).start()
+
+        @pl.when(s + 2 < CHUNKS)
+        def _():
+            start(fetch(s + 2, slot))
+
         return carry
 
-    lax.fori_loop(0, 4, tile, 0, unroll=True)
-
-
-def columns(warm, share, floe, drift, recv):
-    cls = pl.BlockSpec((NCAT, 8, 512), lambda g, h: (0, g, h))
-    col = pl.BlockSpec((NCAT, NLAY, 8, 512), lambda g, h: (0, 0, g, h))
+    lax.fori_loop(1, CHUNKS, chunk, 0)
+    put(CHUNKS - 2, 0).wait()
+    put(CHUNKS - 1, 1).wait()
+    for g in range(CHUNKS // 2):
+        put_flux(g).wait()
+
+
+def columns(warm, share, floe, drift, warm0, classes0, recv):
     return pl.pallas_call(
         column_kernel,
-        grid=(4, 2),
         out_shape=(
             jax.ShapeDtypeStruct((NCAT, NLAY, 32, 1024), F32),
             jax.ShapeDtypeStruct((B * CAP * ROWS_BACK, 128), F32),
         ),
-        in_specs=[col, cls, cls, cls, VSPEC],
-        out_specs=(col, pl.BlockSpec((8 * ROWS_BACK, 128), lambda g, h: (g, 0))),
+        in_specs=[HBM] * 4 + [VSPEC] * 3,
+        out_specs=(HBM, HBM),
+        scratch_shapes=[
+            pltpu.VMEM((2, NCAT, NLAY, 8, CHUNK), F32),
+            pltpu.VMEM((2, 3, NCAT, 8, CHUNK), F32),
+            pltpu.VMEM((2, NCAT, NLAY, 8, CHUNK), F32),
+            pltpu.VMEM((B * CAP * ROWS_BACK, 128), F32),
+            pltpu.SemaphoreType.DMA((2, 4)),
+            pltpu.SemaphoreType.DMA((2,)),
+            pltpu.SemaphoreType.DMA((4,)),
+        ],
         name="columns",
-    )(warm, share, floe, drift, vmem(recv))
+    )(warm, share, floe, drift, *vmem(warm0, classes0, recv))
 
 
 def unpack_kernel(own, land, back, kept, out, tile, count, sems):
@@ -268,7 +350,13 @@
     )(own, land, *vmem(back, kept))
 
 
-def prepare_kernel(land, vel, stress, drive, weight, pressure, fields, left, right):
+def prepare_kernel(
+    land, vel, stress, drive, weight, pressure, warm, share, floe, drift,
+    fields, left, right, up, down, warm0, classes0, sems,
+):
+    copies = fetches(0, warm, (share, floe, drift), warm0, classes0, sems)
+    for copy in copies:
+        copy.start()
     group = lax.broadcasted_iota(jnp.int32, (32, 128), 1) // 32
     fields[0:2] = vel[...]
     fields[2:5] = stress[...]
@@ -295,6 +383,10 @@
             to_right = jnp.where(piece == t, turn(x, 8 * t + 8), to_right)
         left[f] = to_left
         right[f] = to_right
+    up[...] = fields[:, 0:8, :]
+    down[...] = fields[:, 120:128, :]
+    for copy in copies:
+        copy.wait()
 
 
 def turn(x, shift):
@@ -302,21 +394,30 @@
     return pltpu.roll(x, shift, 1) if shift else x
 
 
-def prepare(land, vel, stress, drive, weight, pressure):
+def prepare(land, vel, stress, drive, weight, pressure, *columns_in):
     edge = pltpu.VMEM((NF, 8, 128), F32)
     return pl.pallas_call(
         prepare_kernel,
-        out_shape=(pltpu.VMEM((NF, 128, 128), F32), edge, edge),
-        in_specs=[SSPEC] + [VSPEC] * 5,
-        out_specs=(VSPEC, VSPEC, VSPEC),
+        out_shape=(
+            jax.ShapeDtypeStruct((NF, 128, 128), F32),
+            edge,
+            edge,
+            edge,
+            edge,
+            pltpu.VMEM((NCAT, NLAY, 8, CHUNK), F32),
+            pltpu.VMEM((3, NCAT, 8, CHUNK), F32),
+        ),
+        in_specs=[SSPEC] + [VSPEC] * 5 + [HBM] * 4,
+        out_specs=(VSPEC,) * 7,
+        scratch_shapes=[pltpu.SemaphoreType.DMA((4,))],
         name="prepare",
-    )(land, vel, stress, drive, weight, pressure)
-
-
-def rows_kernel(fields, left, right, up, down):
+    )(land, vel, stress, drive, weight, pressure, *columns_in)
+
+
+def rows_kernel(first_rows, last_rows, left, right, up, down):
     piece = lax.broadcasted_iota(jnp.int32, (8, 128), 1) // 8
-    for dst, first, t in ((up, 0, 0), (down, 120, 15)):
-        dst[0:NF] = fields[:, first : first + 8, :]
+    for dst, src, t in ((up, first_rows, 0), (down, last_rows, 15)):
+        dst[0:NF] = src[...]
         for i, side in enumerate((left, right)):
             corner = jnp.zeros((8, 128), F32)
             for f in range(NF):
@@ -324,15 +425,32 @@
             dst[NF + i] = corner
 
 
-def edge_rows(fields, left, right):
+def edge_rows(first_rows, last_rows, left, right):
     edge = pltpu.VMEM((NF + 2, 8, 128), F32)
     return pl.pallas_call(
         rows_kernel,
         out_shape=(edge, edge),
-        in_specs=[VSPEC] * 3,
+        in_specs=[VSPEC] * 4,
         out_specs=(VSPEC, VSPEC),
         name="rows",
-    )(*vmem(fields, left, right))
+    )(*vmem(first_rows, last_rows, left, right))
+
+
+def stage_kernel(fields, _, staged, sem):
+    copy = pltpu.make_async_copy(fields, staged, sem)
+    copy.start()
+    copy.wait()
+
+
+def stage(fields, after):
+    return pl.pallas_call(
+        stage_kernel,
+        out_shape=pltpu.VMEM((NF, 128, 128), F32),
+        in_specs=[HBM, VSPEC],
+        out_specs=VSPEC,
+        scratch_shapes=[pltpu.SemaphoreType.DMA(())],
+        name="stage",
+    )(fields, vmem(after))
 
 
 GUARD = 8
@@ -468,19 +586,22 @@
     payload, kept = pack(own, land, conditions)
     recv = swap(payload, ROWS_OUT)
 
-    fields, to_left, to_right = prepare(land, velocity, stress, drive, weight, pressure)
-    left, right = exchange("gy", to_left, to_right)
-
-    new_warm, flux = columns(
+    columns_in = (
         warmth.transpose(1, 2, 0, 3),
         share.transpose(1, 0, 2),
         floe.transpose(1, 0, 2),
         drift.transpose(1, 0, 2),
-        recv,
     )
+    fields, to_left, to_right, first, last, warm0, classes0 = prepare(
+        land, velocity, stress, drive, weight, pressure, *columns_in
+    )
+    left, right = exchange("gy", to_left, to_right)
+
+    new_warm, flux = columns(*columns_in, warm0, classes0, recv)
     back = swap(flux, ROWS_BACK)
-    first_rows, last_rows = edge_rows(fields, left, right)
+    first_rows, last_rows = edge_rows(first, last, left, right)
     top, bottom = exchange("gx", first_rows, last_rows)
+    fields = stage(fields, first_rows)
     velocity_new, stress_new = evp(fields, left, right, top, bottom)
     exchanges = unpack(own, land, back, kept)
     return (new_warm.transpose(2, 0, 1, 3), exchanges, velocity_new, stress_new)

time: 67.8 us -> 65.7 us (0.969)
  blocking collectives: 18.9 us -> 0 us
  waiting for transfers between devices: 9.4 us -> 17.1 us
  starting transfers between devices: 18.2 us -> 25.7 us
  Pallas kernels: 20 us -> 21.3 us
    all_to_all x1 -> x0, blocking collectives: 18.9 us -> none  [swap(): lax.all_to_all(payload.reshape(n, CAP * rows, 128), 'gy', split_axis=0, c...]
    all_to_all x1 -> x2, waiting for transfers between devices: 0.01 us -> 8.3 us  [swap(): lax.all_to_all(payload.reshape(n, CAP * rows, 128), 'gy', split_axis=0, c...]
    all_to_all x1 -> x2, starting transfers between devices: 5.65 us -> 12.8 us  [swap(): lax.all_to_all(payload.reshape(n, CAP * rows, 128), 'gy', split_axis=0, c...]
    ppermute x2, waiting for transfers between devices: 5.65 us -> 3.84 us  [exchange(): from_upper = lax.ppermute(to_lower, axis, down)]
    ppermute x2, waiting for transfers between devices: 3.74 us -> 5.01 us  [exchange(): from_lower = lax.ppermute(to_upper, axis, up)]
    pallas_call x1, Pallas kernels: 1.77 us -> 2.65 us  [pack(): pl.pallas_call(pack_kernel, out_shape=(pltpu.VMEM((B * CAP * ROWS_OUT, 12...]
    pallas_call x3 -> x4, Pallas kernels: 13.3 us -> 13.7 us  [the longest x1 8.95 us: columns(): pl.pallas_call(column_kernel, out_shape=(jax.ShapeDtypeStruct((NCAT, NLAY...]
  transfers between devices with their start and end apart: 5 -> 6, of which waited for: 3 -> 4; matrix products, arithmetic and copies ran while one was open for 0% -> 0% of each run, Pallas kernels for 7% -> 12%
where the time goes in v4:
time: 65.7 us; the launch traced here: 64.8 us
  starting transfers between devices  25.7 us (39%)
  Pallas kernels  21.3 us (32%)
  waiting for transfers between devices  17.1 us (26%)
  between operations  0.71 us (1%)
    all_to_all x2, starting transfers between devices, swap(): lax.all_to_all(payload.reshape(n, CAP * rows, 128), 'gy', split_axis=0, c...  12.8 us
    pallas_call x1, Pallas kernels, columns(): pl.pallas_call(column_kernel, out_shape=(jax.ShapeDtypeStruct((NCAT, NLAY...  8.95 us
    ppermute x2, starting transfers between devices, exchange(): from_lower = lax.ppermute(to_upper, axis, up)  8.76 us
    all_to_all x2, waiting for transfers between devices, swap(): lax.all_to_all(payload.reshape(n, CAP * rows, 128), 'gy', split_axis=0, c...  8.3 us
    ppermute x2, waiting for transfers between devices, exchange(): from_lower = lax.ppermute(to_upper, axis, up)  5.01 us
    ppermute x2, starting transfers between devices, exchange(): from_upper = lax.ppermute(to_lower, axis, down)  4.11 us
    ppermute x2, waiting for transfers between devices, exchange(): from_upper = lax.ppermute(to_lower, axis, down)  3.84 us
    pallas_call x1, Pallas kernels, prepare(): pl.pallas_call(prepare_kernel, out_shape=(jax.ShapeDtypeStruct((NF, 128,...  3.55 us
  transfers between devices with their start and end apart: 6, of which 4 were waited for; matrix products, arithmetic and copies ran while one was open for 0% of the time, Pallas kernels for 12%

profile of v4, /device:TPU:7, one launch (start us, length us, event | category | flops | bytes accessed | tf_op | source)
XLA Modules:
  0.0 64.8 jit_solution(7899449258484274143)
XLA Ops:
  0.6 2.6 %pack.1 = (f32[1536,128]{1,0:T(8,128)}, f32[2,128,128]{2,1,0:T(8,128)S(1)}) custom-call(s32[16]{0:T(128)} %bitcast.21, s32[16]{0:T(128)} %land.5, f32[8,128,128]{2,1,0:T(8,128)} %x.1), custom_call_target="tpu_custom_call" | custom-call | tf_op jit(solution)/shard_map/pack/pallas_call | solution.py:103
  3.3 7.7 %all-to-all-start = ((f32[16,96,128]{2,1,0:T(8,128)}), f32[16,96,128]{2,1,0:T(8,128)S(1)}, u32[]{:S(2)}, u32[]{:S(2)}) async-start(f32[16,96,128]{2,1,0:T(8,128)} %bitcast.5), calls=%async_computation | async-start | bytes 1572864 | tf_op jit(solution)/shard_map/all_to_all | solution.py:565
  11.0 3.5 %prepare.1 = (f32[10,128,128]{2,1,0:T(8,128)}, f32[10,8,128]{2,1,0:T(8,128)S(1)}, f32[10,8,128]{2,1,0:T(8,128)S(1)}, f32[10,8,128]{2,1,0:T(8,128)S(1)}, f32[10,8...) custom-call(s32[16]{0:T(128)} %land.5, f32[2,128,128]{2,1,0:T(8,128)} %vel.1, ...), custom_call_target="tpu_custom_call" | custom-call | tf_op jit(solution)/shard_map/prepare/pallas_call | solution.py:399
  14.5 8.3 %all-to-all-done = f32[16,96,128]{2,1,0:T(8,128)S(1)} async-done(((f32[16,96,128]{2,1,0:T(8,128)}), f32[16,96,128]{2,1,0:T(8,128)S(1)}, u32[]{:S(2)}, u32[]{:S(2)}) %all-to-all-start) | async-done | bytes 786464 | tf_op jit(solution)/shard_map/all_to_all | solution.py:565
  22.8 9.0 %columns.1 = (f32[5,10,32,1024]{3,2,1,0:T(8,128)}, f32[1792,128]{1,0:T(8,128)}) custom-call(f32[5,10,32,1024]{3,2,1,0:T(8,128)} %bitcast.13, f32[5,32,1024]{2,1,0:T(8,128)} %bitcast.15, f32[5,32,1024]{2,1,0:T(8,128)} %bitcast.17, f32[5,32,1024]{2,1,0:T(8,128)} %bitcast.19, f32[5,10,8,512]{3,2,1,0:T(8,128)S(1)} %get-tuple-element.19.warm0, ...), custom_call_target="tpu_custom_call" | custom-call | tf_op jit(solution)/shard_map/columns/pallas_call | solution.py:291
  31.8 5.1 %all-to-all-start.1 = ((f32[16,112,128]{2,1,0:T(8,128)}), f32[16,112,128]{2,1,0:T(8,128)S(1)}, u32[]{:S(2)}, u32[]{:S(2)}) async-start(f32[16,112,128]{2,1,0:T(8,128)} %bitcast.20), calls=%async_computation.1 | async-start | bytes 1835008 | tf_op jit(solution)/shard_map/all_to_all | solution.py:565
  36.9 3.1 %collective-permute-start = (f32[10,8,128]{2,1,0:T(8,128)S(1)}, f32[10,8,128]{2,1,0:T(8,128)S(1)}, u32[]{:S(2)}, u32[]{:S(2)}) collective-permute-start(f32[10,8,128]{2,1,0:T(8,128)S(1)} %get-tuple-element.28), channel_id=1, source_target_pairs={{0,1},{1,2},{2,3},{3,4},{4,5},{5,6},{6,7},{7,8},{8,9},{9,10},{10,1... | collective-permute-start | bytes 122888 | tf_op jit(solution)/shard_map/ppermute | solution.py:558
  40.0 2.2 %collective-permute-start.1 = (f32[10,8,128]{2,1,0:T(8,128)S(1)}, f32[10,8,128]{2,1,0:T(8,128)S(1)}, u32[]{:S(2)}, u32[]{:S(2)}) collective-permute-start(f32[10,8,128]{2,1,0:T(8,128)S(1)} %get-tuple-element.29), channel_id=1, source_target_pairs={{1,0},{2,1},{3,2},{4,3},{5,4},{6,5},{7,6},{8,7},{9,8},{10,9},{11,1... | collective-permute-start | bytes 122888 | tf_op jit(solution)/shard_map/ppermute | solution.py:559
  42.2 5.0 %collective-permute-done.left = f32[10,8,128]{2,1,0:T(8,128)S(1)} collective-permute-done((f32[10,8,128]{2,1,0:T(8,128)S(1)}, f32[10,8,128]{2,1,0:T(8,128)S(1)}, u32[]{:S(2)}, u32[]{:S(2)}) %collective-permute-start) | collective-permute-done | bytes 40992 | tf_op jit(solution)/shard_map/ppermute | solution.py:558
  47.2 1.5 %collective-permute-done.1.right = f32[10,8,128]{2,1,0:T(8,128)S(1)} collective-permute-done((f32[10,8,128]{2,1,0:T(8,128)S(1)}, f32[10,8,128]{2,1,0:T(8,128)S(1)}, u32[]{:S(2)}, u32[]{:S(2)}) %collective-permute-start.1) | collective-permute-done | bytes 40992 | tf_op jit(solution)/shard_map/ppermute | solution.py:559
  48.7 0.1 rows.1
  48.8 5.7 %collective-permute-start.2 = (f32[12,8,128]{2,1,0:T(8,128)S(1)}, f32[12,8,128]{2,1,0:T(8,128)S(1)}, u32[]{:S(2)}, u32[]{:S(2)}) collective-permute-start(f32[12,8,128]{2,1,0:T(8,128)S(1)} %get-tuple-element.31), channel_id=1, source_target_pairs={{0,16},{16,32},{32,48},{48,64},{64,80},{80,96},{96,112},{1,17},{17... | collective-permute-start | bytes 147464 | tf_op jit(solution)/shard_map/ppermute | solution.py:558
  54.4 1.9 %collective-permute-start.3 = (f32[12,8,128]{2,1,0:T(8,128)S(1)}, f32[12,8,128]{2,1,0:T(8,128)S(1)}, u32[]{:S(2)}, u32[]{:S(2)}) collective-permute-start(f32[12,8,128]{2,1,0:T(8,128)S(1)} %get-tuple-element.30._), channel_id=1, source_target_pairs={{16,0},{32,16},{48,32},{64,48},{80,64},{96,80},{112,96},{17,1},{33... | collective-permute-start | bytes 147464 | tf_op jit(solution)/shard_map/ppermute | solution.py:559
  56.4 1.1 %stage.1.fields = f32[10,128,128]{2,1,0:T(8,128)S(1)} custom-call(f32[10,128,128]{2,1,0:T(8,128)} %get-tuple-element.25.fields, f32[12,8,128]{2,1,0:T(8,128)S(1)} %get-tuple-element.30._), custom_call_target="tpu_custom_call" | custom-call | tf_op jit(solution)/shard_map/stage/pallas_call | solution.py:446
  57.5 0.0 collective-permute-done.2.top
  57.5 2.4 %collective-permute-done.3.bottom = f32[12,8,128]{2,1,0:T(8,128)S(1)} collective-permute-done((f32[12,8,128]{2,1,0:T(8,128)S(1)}, f32[12,8,128]{2,1,0:T(8,128)S(1)}, u32[]{:S(2)}, u32[]{:S(2)}) %collective-permute-start.3) | collective-permute-done | bytes 49184 | tf_op jit(solution)/shard_map/ppermute | solution.py:559
  59.9 2.8 %evp.1 = (f32[2,128,128]{2,1,0:T(8,128)}, f32[3,128,128]{2,1,0:T(8,128)}) custom-call(f32[10,128,128]{2,1,0:T(8,128)S(1)} %stage.1.fields, f32[10,8,128]{2,1,0:T(8,128)S(1)} %collective-permute-done.left, f32[10,8,128]{2,1,0:T(8,128)S(1)} %collective-permute-done.1.right, f32[12,8,128]{2,1,0:T(8,128)S(1)} %collective-permute-done.2.top, ...), custom_call_target="tpu_custom_call" | custom-call | tf_op jit(solution)/shard_map/evp/pallas_call | solution.py:541
  62.6 0.0 all-to-all-done.1
  62.6 2.2 %unpack.1 = f32[8,128,128]{2,1,0:T(8,128)} custom-call(s32[16]{0:T(128)} %bitcast.22, s32[16]{0:T(128)} %land.5, f32[1792,128]{1,0:T(8,128)S(1)} %bitcast.10, f32[2,128,128]{2,1,0:T(8,128)S(1)} %get-tuple-element.24.kept), custom_call_target="tpu_custom_call" | custom-call | tf_op jit(solution)/shard_map/unpack/pallas_call | solution.py:339
Async XLA Ops:
  3.3 19.6 %all-to-all-start = ((f32[16,96,128]{2,1,0:T(8,128)}), f32[16,96,128]{2,1,0:T(8,128)S(1)}, u32[]{:S(2)}, u32[]{:S(2)}) async-start(f32[16,96,128]{2,1,0:T(8,128)} %bitcast.5), calls=%async_computation | async-start | bytes 1572864 | tf_op jit(solution)/shard_map/all_to_all | solution.py:565
  31.8 30.8 %all-to-all-start.1 = ((f32[16,112,128]{2,1,0:T(8,128)}), f32[16,112,128]{2,1,0:T(8,128)S(1)}, u32[]{:S(2)}, u32[]{:S(2)}) async-start(f32[16,112,128]{2,1,0:T(8,128)} %bitcast.20), calls=%async_computation.1 | async-start | bytes 1835008 | tf_op jit(solution)/shard_map/all_to_all | solution.py:565
  36.9 10.3 %collective-permute-start = (f32[10,8,128]{2,1,0:T(8,128)S(1)}, f32[10,8,128]{2,1,0:T(8,128)S(1)}, u32[]{:S(2)}, u32[]{:S(2)}) collective-permute-start(f32[10,8,128]{2,1,0:T(8,128)S(1)} %get-tuple-element.28), channel_id=1, source_target_pairs={{0,1},{1,2},{2,3},{3,4},{4,5},{5,6},{6,7},{7,8},{8,9},{9,10},{10,1... | collective-permute-start | bytes 122888 | tf_op jit(solution)/shard_map/ppermute | solution.py:558
  40.0 8.7 %collective-permute-start.1 = (f32[10,8,128]{2,1,0:T(8,128)S(1)}, f32[10,8,128]{2,1,0:T(8,128)S(1)}, u32[]{:S(2)}, u32[]{:S(2)}) collective-permute-start(f32[10,8,128]{2,1,0:T(8,128)S(1)} %get-tuple-element.29), channel_id=1, source_target_pairs={{1,0},{2,1},{3,2},{4,3},{5,4},{6,5},{7,6},{8,7},{9,8},{10,9},{11,1... | collective-permute-start | bytes 122888 | tf_op jit(solution)/shard_map/ppermute | solution.py:559
  48.8 8.7 %collective-permute-start.2 = (f32[12,8,128]{2,1,0:T(8,128)S(1)}, f32[12,8,128]{2,1,0:T(8,128)S(1)}, u32[]{:S(2)}, u32[]{:S(2)}) collective-permute-start(f32[12,8,128]{2,1,0:T(8,128)S(1)} %get-tuple-element.31), channel_id=1, source_target_pairs={{0,16},{16,32},{32,48},{48,64},{64,80},{80,96},{96,112},{1,17},{17... | collective-permute-start | bytes 147464 | tf_op jit(solution)/shard_map/ppermute | solution.py:558
  54.4 5.4 %collective-permute-start.3 = (f32[12,8,128]{2,1,0:T(8,128)S(1)}, f32[12,8,128]{2,1,0:T(8,128)S(1)}, u32[]{:S(2)}, u32[]{:S(2)}) collective-permute-start(f32[12,8,128]{2,1,0:T(8,128)S(1)} %get-tuple-element.30._), channel_id=1, source_target_pairs={{16,0},{32,16},{48,32},{64,48},{80,64},{96,80},{112,96},{17,1},{33... | collective-permute-start | bytes 147464 | tf_op jit(solution)/shard_map/ppermute | solution.py:559

commit v5 on v4

--- a/solution.py
+++ b/solution.py
@@ -22,6 +22,7 @@
 LOG2E = 1.4426950408889634
 VSPEC = pl.BlockSpec(memory_space=pltpu.VMEM)
 SSPEC = pl.BlockSpec(memory_space=pltpu.SMEM)
+HBM = pl.BlockSpec(memory_space=pltpu.HBM)
 
 
 def vmem(*arrays):
@@ -68,14 +69,37 @@
         count[o] = 0
 
 
-def pack_kernel(own, land, x, out, kept, count):
-    out[...] = jnp.zeros_like(out)
-    kept[0] = 0.7 * x[3]
-    kept[1] = -0.05 * x[1]
+def pack_kernel(own, land, x_hbm, out, kept, x, staged, count, taken, insem, outsem):
+    reads = []
+    for bx in range(4):
+        part = pl.ds(32 * bx, 32)
+        reads.append(pltpu.make_async_copy(x_hbm.at[:, part, :], x.at[:, part, :], insem.at[bx]))
+        reads[-1].start()
+    zeros = pl.ds(B * ROWS_OUT, ROWS_OUT)
+    staged[zeros, :] = jnp.zeros((ROWS_OUT, 128), F32)
     start_count(count)
     slots = block_slots(own, land, count, range(B))
+    for s in range(B * CAP):
+        taken[s] = 0
+    for b in range(B):
+
+        @pl.when(land[b] == 0)
+        def _():
+            taken[slots[b]] = 1
+
+    def send(source, slot):
+        rows = pl.ds(pl.multiple_of(slot * ROWS_OUT, 8), ROWS_OUT)
+        pltpu.make_async_copy(staged.at[source, :], out.at[rows, :], outsem).start()
+
+    for s in range(B * CAP):
+
+        @pl.when(taken[s] == 0)
+        def _():
+            send(zeros, s)
+
     group = lane_groups()
     for bx in range(4):
+        reads[bx].wait()
 
         def rows(f):
             return [x[f, pl.ds(32 * bx + q, 8, stride=4), :] for q in range(4)]
@@ -92,20 +116,36 @@
         blocks = [swap_groups(r, group) for r in fields]
         for by in range(4):
             b = 4 * bx + by
+            for f in range(NSEND):
+                staged[b * ROWS_OUT + f * 8 : b * ROWS_OUT + f * 8 + 8, :] = blocks[f][by]
 
             @pl.when(land[b] == 0)
             def _():
-                for f in range(NSEND):
-                    out[pl.ds(pl.multiple_of(slots[b] * ROWS_OUT + f * 8, 8), 8), :] = blocks[f][by]
+                send(pl.ds(b * ROWS_OUT, ROWS_OUT), slots[b])
+
+    kept[0] = 0.7 * x[3]
+    kept[1] = -0.05 * x[1]
+    whole = pl.ds(0, B * CAP * ROWS_OUT)
+    pltpu.make_async_copy(out.at[whole, :], out.at[whole, :], outsem).wait()
 
 
 def pack(own, land, conditions):
     return pl.pallas_call(
         pack_kernel,
-        out_shape=(pltpu.VMEM((B * CAP * ROWS_OUT, 128), F32), pltpu.VMEM((2, 128, 128), F32)),
-        in_specs=[SSPEC, SSPEC, VSPEC],
-        out_specs=(VSPEC, VSPEC),
-        scratch_shapes=[pltpu.SMEM((B,), jnp.int32)],
+        out_shape=(
+            jax.ShapeDtypeStruct((B * CAP * ROWS_OUT, 128), F32),
+            pltpu.VMEM((2, 128, 128), F32),
+        ),
+        in_specs=[SSPEC, SSPEC, HBM],
+        out_specs=(HBM, VSPEC),
+        scratch_shapes=[
+            pltpu.VMEM((8, 128, 128), F32),
+            pltpu.VMEM(((B + 1) * ROWS_OUT, 128), F32),
+            pltpu.SMEM((B,), jnp.int32),
+            pltpu.SMEM((B * CAP,), jnp.int32),
+            pltpu.SemaphoreType.DMA((4,)),
+            pltpu.SemaphoreType.DMA(()),
+        ],
         name="pack",
     )(own, land, conditions)
 
@@ -165,7 +205,6 @@
     )
 
 
-HBM = pl.BlockSpec(memory_space=pltpu.HBM)
 CHUNKS = 8
 CHUNK = 512
 

time: 65.7 us -> 66.2 us (level)
  transfers between devices with their start and end apart: 6 -> 6, of which waited for: 4 -> 4; matrix products, arithmetic and copies ran while one was open for 0% -> 0% of each run, Pallas kernels for 12% -> 11%
where the time goes in v5:
time: 66.2 us; the launch traced here: 65.3 us
  starting transfers between devices  25.7 us (39%)
  Pallas kernels  21.8 us (33%)
  waiting for transfers between devices  17.1 us (26%)
  between operations  0.71 us (1%)
    all_to_all x2, starting transfers between devices, swap(): lax.all_to_all(payload.reshape(n, CAP * rows, 128), 'gy', split_axis=0, c...  12.8 us
    pallas_call x1, Pallas kernels, columns(): pl.pallas_call(column_kernel, out_shape=(jax.ShapeDtypeStruct((NCAT, NLAY...  8.95 us
    ppermute x2, starting transfers between devices, exchange(): from_lower = lax.ppermute(to_upper, axis, up)  8.78 us
    all_to_all x2, waiting for transfers between devices, swap(): lax.all_to_all(payload.reshape(n, CAP * rows, 128), 'gy', split_axis=0, c...  8.3 us
    ppermute x2, waiting for transfers between devices, exchange(): from_lower = lax.ppermute(to_upper, axis, up)  5.01 us
    ppermute x2, starting transfers between devices, exchange(): from_upper = lax.ppermute(to_lower, axis, down)  4.11 us
    ppermute x2, waiting for transfers between devices, exchange(): from_upper = lax.ppermute(to_lower, axis, down)  3.83 us
    pallas_call x1, Pallas kernels, prepare(): pl.pallas_call(prepare_kernel, out_shape=(jax.ShapeDtypeStruct((NF, 128,...  3.55 us
  transfers between devices with their start and end apart: 6, of which 4 were waited for; matrix products, arithmetic and copies ran while one was open for 0% of the time, Pallas kernels for 11%

profile of v5, /device:TPU:7, one launch (start us, length us, event | category | flops | bytes accessed | tf_op | source)
XLA Modules:
  0.0 65.3 jit_solution(14168636452810281078)
XLA Ops:
  0.6 3.1 %pack.1 = (f32[1536,128]{1,0:T(8,128)}, f32[2,128,128]{2,1,0:T(8,128)S(1)}) custom-call(s32[16]{0:T(128)} %bitcast.22, s32[16]{0:T(128)} %land.5, f32[8,128,128]{2,1,0:T(8,128)} %x_hbm.1), custom_call_target="tpu_custom_call" | custom-call | tf_op jit(solution)/shard_map/pack/pallas_call | solution.py:133
  3.7 7.7 %all-to-all-start = ((f32[16,96,128]{2,1,0:T(8,128)}), f32[16,96,128]{2,1,0:T(8,128)S(1)}, u32[]{:S(2)}, u32[]{:S(2)}) async-start(f32[16,96,128]{2,1,0:T(8,128)} %bitcast.21), calls=%async_computation | async-start | bytes 1572864 | tf_op jit(solution)/shard_map/all_to_all | solution.py:604
  11.4 3.5 %prepare.1 = (f32[10,128,128]{2,1,0:T(8,128)}, f32[10,8,128]{2,1,0:T(8,128)S(1)}, f32[10,8,128]{2,1,0:T(8,128)S(1)}, f32[10,8,128]{2,1,0:T(8,128)S(1)}, f32[10,8...) custom-call(s32[16]{0:T(128)} %land.5, f32[2,128,128]{2,1,0:T(8,128)} %vel.1, ...), custom_call_target="tpu_custom_call" | custom-call | tf_op jit(solution)/shard_map/prepare/pallas_call | solution.py:438
  15.0 8.3 %all-to-all-done = f32[16,96,128]{2,1,0:T(8,128)S(1)} async-done(((f32[16,96,128]{2,1,0:T(8,128)}), f32[16,96,128]{2,1,0:T(8,128)S(1)}, u32[]{:S(2)}, u32[]{:S(2)}) %all-to-all-start) | async-done | bytes 786464 | tf_op jit(solution)/shard_map/all_to_all | solution.py:604
  23.3 9.0 %columns.1 = (f32[5,10,32,1024]{3,2,1,0:T(8,128)}, f32[1792,128]{1,0:T(8,128)}) custom-call(f32[5,10,32,1024]{3,2,1,0:T(8,128)} %bitcast.13, f32[5,32,1024]{2,1,0:T(8,128)} %bitcast.15, f32[5,32,1024]{2,1,0:T(8,128)} %bitcast.17, f32[5,32,1024]{2,1,0:T(8,128)} %bitcast.19, f32[5,10,8,512]{3,2,1,0:T(8,128)S(1)} %get-tuple-element.19.warm0, ...), custom_call_target="tpu_custom_call" | custom-call | tf_op jit(solution)/shard_map/columns/pallas_call | solution.py:330
  32.2 5.1 %all-to-all-start.1 = ((f32[16,112,128]{2,1,0:T(8,128)}), f32[16,112,128]{2,1,0:T(8,128)S(1)}, u32[]{:S(2)}, u32[]{:S(2)}) async-start(f32[16,112,128]{2,1,0:T(8,128)} %bitcast.20), calls=%async_computation.1 | async-start | bytes 1835008 | tf_op jit(solution)/shard_map/all_to_all | solution.py:604
  37.3 3.1 %collective-permute-start = (f32[10,8,128]{2,1,0:T(8,128)S(1)}, f32[10,8,128]{2,1,0:T(8,128)S(1)}, u32[]{:S(2)}, u32[]{:S(2)}) collective-permute-start(f32[10,8,128]{2,1,0:T(8,128)S(1)} %get-tuple-element.28), channel_id=1, source_target_pairs={{0,1},{1,2},{2,3},{3,4},{4,5},{5,6},{6,7},{7,8},{8,9},{9,10},{10,1... | collective-permute-start | bytes 122888 | tf_op jit(solution)/shard_map/ppermute | solution.py:597
  40.4 2.2 %collective-permute-start.1 = (f32[10,8,128]{2,1,0:T(8,128)S(1)}, f32[10,8,128]{2,1,0:T(8,128)S(1)}, u32[]{:S(2)}, u32[]{:S(2)}) collective-permute-start(f32[10,8,128]{2,1,0:T(8,128)S(1)} %get-tuple-element.29), channel_id=1, source_target_pairs={{1,0},{2,1},{3,2},{4,3},{5,4},{6,5},{7,6},{8,7},{9,8},{10,9},{11,1... | collective-permute-start | bytes 122888 | tf_op jit(solution)/shard_map/ppermute | solution.py:598
  42.6 5.0 %collective-permute-done.left = f32[10,8,128]{2,1,0:T(8,128)S(1)} collective-permute-done((f32[10,8,128]{2,1,0:T(8,128)S(1)}, f32[10,8,128]{2,1,0:T(8,128)S(1)}, u32[]{:S(2)}, u32[]{:S(2)}) %collective-permute-start) | collective-permute-done | bytes 40992 | tf_op jit(solution)/shard_map/ppermute | solution.py:597
  47.6 1.5 %collective-permute-done.1.right = f32[10,8,128]{2,1,0:T(8,128)S(1)} collective-permute-done((f32[10,8,128]{2,1,0:T(8,128)S(1)}, f32[10,8,128]{2,1,0:T(8,128)S(1)}, u32[]{:S(2)}, u32[]{:S(2)}) %collective-permute-start.1) | collective-permute-done | bytes 40992 | tf_op jit(solution)/shard_map/ppermute | solution.py:598
  49.1 0.1 rows.1
  49.2 5.7 %collective-permute-start.2 = (f32[12,8,128]{2,1,0:T(8,128)S(1)}, f32[12,8,128]{2,1,0:T(8,128)S(1)}, u32[]{:S(2)}, u32[]{:S(2)}) collective-permute-start(f32[12,8,128]{2,1,0:T(8,128)S(1)} %get-tuple-element.31), channel_id=1, source_target_pairs={{0,16},{16,32},{32,48},{48,64},{64,80},{80,96},{96,112},{1,17},{17... | collective-permute-start | bytes 147464 | tf_op jit(solution)/shard_map/ppermute | solution.py:597
  54.9 1.9 %collective-permute-start.3 = (f32[12,8,128]{2,1,0:T(8,128)S(1)}, f32[12,8,128]{2,1,0:T(8,128)S(1)}, u32[]{:S(2)}, u32[]{:S(2)}) collective-permute-start(f32[12,8,128]{2,1,0:T(8,128)S(1)} %get-tuple-element.30._), channel_id=1, source_target_pairs={{16,0},{32,16},{48,32},{64,48},{80,64},{96,80},{112,96},{17,1},{33... | collective-permute-start | bytes 147464 | tf_op jit(solution)/shard_map/ppermute | solution.py:598
  56.9 1.1 %stage.1.fields = f32[10,128,128]{2,1,0:T(8,128)S(1)} custom-call(f32[10,128,128]{2,1,0:T(8,128)} %get-tuple-element.25.fields, f32[12,8,128]{2,1,0:T(8,128)S(1)} %get-tuple-element.30._), custom_call_target="tpu_custom_call" | custom-call | tf_op jit(solution)/shard_map/stage/pallas_call | solution.py:485
  58.0 0.0 collective-permute-done.2.top
  58.0 2.4 %collective-permute-done.3.bottom = f32[12,8,128]{2,1,0:T(8,128)S(1)} collective-permute-done((f32[12,8,128]{2,1,0:T(8,128)S(1)}, f32[12,8,128]{2,1,0:T(8,128)S(1)}, u32[]{:S(2)}, u32[]{:S(2)}) %collective-permute-start.3) | collective-permute-done | bytes 49184 | tf_op jit(solution)/shard_map/ppermute | solution.py:598
  60.3 2.8 %evp.1 = (f32[2,128,128]{2,1,0:T(8,128)}, f32[3,128,128]{2,1,0:T(8,128)}) custom-call(f32[10,128,128]{2,1,0:T(8,128)S(1)} %stage.1.fields, f32[10,8,128]{2,1,0:T(8,128)S(1)} %collective-permute-done.left, f32[10,8,128]{2,1,0:T(8,128)S(1)} %collective-permute-done.1.right, f32[12,8,128]{2,1,0:T(8,128)S(1)} %collective-permute-done.2.top, ...), custom_call_target="tpu_custom_call" | custom-call | tf_op jit(solution)/shard_map/evp/pallas_call | solution.py:580
  63.1 0.0 all-to-all-done.1
  63.1 2.2 %unpack.1 = f32[8,128,128]{2,1,0:T(8,128)} custom-call(s32[16]{0:T(128)} %bitcast.23, s32[16]{0:T(128)} %land.5, f32[1792,128]{1,0:T(8,128)S(1)} %bitcast.10, f32[2,128,128]{2,1,0:T(8,128)S(1)} %get-tuple-element.24.kept), custom_call_target="tpu_custom_call" | custom-call | tf_op jit(solution)/shard_map/unpack/pallas_call | solution.py:378
Async XLA Ops:
  3.7 19.6 %all-to-all-start = ((f32[16,96,128]{2,1,0:T(8,128)}), f32[16,96,128]{2,1,0:T(8,128)S(1)}, u32[]{:S(2)}, u32[]{:S(2)}) async-start(f32[16,96,128]{2,1,0:T(8,128)} %bitcast.21), calls=%async_computation | async-start | bytes 1572864 | tf_op jit(solution)/shard_map/all_to_all | solution.py:604
  32.2 30.9 %all-to-all-start.1 = ((f32[16,112,128]{2,1,0:T(8,128)}), f32[16,112,128]{2,1,0:T(8,128)S(1)}, u32[]{:S(2)}, u32[]{:S(2)}) async-start(f32[16,112,128]{2,1,0:T(8,128)} %bitcast.20), calls=%async_computation.1 | async-start | bytes 1835008 | tf_op jit(solution)/shard_map/all_to_all | solution.py:604
  37.3 10.3 %collective-permute-start = (f32[10,8,128]{2,1,0:T(8,128)S(1)}, f32[10,8,128]{2,1,0:T(8,128)S(1)}, u32[]{:S(2)}, u32[]{:S(2)}) collective-permute-start(f32[10,8,128]{2,1,0:T(8,128)S(1)} %get-tuple-element.28), channel_id=1, source_target_pairs={{0,1},{1,2},{2,3},{3,4},{4,5},{5,6},{6,7},{7,8},{8,9},{9,10},{10,1... | collective-permute-start | bytes 122888 | tf_op jit(solution)/shard_map/ppermute | solution.py:597
  40.4 8.7 %collective-permute-start.1 = (f32[10,8,128]{2,1,0:T(8,128)S(1)}, f32[10,8,128]{2,1,0:T(8,128)S(1)}, u32[]{:S(2)}, u32[]{:S(2)}) collective-permute-start(f32[10,8,128]{2,1,0:T(8,128)S(1)} %get-tuple-element.29), channel_id=1, source_target_pairs={{1,0},{2,1},{3,2},{4,3},{5,4},{6,5},{7,6},{8,7},{9,8},{10,9},{11,1... | collective-permute-start | bytes 122888 | tf_op jit(solution)/shard_map/ppermute | solution.py:598
  49.2 8.7 %collective-permute-start.2 = (f32[12,8,128]{2,1,0:T(8,128)S(1)}, f32[12,8,128]{2,1,0:T(8,128)S(1)}, u32[]{:S(2)}, u32[]{:S(2)}) collective-permute-start(f32[12,8,128]{2,1,0:T(8,128)S(1)} %get-tuple-element.31), channel_id=1, source_target_pairs={{0,16},{16,32},{32,48},{48,64},{64,80},{80,96},{96,112},{1,17},{17... | collective-permute-start | bytes 147464 | tf_op jit(solution)/shard_map/ppermute | solution.py:597
  54.9 5.4 %collective-permute-start.3 = (f32[12,8,128]{2,1,0:T(8,128)S(1)}, f32[12,8,128]{2,1,0:T(8,128)S(1)}, u32[]{:S(2)}, u32[]{:S(2)}) collective-permute-start(f32[12,8,128]{2,1,0:T(8,128)S(1)} %get-tuple-element.30._), channel_id=1, source_target_pairs={{16,0},{32,16},{48,32},{64,48},{80,64},{96,80},{112,96},{17,1},{33... | collective-permute-start | bytes 147464 | tf_op jit(solution)/shard_map/ppermute | solution.py:598

commit v6 on v4

--- a/solution.py
+++ b/solution.py
@@ -259,28 +259,17 @@
     compute(0, warm0, classes0, obuf.at[0])
     put(0, 0).start()
 
-    def chunk(s, carry):
+    for s in range(1, CHUNKS):
         slot = s % 2
         wait(fetch(s, slot))
-
-        @pl.when(s >= 2)
-        def _():
+        if s >= 2:
             put(s - 2, slot).wait()
-
         compute(s, wbuf.at[slot], cbuf.at[slot], obuf.at[slot])
         put(s, slot).start()
-
-        @pl.when(slot == 1)
-        def _():
+        if slot == 1:
             put_flux(s // 2).start()
-
-        @pl.when(s + 2 < CHUNKS)
-        def _():
+        if s + 2 < CHUNKS:
             start(fetch(s + 2, slot))
-
-        return carry
-
-    lax.fori_loop(1, CHUNKS, chunk, 0)
     put(CHUNKS - 2, 0).wait()
     put(CHUNKS - 1, 1).wait()
     for g in range(CHUNKS // 2):

time: 65.7 us -> 65.4 us (level)
  no operation moved by 1% of the time
where the time goes in v6:
time: 65.4 us; the launch traced here: 64.6 us
  starting transfers between devices  25.7 us (39%)
  Pallas kernels  21.1 us (32%)
  waiting for transfers between devices  17.1 us (26%)
  between operations  0.71 us (1%)
    all_to_all x2, starting transfers between devices, swap(): lax.all_to_all(payload.reshape(n, CAP * rows, 128), 'gy', split_axis=0, c...  12.8 us
    ppermute x2, starting transfers between devices, exchange(): from_lower = lax.ppermute(to_upper, axis, up)  8.76 us
    pallas_call x1, Pallas kernels, columns(): pl.pallas_call(column_kernel, out_shape=(jax.ShapeDtypeStruct((NCAT, NLAY...  8.7 us
    all_to_all x2, waiting for transfers between devices, swap(): lax.all_to_all(payload.reshape(n, CAP * rows, 128), 'gy', split_axis=0, c...  8.3 us
    ppermute x2, waiting for transfers between devices, exchange(): from_lower = lax.ppermute(to_upper, axis, up)  5.01 us
    ppermute x2, starting transfers between devices, exchange(): from_upper = lax.ppermute(to_lower, axis, down)  4.11 us
    ppermute x2, waiting for transfers between devices, exchange(): from_upper = lax.ppermute(to_lower, axis, down)  3.84 us
    pallas_call x1, Pallas kernels, prepare(): pl.pallas_call(prepare_kernel, out_shape=(jax.ShapeDtypeStruct((NF, 128,...  3.55 us
  transfers between devices with their start and end apart: 6, of which 4 were waited for; matrix products, arithmetic and copies ran while one was open for 0% of the time, Pallas kernels for 12%

profile of v6, /device:TPU:7, one launch (start us, length us, event | category | flops | bytes accessed | tf_op | source)
XLA Modules:
  0.0 64.6 jit_solution(14821603267942431883)
XLA Ops:
  0.6 2.6 %pack.1 = (f32[1536,128]{1,0:T(8,128)}, f32[2,128,128]{2,1,0:T(8,128)S(1)}) custom-call(s32[16]{0:T(128)} %bitcast.21, s32[16]{0:T(128)} %land.5, f32[8,128,128]{2,1,0:T(8,128)} %x.1), custom_call_target="tpu_custom_call" | custom-call | tf_op jit(solution)/shard_map/pack/pallas_call | solution.py:103
  3.3 7.7 %all-to-all-start = ((f32[16,96,128]{2,1,0:T(8,128)}), f32[16,96,128]{2,1,0:T(8,128)S(1)}, u32[]{:S(2)}, u32[]{:S(2)}) async-start(f32[16,96,128]{2,1,0:T(8,128)} %bitcast.5), calls=%async_computation | async-start | bytes 1572864 | tf_op jit(solution)/shard_map/all_to_all | solution.py:554
  11.0 3.5 %prepare.1 = (f32[10,128,128]{2,1,0:T(8,128)}, f32[10,8,128]{2,1,0:T(8,128)S(1)}, f32[10,8,128]{2,1,0:T(8,128)S(1)}, f32[10,8,128]{2,1,0:T(8,128)S(1)}, f32[10,8...) custom-call(s32[16]{0:T(128)} %land.5, f32[2,128,128]{2,1,0:T(8,128)} %vel.1, ...), custom_call_target="tpu_custom_call" | custom-call | tf_op jit(solution)/shard_map/prepare/pallas_call | solution.py:388
  14.5 8.3 %all-to-all-done = f32[16,96,128]{2,1,0:T(8,128)S(1)} async-done(((f32[16,96,128]{2,1,0:T(8,128)}), f32[16,96,128]{2,1,0:T(8,128)S(1)}, u32[]{:S(2)}, u32[]{:S(2)}) %all-to-all-start) | async-done | bytes 786464 | tf_op jit(solution)/shard_map/all_to_all | solution.py:554
  22.8 8.7 %columns.1 = (f32[5,10,32,1024]{3,2,1,0:T(8,128)}, f32[1792,128]{1,0:T(8,128)}) custom-call(f32[5,10,32,1024]{3,2,1,0:T(8,128)} %bitcast.13, f32[5,32,1024]{2,1,0:T(8,128)} %bitcast.15, f32[5,32,1024]{2,1,0:T(8,128)} %bitcast.17, f32[5,32,1024]{2,1,0:T(8,128)} %bitcast.19, f32[5,10,8,512]{3,2,1,0:T(8,128)S(1)} %get-tuple-element.19.warm0, ...), custom_call_target="tpu_custom_call" | custom-call | tf_op jit(solution)/shard_map/columns/pallas_call | solution.py:280
  31.5 5.1 %all-to-all-start.1 = ((f32[16,112,128]{2,1,0:T(8,128)}), f32[16,112,128]{2,1,0:T(8,128)S(1)}, u32[]{:S(2)}, u32[]{:S(2)}) async-start(f32[16,112,128]{2,1,0:T(8,128)} %bitcast.20), calls=%async_computation.1 | async-start | bytes 1835008 | tf_op jit(solution)/shard_map/all_to_all | solution.py:554
  36.6 3.1 %collective-permute-start = (f32[10,8,128]{2,1,0:T(8,128)S(1)}, f32[10,8,128]{2,1,0:T(8,128)S(1)}, u32[]{:S(2)}, u32[]{:S(2)}) collective-permute-start(f32[10,8,128]{2,1,0:T(8,128)S(1)} %get-tuple-element.28), channel_id=1, source_target_pairs={{0,1},{1,2},{2,3},{3,4},{4,5},{5,6},{6,7},{7,8},{8,9},{9,10},{10,1... | collective-permute-start | bytes 122888 | tf_op jit(solution)/shard_map/ppermute | solution.py:547
  39.7 2.2 %collective-permute-start.1 = (f32[10,8,128]{2,1,0:T(8,128)S(1)}, f32[10,8,128]{2,1,0:T(8,128)S(1)}, u32[]{:S(2)}, u32[]{:S(2)}) collective-permute-start(f32[10,8,128]{2,1,0:T(8,128)S(1)} %get-tuple-element.29), channel_id=1, source_target_pairs={{1,0},{2,1},{3,2},{4,3},{5,4},{6,5},{7,6},{8,7},{9,8},{10,9},{11,1... | collective-permute-start | bytes 122888 | tf_op jit(solution)/shard_map/ppermute | solution.py:548
  41.9 5.0 %collective-permute-done.left = f32[10,8,128]{2,1,0:T(8,128)S(1)} collective-permute-done((f32[10,8,128]{2,1,0:T(8,128)S(1)}, f32[10,8,128]{2,1,0:T(8,128)S(1)}, u32[]{:S(2)}, u32[]{:S(2)}) %collective-permute-start) | collective-permute-done | bytes 40992 | tf_op jit(solution)/shard_map/ppermute | solution.py:547
  46.9 1.5 %collective-permute-done.1.right = f32[10,8,128]{2,1,0:T(8,128)S(1)} collective-permute-done((f32[10,8,128]{2,1,0:T(8,128)S(1)}, f32[10,8,128]{2,1,0:T(8,128)S(1)}, u32[]{:S(2)}, u32[]{:S(2)}) %collective-permute-start.1) | collective-permute-done | bytes 40992 | tf_op jit(solution)/shard_map/ppermute | solution.py:548
  48.4 0.1 rows.1
  48.5 5.7 %collective-permute-start.2 = (f32[12,8,128]{2,1,0:T(8,128)S(1)}, f32[12,8,128]{2,1,0:T(8,128)S(1)}, u32[]{:S(2)}, u32[]{:S(2)}) collective-permute-start(f32[12,8,128]{2,1,0:T(8,128)S(1)} %get-tuple-element.31), channel_id=1, source_target_pairs={{0,16},{16,32},{32,48},{48,64},{64,80},{80,96},{96,112},{1,17},{17... | collective-permute-start | bytes 147464 | tf_op jit(solution)/shard_map/ppermute | solution.py:547
  54.2 1.9 %collective-permute-start.3 = (f32[12,8,128]{2,1,0:T(8,128)S(1)}, f32[12,8,128]{2,1,0:T(8,128)S(1)}, u32[]{:S(2)}, u32[]{:S(2)}) collective-permute-start(f32[12,8,128]{2,1,0:T(8,128)S(1)} %get-tuple-element.30._), channel_id=1, source_target_pairs={{16,0},{32,16},{48,32},{64,48},{80,64},{96,80},{112,96},{17,1},{33... | collective-permute-start | bytes 147464 | tf_op jit(solution)/shard_map/ppermute | solution.py:548
  56.1 1.1 %stage.1.fields = f32[10,128,128]{2,1,0:T(8,128)S(1)} custom-call(f32[10,128,128]{2,1,0:T(8,128)} %get-tuple-element.25.fields, f32[12,8,128]{2,1,0:T(8,128)S(1)} %get-tuple-element.30._), custom_call_target="tpu_custom_call" | custom-call | tf_op jit(solution)/shard_map/stage/pallas_call | solution.py:435
  57.2 0.0 collective-permute-done.2.top
  57.2 2.4 %collective-permute-done.3.bottom = f32[12,8,128]{2,1,0:T(8,128)S(1)} collective-permute-done((f32[12,8,128]{2,1,0:T(8,128)S(1)}, f32[12,8,128]{2,1,0:T(8,128)S(1)}, u32[]{:S(2)}, u32[]{:S(2)}) %collective-permute-start.3) | collective-permute-done | bytes 49184 | tf_op jit(solution)/shard_map/ppermute | solution.py:548
  59.6 2.8 %evp.1 = (f32[2,128,128]{2,1,0:T(8,128)}, f32[3,128,128]{2,1,0:T(8,128)}) custom-call(f32[10,128,128]{2,1,0:T(8,128)S(1)} %stage.1.fields, f32[10,8,128]{2,1,0:T(8,128)S(1)} %collective-permute-done.left, f32[10,8,128]{2,1,0:T(8,128)S(1)} %collective-permute-done.1.right, f32[12,8,128]{2,1,0:T(8,128)S(1)} %collective-permute-done.2.top, ...), custom_call_target="tpu_custom_call" | custom-call | tf_op jit(solution)/shard_map/evp/pallas_call | solution.py:530
  62.4 0.0 all-to-all-done.1
  62.4 2.2 %unpack.1 = f32[8,128,128]{2,1,0:T(8,128)} custom-call(s32[16]{0:T(128)} %bitcast.22, s32[16]{0:T(128)} %land.5, f32[1792,128]{1,0:T(8,128)S(1)} %bitcast.10, f32[2,128,128]{2,1,0:T(8,128)S(1)} %get-tuple-element.24.kept), custom_call_target="tpu_custom_call" | custom-call | tf_op jit(solution)/shard_map/unpack/pallas_call | solution.py:328
Async XLA Ops:
  3.3 19.6 %all-to-all-start = ((f32[16,96,128]{2,1,0:T(8,128)}), f32[16,96,128]{2,1,0:T(8,128)S(1)}, u32[]{:S(2)}, u32[]{:S(2)}) async-start(f32[16,96,128]{2,1,0:T(8,128)} %bitcast.5), calls=%async_computation | async-start | bytes 1572864 | tf_op jit(solution)/shard_map/all_to_all | solution.py:554
  31.5 30.8 %all-to-all-start.1 = ((f32[16,112,128]{2,1,0:T(8,128)}), f32[16,112,128]{2,1,0:T(8,128)S(1)}, u32[]{:S(2)}, u32[]{:S(2)}) async-start(f32[16,112,128]{2,1,0:T(8,128)} %bitcast.20), calls=%async_computation.1 | async-start | bytes 1835008 | tf_op jit(solution)/shard_map/all_to_all | solution.py:554
  36.6 10.3 %collective-permute-start = (f32[10,8,128]{2,1,0:T(8,128)S(1)}, f32[10,8,128]{2,1,0:T(8,128)S(1)}, u32[]{:S(2)}, u32[]{:S(2)}) collective-permute-start(f32[10,8,128]{2,1,0:T(8,128)S(1)} %get-tuple-element.28), channel_id=1, source_target_pairs={{0,1},{1,2},{2,3},{3,4},{4,5},{5,6},{6,7},{7,8},{8,9},{9,10},{10,1... | collective-permute-start | bytes 122888 | tf_op jit(solution)/shard_map/ppermute | solution.py:547
  39.7 8.7 %collective-permute-start.1 = (f32[10,8,128]{2,1,0:T(8,128)S(1)}, f32[10,8,128]{2,1,0:T(8,128)S(1)}, u32[]{:S(2)}, u32[]{:S(2)}) collective-permute-start(f32[10,8,128]{2,1,0:T(8,128)S(1)} %get-tuple-element.29), channel_id=1, source_target_pairs={{1,0},{2,1},{3,2},{4,3},{5,4},{6,5},{7,6},{8,7},{9,8},{10,9},{11,1... | collective-permute-start | bytes 122888 | tf_op jit(solution)/shard_map/ppermute | solution.py:548
  48.5 8.7 %collective-permute-start.2 = (f32[12,8,128]{2,1,0:T(8,128)S(1)}, f32[12,8,128]{2,1,0:T(8,128)S(1)}, u32[]{:S(2)}, u32[]{:S(2)}) collective-permute-start(f32[12,8,128]{2,1,0:T(8,128)S(1)} %get-tuple-element.31), channel_id=1, source_target_pairs={{0,16},{16,32},{32,48},{48,64},{64,80},{80,96},{96,112},{1,17},{17... | collective-permute-start | bytes 147464 | tf_op jit(solution)/shard_map/ppermute | solution.py:547
  54.2 5.4 %collective-permute-start.3 = (f32[12,8,128]{2,1,0:T(8,128)S(1)}, f32[12,8,128]{2,1,0:T(8,128)S(1)}, u32[]{:S(2)}, u32[]{:S(2)}) collective-permute-start(f32[12,8,128]{2,1,0:T(8,128)S(1)} %get-tuple-element.30._), channel_id=1, source_target_pairs={{16,0},{32,16},{48,32},{64,48},{80,64},{96,80},{112,96},{17,1},{33... | collective-permute-start | bytes 147464 | tf_op jit(solution)/shard_map/ppermute | solution.py:548
